TPU v7x, 32 devices: a whole 2x2x4 slice. The times are simulated.
32 devices in a mesh: grp: 2 (over x), seq: 16 (over z, y, core).
Axes of the slice: x: 2, y: 2, z: 4, core: 2. Of those that a mesh axis runs over, the one named last changes fastest.
Arguments:
- query_inputs: bfloat16 [32768, 128], P(('grp', 'seq')), parts along dimension 0, may hold values from -6 to 6
- key_inputs: bfloat16 [32768, 128], P(('grp', 'seq')), parts along dimension 0, may hold values from -5.3 to 4.8
- value_inputs: bfloat16 [32768, 2048], P(('grp', 'seq')), parts along dimension 0, may hold values from -5.3 to 4.8
- log_decay: float32 [16, 32768], P(None, ('grp', 'seq')), parts along dimension 1, may hold values from -0.9 to 0, as said below
- level_weight: bfloat16 [15, 16, 32768], P(None, None, ('grp', 'seq')), parts along dimension 2, may hold values from 0.099609375 to 1
- conv_weight: float32 [4, 2304], replicated, may hold values from 0.35 to 0.65
- norm_gain: float32 [2048], replicated, may hold values from 0.1 to 1.9
Outputs:
- mixer_out: bfloat16 [32768, 2048], P(('grp', 'seq')), parts along dimension 0
There are 2 independent parts, one for each index of `grp`. A program takes and returns all parts, laid end to end along the dimension named above; an argument that names none is the same for every part. Nothing has to cross between parts.
Inputs may be any that keep to these rules, and one draw needn't show every extreme that they name: `log_decay`: each entry is the logarithm of one head's decay factor at one token.
All inputs are finite; a program needn't handle non-finite values.
Results may differ from a plain program's by a relative error of at most 0.014.
Values may be sent and summed in bfloat16 or wider, within the bound.
No kernel may reach another device: no remote copies, remote signals or barrier semaphores. Data moves between devices by JAX's collectives and lax.ppermute only.
A program may use at most 64 MiB of HBM per device.

v0:
```python
import jax
import jax.numpy as jnp
from jax import lax
from jax.sharding import PartitionSpec as P

EPSILON = 1e-05


def partner(x, axis, distance):
    return lax.ppermute(x, axis, [(i, i ^ 1 << distance) for i in range(lax.axis_size(axis))])


def from_behind(x, axis, by):
    size = lax.axis_size(axis)
    pairs = [(i, i + by) for i in range(size) if 0 <= i + by < size]
    return lax.ppermute(x, axis, pairs)


def causal_conv(current, previous, weight):
    length = current.shape[0]
    tap_count = weight.shape[0]
    joined = jnp.concatenate([previous, current], axis=0).astype(jnp.float32)
    summed = jnp.zeros(current.shape, jnp.float32)
    for tap_pos in range(tap_count):
        summed = summed + weight[tap_pos][None, :] * joined[tap_pos : tap_pos + length]
    return jax.nn.silu(summed).astype(jnp.bfloat16)


def level_of(length, bit_count):
    position_list = lax.iota(jnp.int32, length)
    differ = jnp.bitwise_xor(position_list[:, None], position_list[None, :])
    levels = jnp.zeros((length, length), jnp.int32)
    for bit_pos in range(bit_count):
        levels = levels + (differ >= 1 << bit_pos).astype(jnp.int32)
    return (levels, position_list[:, None] >= position_list[None, :])


def climb(group_state, shard_total, shard_index, bit_count):
    block_state = group_state
    block_total = shard_total
    offset = jnp.zeros_like(shard_total)
    buckets = []
    for bit_pos in range(bit_count):
        other_state, other_total = partner((block_state, block_total), "seq", bit_pos)
        upper_half = shard_index >> bit_pos & 1 == 1
        lifted = jnp.exp(offset)[:, None, None] * other_state
        buckets.append(jnp.where(upper_half, lifted, 0.0).astype(jnp.bfloat16))
        if bit_pos + 1 < bit_count:
            block_state = jnp.where(
                upper_half,
                block_state + jnp.exp(block_total)[:, None, None] * other_state,
                other_state + jnp.exp(other_total)[:, None, None] * block_state,
            )
            block_total = block_total + other_total
            offset = offset + jnp.where(upper_half, other_total, 0.0)
    return jnp.stack(buckets, axis=0)


def on_device(
    query_inputs, key_inputs, value_inputs, log_decay, level_weight, conv_weight, norm_gain
):
    length = query_inputs.shape[0]
    state_dim = query_inputs.shape[1]
    head_count = log_decay.shape[0]
    head_width = value_inputs.shape[1] // head_count
    rim_width = conv_weight.shape[0] - 1
    seq_bits = lax.axis_size("seq").bit_length() - 1
    token_bits = length.bit_length() - 1
    shard_index = lax.axis_index("seq")
    rim_parts = from_behind(
        (
            query_inputs[length - rim_width :],
            key_inputs[length - rim_width :],
            value_inputs[length - rim_width :],
        ),
        "seq",
        1,
    )
    queries = causal_conv(query_inputs, rim_parts[0], conv_weight[:, :state_dim])
    keys_conv = causal_conv(key_inputs, rim_parts[1], conv_weight[:, state_dim : 2 * state_dim])
    values_conv = causal_conv(value_inputs, rim_parts[2], conv_weight[:, 2 * state_dim :])
    cumul_decay = jnp.cumsum(log_decay, axis=1)
    shard_total = cumul_decay[:, length - 1]
    tail_decay = jnp.exp(shard_total[:, None] - cumul_decay)
    decayed = (keys_conv.astype(jnp.float32)[None, :, :] * tail_decay[:, :, None]).astype(
        jnp.bfloat16
    )
    value_heads = values_conv.reshape(length, head_count, head_width)
    group_state = jnp.einsum(
        "hcn,chp->hnp", decayed, value_heads, preferred_element_type=jnp.float32
    )
    scores = lax.dot_general(
        queries, keys_conv, (((1,), (1,)), ((), ())), preferred_element_type=jnp.float32
    )
    near_levels = level_weight[: token_bits + 1]
    far_levels = level_weight[token_bits + 1 :]
    query_float = queries.astype(jnp.float32)
    levels, causal = level_of(length, token_bits)

    def near_part(head_idx):
        decay_row = lax.dynamic_index_in_dim(cumul_decay, head_idx, 0, keepdims=False)
        weights_row = lax.dynamic_index_in_dim(near_levels, head_idx, 1, keepdims=False).astype(
            jnp.float32
        )
        mixing = jnp.zeros((length, length), jnp.float32)
        for level_pos in range(token_bits + 1):
            mixing = mixing + jnp.where(levels == level_pos, weights_row[level_pos][:, None], 0.0)
        decay_gap = jnp.where(causal, decay_row[:, None] - decay_row[None, :], -1e30)
        near_weight = (scores * mixing * jnp.exp(decay_gap)).astype(jnp.bfloat16)
        own_values = lax.dynamic_slice_in_dim(values_conv, head_idx * head_width, head_width, 1)
        return jnp.dot(near_weight, own_values, preferred_element_type=jnp.float32)

    def far_part(head_idx, buckets):
        decay_row = lax.dynamic_index_in_dim(cumul_decay, head_idx, 0, keepdims=False)
        far_scale = (
            lax.dynamic_index_in_dim(far_levels, head_idx, 1, keepdims=False).astype(jnp.float32)
            * jnp.exp(decay_row)[None, :]
        )
        far_query = (
            (query_float[:, None, :] * far_scale.T[:, :, None])
            .astype(jnp.bfloat16)
            .reshape(length, seq_bits * state_dim)
        )
        head_buckets = lax.dynamic_index_in_dim(buckets, head_idx, 1, keepdims=False).reshape(
            seq_bits * state_dim, head_width
        )
        return jnp.dot(far_query, head_buckets, preferred_element_type=jnp.float32)

    def finish(head_idx, pre_norm, output):
        gain_row = lax.dynamic_slice_in_dim(norm_gain, head_idx * head_width, head_width, 0)
        normed = (
            pre_norm
            * lax.rsqrt(jnp.mean(pre_norm * pre_norm, axis=1, keepdims=True) + EPSILON)
            * gain_row[None, :]
        )
        return lax.dynamic_update_slice_in_dim(
            output, normed.astype(jnp.bfloat16), head_idx * head_width, 1
        )

    blank_out = jnp.zeros((length, head_count * head_width), jnp.bfloat16)

    def near_step(head_idx, near_all):
        return lax.dynamic_update_slice_in_dim(
            near_all, near_part(head_idx), head_idx * head_width, 1
        )

    near_all = lax.fori_loop(
        0, head_count, near_step, jnp.zeros((length, head_count * head_width), jnp.float32)
    )
    buckets = climb(group_state, shard_total, shard_index, seq_bits)

    def far_step(head_idx, output):
        near_term = lax.dynamic_slice_in_dim(near_all, head_idx * head_width, head_width, 1)
        return finish(head_idx, near_term + far_part(head_idx, buckets), output)

    return lax.fori_loop(0, head_count, far_step, blank_out)


def solution(mesh):
    return jax.shard_map(
        on_device,
        mesh=mesh,
        in_specs=(
            P(("grp", "seq"), None),
            P(("grp", "seq"), None),
            P(("grp", "seq"), None),
            P(None, ("grp", "seq")),
            P(None, None, ("grp", "seq")),
            P(),
            P(),
        ),
        out_specs=P(("grp", "seq"), None),
        check_vma=False,
    )
```

profile of v0, /device:TPU:0, one launch (start us, length us, event | category | flops | bytes accessed | tf_op | source)
XLA Modules:
  0.0 439.1 jit_solution(3361163196439672587)
XLA Ops:
  3.9 4.5 %collective-permute-start.2 = (bf16[3,2048]{1,0:T(4,128)(2,1)S(1)}, bf16[3,2048]{1,0:T(4,128)(2,1)S(1)}, u32[]{:S(2)}, u32[]{:S(2)}) collective-permute-start(bf16[3,2048]{1,0:T(4,128)(2,1)S(1)} %slice.223), channel_id=1, source_target_pairs={{0,1},{1,2},{2,3},{3,4},{4,5},{5,6},{6,7},{7,8},{8,9},{9,10},{10,1... | collective-permute-start | bytes 36872 | tf_op jit(solution)/shard_map/ppermute | solution.py:16
  9.2 4.5 %reduce-window.6 = f32[16,8,128]{2,1,0:T(8,128)S(1)} reduce-window(f32[16,8,128]{2,1,0:T(8,128)S(1)} %bitcast.116, f32[]{:T(128)} %constant.201.clone.1), window={size=1x1x128 pad=0_0x0_0x127_0}, to_apply=%region_0.1 | reduce-window | flops 2080768 | bytes 131076 | tf_op jit(solution)/shard_map/reduce-window
  21.2 5.9 %fusion.42 = f32[16,128,128]{2,1,0:T(8,128)S(1)} fusion(f32[16,1024]{1,0:T(8,128)S(1)} %subtract_exponential_fusion, f32[1024,128]{0,1:T(8,128)S(1)} %copy.18, f32[1027,2048]{1,0:T(8,128)S(1)} %maximum_convert_fusion, f32[2048]{0:T(1024)S(1)} %bitcast.136, f32[2048]{0:T(1024)S(1)} %bitcast.138, f32[2048]{0:T(1024)S(1)} %bitcast.134, f32[2048]{0:T(1024)S(1)} %bitcast.132), kind=kOutput, calls=%fused_computation.64 | convolution fusion | flops 566231040 | bytes 35225600 | tf_op jit(solution)/shard_map/hcn,chp->hnp/dot_general | solution.py:89
  40.4 20.3 %collective-permute-done.5 = f32[16,128,128]{2,1,0:T(8,128)S(1)} collective-permute-done((f32[16,128,128]{2,1,0:T(8,128)S(1)}, f32[16,128,128]{2,1,0:T(8,128)S(1)}, u32[]{:S(2)}, u32[]{:S(2)}) %collective-permute-start.5) | collective-permute-done | bytes 1048608 | tf_op jit(solution)/shard_map/ppermute | solution.py:10
  61.6 6.4 %multiply_convert_fusion.7 = bf16[1024,2048]{1,0:T(8,128)(2,1)} fusion(f32[1027,2048]{1,0:T(8,128)S(1)} %copy-done.1, f32[2048]{0:T(1024)S(1)} %bitcast.137, f32[2048]{0:T(1024)S(1)} %bitcast.139, f32[2048]{0:T(1024)S(1)} %bitcast.135, f32[2048]{0:T(1024)S(1)} %bitcast.133), kind=kLoop, calls=%fused_computation.62 | loop fusion | flops 25165824 | bytes 37781504 | tf_op jit(solution)/shard_map/convert_element_type | solution.py:26
  68.0 17.5 %collective-permute-done.7 = f32[16,128,128]{2,1,0:T(8,128)S(1)} collective-permute-done((f32[16,128,128]{2,1,0:T(8,128)S(1)}, f32[16,128,128]{2,1,0:T(8,128)S(1)}, u32[]{:S(2)}, u32[]{:S(2)}) %collective-permute-start.7) | collective-permute-done | bytes 1048608 | tf_op jit(solution)/shard_map/ppermute | solution.py:10
  88.2 4.3 broadcast_in_dim.270
  92.5 201.8 %while.29 = (s32[]{:T(128)}, f32[1024,2048]{1,0:T(8,128)}, bf16[11,16,1024]{2,1,0:T(8,128)(2,1)S(1)}, f32[1024,1024]{1,0:T(8,128)}, f32[16,1024]{1,0:T(8,128)S(1...) while((s32[]{:T(128)}, f32[1024,2048]{1,0:T(8,128)}, ...), condition=%wide.region_3.4_spmd.clone.clone, body=%wide.region_2.3_spmd.clone.clone.sunk | while | flops 339749888 | bytes 5201051 | solution.py:147
  92.6 12.5 %fusion.84 = f32[1024,2048]{1,0:T(8,128)} fusion(f32[1024,2048]{1,0:T(8,128)} %get-tuple-element.571, s32[]{:T(128)S(6)} %select_n.350, f32[1024,1024]{1,0:T(8,128)} %get-tuple-element.583, f32[1024]{0:T(1024)S(1)} %bitcast.130, f32[1024]{0:T(1024)S(1)} %bitcast.120, f32[1024]{0:T(1024)S(1)} %bitcast.121, f32[1024]{0:T(1024)S(1)} %bitcast.122, ...), kind=kOutput, calls=%fused_computation.31.clone.1 | convolution fusion | flops 339738624 | bytes 5035008 | tf_op jit(solution)/shard_map/while/body/eval_jaxpr/dot_general | solution.py:111
  105.2 12.5 %fusion.84 = f32[1024,2048]{1,0:T(8,128)} fusion(f32[1024,2048]{1,0:T(8,128)} %get-tuple-element.571, s32[]{:T(128)S(6)} %select_n.350, f32[1024,1024]{1,0:T(8,128)} %get-tuple-element.583, f32[1024]{0:T(1024)S(1)} %bitcast.130, f32[1024]{0:T(1024)S(1)} %bitcast.120, f32[1024]{0:T(1024)S(1)} %bitcast.121, f32[1024]{0:T(1024)S(1)} %bitcast.122, ...), kind=kOutput, calls=%fused_computation.31.clone.1 | convolution fusion | flops 339738624 | bytes 5035008 | tf_op jit(solution)/shard_map/while/body/eval_jaxpr/dot_general | solution.py:111
  117.8 12.5 %fusion.84 = f32[1024,2048]{1,0:T(8,128)} fusion(f32[1024,2048]{1,0:T(8,128)} %get-tuple-element.571, s32[]{:T(128)S(6)} %select_n.350, f32[1024,1024]{1,0:T(8,128)} %get-tuple-element.583, f32[1024]{0:T(1024)S(1)} %bitcast.130, f32[1024]{0:T(1024)S(1)} %bitcast.120, f32[1024]{0:T(1024)S(1)} %bitcast.121, f32[1024]{0:T(1024)S(1)} %bitcast.122, ...), kind=kOutput, calls=%fused_computation.31.clone.1 | convolution fusion | flops 339738624 | bytes 5035008 | tf_op jit(solution)/shard_map/while/body/eval_jaxpr/dot_general | solution.py:111
  130.4 12.5 %fusion.84 = f32[1024,2048]{1,0:T(8,128)} fusion(f32[1024,2048]{1,0:T(8,128)} %get-tuple-element.571, s32[]{:T(128)S(6)} %select_n.350, f32[1024,1024]{1,0:T(8,128)} %get-tuple-element.583, f32[1024]{0:T(1024)S(1)} %bitcast.130, f32[1024]{0:T(1024)S(1)} %bitcast.120, f32[1024]{0:T(1024)S(1)} %bitcast.121, f32[1024]{0:T(1024)S(1)} %bitcast.122, ...), kind=kOutput, calls=%fused_computation.31.clone.1 | convolution fusion | flops 339738624 | bytes 5035008 | tf_op jit(solution)/shard_map/while/body/eval_jaxpr/dot_general | solution.py:111
  143.0 12.5 %fusion.84 = f32[1024,2048]{1,0:T(8,128)} fusion(f32[1024,2048]{1,0:T(8,128)} %get-tuple-element.571, s32[]{:T(128)S(6)} %select_n.350, f32[1024,1024]{1,0:T(8,128)} %get-tuple-element.583, f32[1024]{0:T(1024)S(1)} %bitcast.130, f32[1024]{0:T(1024)S(1)} %bitcast.120, f32[1024]{0:T(1024)S(1)} %bitcast.121, f32[1024]{0:T(1024)S(1)} %bitcast.122, ...), kind=kOutput, calls=%fused_computation.31.clone.1 | convolution fusion | flops 339738624 | bytes 5035008 | tf_op jit(solution)/shard_map/while/body/eval_jaxpr/dot_general | solution.py:111
  155.6 12.5 %fusion.84 = f32[1024,2048]{1,0:T(8,128)} fusion(f32[1024,2048]{1,0:T(8,128)} %get-tuple-element.571, s32[]{:T(128)S(6)} %select_n.350, f32[1024,1024]{1,0:T(8,128)} %get-tuple-element.583, f32[1024]{0:T(1024)S(1)} %bitcast.130, f32[1024]{0:T(1024)S(1)} %bitcast.120, f32[1024]{0:T(1024)S(1)} %bitcast.121, f32[1024]{0:T(1024)S(1)} %bitcast.122, ...), kind=kOutput, calls=%fused_computation.31.clone.1 | convolution fusion | flops 339738624 | bytes 5035008 | tf_op jit(solution)/shard_map/while/body/eval_jaxpr/dot_general | solution.py:111
  168.3 12.5 %fusion.84 = f32[1024,2048]{1,0:T(8,128)} fusion(f32[1024,2048]{1,0:T(8,128)} %get-tuple-element.571, s32[]{:T(128)S(6)} %select_n.350, f32[1024,1024]{1,0:T(8,128)} %get-tuple-element.583, f32[1024]{0:T(1024)S(1)} %bitcast.130, f32[1024]{0:T(1024)S(1)} %bitcast.120, f32[1024]{0:T(1024)S(1)} %bitcast.121, f32[1024]{0:T(1024)S(1)} %bitcast.122, ...), kind=kOutput, calls=%fused_computation.31.clone.1 | convolution fusion | flops 339738624 | bytes 5035008 | tf_op jit(solution)/shard_map/while/body/eval_jaxpr/dot_general | solution.py:111
  180.9 12.5 %fusion.84 = f32[1024,2048]{1,0:T(8,128)} fusion(f32[1024,2048]{1,0:T(8,128)} %get-tuple-element.571, s32[]{:T(128)S(6)} %select_n.350, f32[1024,1024]{1,0:T(8,128)} %get-tuple-element.583, f32[1024]{0:T(1024)S(1)} %bitcast.130, f32[1024]{0:T(1024)S(1)} %bitcast.120, f32[1024]{0:T(1024)S(1)} %bitcast.121, f32[1024]{0:T(1024)S(1)} %bitcast.122, ...), kind=kOutput, calls=%fused_computation.31.clone.1 | convolution fusion | flops 339738624 | bytes 5035008 | tf_op jit(solution)/shard_map/while/body/eval_jaxpr/dot_general | solution.py:111
  193.5 12.6 %fusion.84 = f32[1024,2048]{1,0:T(8,128)} fusion(f32[1024,2048]{1,0:T(8,128)} %get-tuple-element.571, s32[]{:T(128)S(6)} %select_n.350, f32[1024,1024]{1,0:T(8,128)} %get-tuple-element.583, f32[1024]{0:T(1024)S(1)} %bitcast.130, f32[1024]{0:T(1024)S(1)} %bitcast.120, f32[1024]{0:T(1024)S(1)} %bitcast.121, f32[1024]{0:T(1024)S(1)} %bitcast.122, ...), kind=kOutput, calls=%fused_computation.31.clone.1 | convolution fusion | flops 339738624 | bytes 5035008 | tf_op jit(solution)/shard_map/while/body/eval_jaxpr/dot_general | solution.py:111
  206.1 12.5 %fusion.84 = f32[1024,2048]{1,0:T(8,128)} fusion(f32[1024,2048]{1,0:T(8,128)} %get-tuple-element.571, s32[]{:T(128)S(6)} %select_n.350, f32[1024,1024]{1,0:T(8,128)} %get-tuple-element.583, f32[1024]{0:T(1024)S(1)} %bitcast.130, f32[1024]{0:T(1024)S(1)} %bitcast.120, f32[1024]{0:T(1024)S(1)} %bitcast.121, f32[1024]{0:T(1024)S(1)} %bitcast.122, ...), kind=kOutput, calls=%fused_computation.31.clone.1 | convolution fusion | flops 339738624 | bytes 5035008 | tf_op jit(solution)/shard_map/while/body/eval_jaxpr/dot_general | solution.py:111
  218.7 12.5 %fusion.84 = f32[1024,2048]{1,0:T(8,128)} fusion(f32[1024,2048]{1,0:T(8,128)} %get-tuple-element.571, s32[]{:T(128)S(6)} %select_n.350, f32[1024,1024]{1,0:T(8,128)} %get-tuple-element.583, f32[1024]{0:T(1024)S(1)} %bitcast.130, f32[1024]{0:T(1024)S(1)} %bitcast.120, f32[1024]{0:T(1024)S(1)} %bitcast.121, f32[1024]{0:T(1024)S(1)} %bitcast.122, ...), kind=kOutput, calls=%fused_computation.31.clone.1 | convolution fusion | flops 339738624 | bytes 5035008 | tf_op jit(solution)/shard_map/while/body/eval_jaxpr/dot_general | solution.py:111
  231.3 12.6 %fusion.84 = f32[1024,2048]{1,0:T(8,128)} fusion(f32[1024,2048]{1,0:T(8,128)} %get-tuple-element.571, s32[]{:T(128)S(6)} %select_n.350, f32[1024,1024]{1,0:T(8,128)} %get-tuple-element.583, f32[1024]{0:T(1024)S(1)} %bitcast.130, f32[1024]{0:T(1024)S(1)} %bitcast.120, f32[1024]{0:T(1024)S(1)} %bitcast.121, f32[1024]{0:T(1024)S(1)} %bitcast.122, ...), kind=kOutput, calls=%fused_computation.31.clone.1 | convolution fusion | flops 339738624 | bytes 5035008 | tf_op jit(solution)/shard_map/while/body/eval_jaxpr/dot_general | solution.py:111
  244.0 12.5 %fusion.84 = f32[1024,2048]{1,0:T(8,128)} fusion(f32[1024,2048]{1,0:T(8,128)} %get-tuple-element.571, s32[]{:T(128)S(6)} %select_n.350, f32[1024,1024]{1,0:T(8,128)} %get-tuple-element.583, f32[1024]{0:T(1024)S(1)} %bitcast.130, f32[1024]{0:T(1024)S(1)} %bitcast.120, f32[1024]{0:T(1024)S(1)} %bitcast.121, f32[1024]{0:T(1024)S(1)} %bitcast.122, ...), kind=kOutput, calls=%fused_computation.31.clone.1 | convolution fusion | flops 339738624 | bytes 5035008 | tf_op jit(solution)/shard_map/while/body/eval_jaxpr/dot_general | solution.py:111
  256.6 12.5 %fusion.84 = f32[1024,2048]{1,0:T(8,128)} fusion(f32[1024,2048]{1,0:T(8,128)} %get-tuple-element.571, s32[]{:T(128)S(6)} %select_n.350, f32[1024,1024]{1,0:T(8,128)} %get-tuple-element.583, f32[1024]{0:T(1024)S(1)} %bitcast.130, f32[1024]{0:T(1024)S(1)} %bitcast.120, f32[1024]{0:T(1024)S(1)} %bitcast.121, f32[1024]{0:T(1024)S(1)} %bitcast.122, ...), kind=kOutput, calls=%fused_computation.31.clone.1 | convolution fusion | flops 339738624 | bytes 5035008 | tf_op jit(solution)/shard_map/while/body/eval_jaxpr/dot_general | solution.py:111
  269.2 12.5 %fusion.84 = f32[1024,2048]{1,0:T(8,128)} fusion(f32[1024,2048]{1,0:T(8,128)} %get-tuple-element.571, s32[]{:T(128)S(6)} %select_n.350, f32[1024,1024]{1,0:T(8,128)} %get-tuple-element.583, f32[1024]{0:T(1024)S(1)} %bitcast.130, f32[1024]{0:T(1024)S(1)} %bitcast.120, f32[1024]{0:T(1024)S(1)} %bitcast.121, f32[1024]{0:T(1024)S(1)} %bitcast.122, ...), kind=kOutput, calls=%fused_computation.31.clone.1 | convolution fusion | flops 339738624 | bytes 5035008 | tf_op jit(solution)/shard_map/while/body/eval_jaxpr/dot_general | solution.py:111
  281.8 12.5 %fusion.84 = f32[1024,2048]{1,0:T(8,128)} fusion(f32[1024,2048]{1,0:T(8,128)} %get-tuple-element.571, s32[]{:T(128)S(6)} %select_n.350, f32[1024,1024]{1,0:T(8,128)} %get-tuple-element.583, f32[1024]{0:T(1024)S(1)} %bitcast.130, f32[1024]{0:T(1024)S(1)} %bitcast.120, f32[1024]{0:T(1024)S(1)} %bitcast.121, f32[1024]{0:T(1024)S(1)} %bitcast.122, ...), kind=kOutput, calls=%fused_computation.31.clone.1 | convolution fusion | flops 339738624 | bytes 5035008 | tf_op jit(solution)/shard_map/while/body/eval_jaxpr/dot_general | solution.py:111
  300.1 139.1 %while.28 = (s32[]{:T(128)}, bf16[1024,2048]{1,0:T(8,128)(2,1)}, f32[1024,2048]{1,0:T(8,128)}, f32[1024,128]{1,0:T(8,128)S(1)}, bf16[4,16,1024]{2,1,0:T(8,128)(2...) while((s32[]{:T(128)}, bf16[1024,2048]{1,0:T(8,128)(2,1)}, ...), condition=%wide.region_6.7_spmd, body=%wide.region_4.6_spmd.sunk | while | flops 136061952 | bytes 8132283 | solution.py:156
  310.4 3.9 multiply_convert_fusion.15
  327.7 3.9 multiply_convert_fusion.15
  336.4 3.9 multiply_convert_fusion.15
  353.8 3.9 multiply_convert_fusion.15
  362.5 3.9 multiply_convert_fusion.15
  379.9 3.9 multiply_convert_fusion.15
  388.6 3.9 multiply_convert_fusion.15
  (324 shorter events, 146.3 us)
Async XLA Ops:
  0.7 15.6 %collective-permute-start.1 = (bf16[3,128]{1,0:T(4,128)(2,1)S(1)}, bf16[3,128]{1,0:T(4,128)(2,1)S(1)}, u32[]{:S(2)}, u32[]{:S(2)}) collective-permute-start(bf16[3,128]{1,0:T(4,128)(2,1)S(1)} %slice.212), channel_id=1, source_target_pairs={{0,1},{1,2},{2,3},{3,4},{4,5},{5,6},{6,7},{7,8},{8,9},{9,10},{10,1... | collective-permute-start | bytes 2312 | tf_op jit(solution)/shard_map/ppermute | solution.py:16
  3.9 13.9 %collective-permute-start.2 = (bf16[3,2048]{1,0:T(4,128)(2,1)S(1)}, bf16[3,2048]{1,0:T(4,128)(2,1)S(1)}, u32[]{:S(2)}, u32[]{:S(2)}) collective-permute-start(bf16[3,2048]{1,0:T(4,128)(2,1)S(1)} %slice.223), channel_id=1, source_target_pairs={{0,1},{1,2},{2,3},{3,4},{4,5},{5,6},{6,7},{7,8},{8,9},{9,10},{10,1... | collective-permute-start | bytes 36872 | tf_op jit(solution)/shard_map/ppermute | solution.py:16
  21.2 5.9 %copy-start = (f32[1027,2048]{1,0:T(8,128)}, f32[1027,2048]{1,0:T(8,128)S(1)}, u32[]{:S(2)}) copy-start(f32[1027,2048]{1,0:T(8,128)S(1)} %maximum_convert_fusion) | copy-start | bytes 25239556
  21.2 6.5 %copy-start.2 = (bf16[1024,128]{1,0:T(8,128)(2,1)S(1)}, bf16[1024,128]{1,0:T(8,128)(2,1)}, u32[]{:S(2)}) copy-start(bf16[1024,128]{1,0:T(8,128)(2,1)} %param.11) | copy-start | bytes 786436
  27.1 8.1 %collective-permute-start.3 = (f32[16,128,128]{2,1,0:T(8,128)S(1)}, f32[16,128,128]{2,1,0:T(8,128)S(1)}, u32[]{:S(2)}, u32[]{:S(2)}) collective-permute-start(f32[16,128,128]{2,1,0:T(8,128)S(1)} %fusion.42), channel_id=1, source_target_pairs={{0,1},{1,0},{2,3},{3,2},{4,5},{5,4},{6,7},{7,6},{8,9},{9,8},{10,11... | collective-permute-start | bytes 3145736 | tf_op jit(solution)/shard_map/ppermute | solution.py:10
  27.2 2.7 collective-permute-start.4
  27.7 9.5 %collective-permute-start = (bf16[3,128]{1,0:T(4,128)(2,1)S(1)}, bf16[3,128]{1,0:T(4,128)(2,1)S(1)}, u32[]{:S(2)}, u32[]{:S(2)}) collective-permute-start(bf16[3,128]{1,0:T(4,128)(2,1)S(1)} %slice.203), channel_id=1, source_target_pairs={{0,1},{1,2},{2,3},{3,4},{4,5},{5,6},{6,7},{7,8},{8,9},{9,10},{10,1... | collective-permute-start | bytes 2312 | tf_op jit(solution)/shard_map/ppermute | solution.py:16
  29.9 3.6 collective-permute-start.6
  33.5 3.6 collective-permute-start.8
  35.4 25.3 %collective-permute-start.5 = (f32[16,128,128]{2,1,0:T(8,128)S(1)}, f32[16,128,128]{2,1,0:T(8,128)S(1)}, u32[]{:S(2)}, u32[]{:S(2)}) collective-permute-start(f32[16,128,128]{2,1,0:T(8,128)S(1)} %add_select_fusion.2), channel_id=1, source_target_pairs={{0,2},{1,3},{2,0},{3,1},{4,6},{5,7},{6,4},{7,5},{8,10},{9,11},{10,... | collective-permute-start | bytes 3145736 | tf_op jit(solution)/shard_map/ppermute | solution.py:10
  37.2 24.4 %copy-start.1 = (f32[1027,2048]{1,0:T(8,128)S(1)}, f32[1027,2048]{1,0:T(8,128)}, u32[]{:S(2)}) copy-start(f32[1027,2048]{1,0:T(8,128)} %copy-done) | copy-start | bytes 25239556
  61.1 24.4 %collective-permute-start.7 = (f32[16,128,128]{2,1,0:T(8,128)S(1)}, f32[16,128,128]{2,1,0:T(8,128)S(1)}, u32[]{:S(2)}, u32[]{:S(2)}) collective-permute-start(f32[16,128,128]{2,1,0:T(8,128)S(1)} %get-tuple-element.425), channel_id=1, source_target_pairs={{0,4},{1,5},{2,6},{3,7},{4,0},{5,1},{6,2},{7,3},{8,12},{9,13},{10,... | collective-permute-start | bytes 3145736 | tf_op jit(solution)/shard_map/ppermute | solution.py:10
  86.9 5.6 %slice-start = ((bf16[15,16,1024]{2,1,0:T(8,128)(2,1)}), bf16[11,16,1024]{2,1,0:T(8,128)(2,1)S(1)}, s32[]{:S(2)}) async-start(bf16[15,16,1024]{2,1,0:T(8,128)(2,1)} %param.15), calls=%async_computation | async-start | bytes 720896 | tf_op jit(solution)/shard_map/slice | solution.py:95
  86.9 207.5 %collective-permute-start.9 = (f32[16,128,128]{2,1,0:T(8,128)}, f32[16,128,128]{2,1,0:T(8,128)}, u32[]{:S(2)}, u32[]{:S(2)}) collective-permute-start(f32[16,128,128]{2,1,0:T(8,128)} %get-tuple-element.427), channel_id=1, source_target_pairs={{0,8},{1,9},{2,10},{3,11},{4,12},{5,13},{6,14},{7,15},{8,0},{9,1},... | collective-permute-start | bytes 3145736 | tf_op jit(solution)/shard_map/ppermute | solution.py:10
  295.9 4.2 slice-start.1
where the time goes:
time: 442 us; the launch traced here: 439 us
  matrix products  217 us (49%)
  other arithmetic  86.5 us (20%)
  local copies, waits for them, and re-layouts  77.5 us (18%)
  waiting for transfers between devices  39.9 us (9%)
  starting transfers between devices  16.3 us (4%)
    dot_general x16, matrix products, near_part(): return jnp.dot(near_weight, own_values, preferred_element_type=jnp.float32)  201 us
    convert_element_type x16, other arithmetic, far_part(): far_query = (query_float[:, None, :] * far_scale.T[:, :, None]).astype(jn...  62.1 us
    ppermute x7, waiting for transfers between devices, partner(): lax.ppermute(x, axis, [(i, i ^ 1 << distance) for i in range(lax.axis_siz...  39.9 us
    dynamic_slice x32, local copies, waits for them, and re-layouts, far_step(): lax.dynamic_slice_in_dim(near_all, head_idx * head_width, head_width, 1)  20.3 us
    dynamic_slice x16, local copies, waits for them, and re-layouts, far_part(): lax.dynamic_index_in_dim(buckets, head_idx, 1, keepdims=False)  14.8 us
    dynamic_update_slice x32, local copies, waits for them, and re-layouts, finish(): lax.dynamic_update_slice_in_dim(output, normed.astype(jnp.bfloat16), head...  14.3 us
    dynamic_slice x16, local copies, waits for them, and re-layouts, finish(): lax.dynamic_slice_in_dim(norm_gain, head_idx * head_width, head_width, 0)  12.3 us
    ppermute x3, starting transfers between devices, from_behind(): return lax.ppermute(x, axis, pairs)  9.06 us
  transfers between devices with their start and end apart: 10, of which 4 were waited for; matrix products, arithmetic and copies ran while one was open for 51% of the time, Pallas kernels for 0%

commit v1 on v0

v1 whole, which is shorter than its diff:
```python
import functools

import jax
import jax.numpy as jnp
from jax import lax
from jax.experimental import pallas as pl
from jax.experimental.pallas import tpu as pltpu
from jax.sharding import PartitionSpec as P


EPSILON = 1e-05
TILE = 128
GROUP = 16
NEAR_CALLS = 2
STEP = 2
NEVER = -1e30


def log2(value):
    return value.bit_length() - 1


def whole(array):
    rank = array.ndim
    return pl.BlockSpec(array.shape, lambda i: (0,) * rank)


def shape_of(shape, dtype):
    return jax.ShapeDtypeStruct(shape, dtype)


def tile_decays(log_decay):
    length = log_decay.shape[1]
    row = lax.broadcasted_iota(jnp.int32, (TILE, TILE), 0)
    col = lax.broadcasted_iota(jnp.int32, (TILE, TILE), 1)
    parts = [log_decay[:, at : at + TILE] for at in range(0, length, TILE)]
    local = lax.dot_general(
        jnp.concatenate(parts, axis=0),
        (row <= col).astype(jnp.float32),
        (((1,), (0,)), ((), ())),
        precision=lax.Precision.HIGHEST,
        preferred_element_type=jnp.float32,
    )
    middle = jnp.broadcast_to(local[:, TILE // 2 - 1 : TILE // 2], local.shape)
    total = jnp.broadcast_to(local[:, TILE - 1 : TILE], local.shape)
    heads = log_decay.shape[0]

    def split(array):
        return [array[at : at + heads] for at in range(0, array.shape[0], heads)]

    return split(local), split(middle), split(total)


def pair_row(table, head, pair):
    sides = [table[2 * pair + side, pl.ds(head, 1), :] for side in range(2)]
    return jnp.concatenate(sides, axis=1)


def conv_tile(buf, weight, start):
    taps = weight.shape[0]
    total = None
    for tap in range(taps):
        term = weight[tap : tap + 1, :] * buf[pl.ds(8 - (taps - 1) + tap + start, TILE), :]
        total = term if total is None else total + term
    return total + total * jnp.tanh(total)


def fill(buf, source, rim):
    length = source.shape[0]
    buf[pl.ds(8 - rim.shape[0], rim.shape[0]), :] = rim[...].astype(jnp.float32)
    buf[pl.ds(8, length), :] = source[...].astype(jnp.float32)


def state_keys(pairs):
    return [
        (bit, first)
        for bit in range(log2(pairs))
        for first in range(0, pairs, 2 << bit)
    ]


def three_terms(wide):
    terms = []
    for _ in range(3):
        term = wide.astype(jnp.bfloat16)
        terms.append(term)
        wide = wide - term.astype(jnp.float32)
    terms.append(jnp.zeros_like(terms[0]))
    return jnp.concatenate(terms, axis=0)


def sum_terms(terms):
    each = terms.shape[0] // 4
    wide = terms.astype(jnp.float32)
    return wide[:each] + wide[each : 2 * each] + wide[2 * each : 3 * each]


def state_kernel(
    q_ref, k_ref, v_ref, rq_ref, rk_ref, rv_ref, wq_ref, wk_ref, wv_ref, ld_ref,
    vt_ref, st_ref, g_ref, qt_ref, kc_ref,
    buf, scale, total,
):
    step = pl.program_id(0)
    heads = ld_ref.shape[0]
    length = v_ref.shape[0]
    width = v_ref.shape[1] // STEP
    pairs = length // (2 * TILE)

    @pl.when(step == 0)
    def _():
        local, _, totals = tile_decays(ld_ref[...])
        summed = None
        for pair in range(pairs):
            low, high = 2 * pair, 2 * pair + 1
            scale[low] = jnp.exp(totals[low] - local[low] + totals[high])
            scale[high] = jnp.exp(totals[high] - local[high])
            both = totals[low] + totals[high]
            total[pair] = jnp.exp(both)
            summed = both if summed is None else summed + both
        g_ref[pl.ds(heads * width, 4 * heads), :] = three_terms(summed)
        fill(buf.at[0], q_ref, rq_ref)
        fill(buf.at[1], k_ref, rk_ref)
        for tile in range(length // TILE):
            at = tile * TILE
            done = conv_tile(buf.at[0], 0.5 * wq_ref[...], at).astype(jnp.bfloat16)
            qt_ref[:, at : at + TILE] = done.T
            kc_ref[at : at + TILE, :] = conv_tile(buf.at[1], 0.5 * wk_ref[...], at).astype(jnp.bfloat16)

    for place in range(STEP):
        lanes = slice(place * width, (place + 1) * width)
        fill(buf.at[place], v_ref.at[:, lanes], rv_ref.at[:, lanes])
    for place in range(STEP):
        head = step * STEP + place
        lanes = slice(place * width, (place + 1) * width)
        weight = 0.5 * wv_ref[:, lanes]
        states = {}
        for pair in range(pairs):
            at = 2 * pair * TILE
            sides = []
            for start in (at, at + TILE):
                done = conv_tile(buf.at[place], weight, start).astype(jnp.bfloat16).T
                vt_ref[lanes, start : start + TILE] = done
                sides.append(done)
            row = pair_row(scale, head, pair).astype(jnp.bfloat16)
            states[(0, pair)] = jnp.dot(
                jnp.concatenate(sides, axis=1) * row,
                kc_ref[at : at + 2 * TILE, :],
                preferred_element_type=jnp.float32,
            )
        decay = [total[pair, pl.ds(head, 1), :] for pair in range(pairs)]
        for bit in range(log2(pairs)):
            for first in range(0, pairs, 2 << bit):
                keep = states[(bit, first + (1 << bit))]
                factor = decay[first + (1 << bit)]
                for later in range(first + (1 << bit) + 1, first + (2 << bit)):
                    factor = factor * decay[later]
                states[(bit + 1, first)] = keep + factor * states[(bit, first)]
        for order, key in enumerate(state_keys(pairs)):
            st_ref[order, lanes, :] = states[key].astype(jnp.bfloat16)
        at = pl.multiple_of(head * width, width)
        g_ref[pl.ds(at, width), :] = states[(log2(pairs), 0)].astype(jnp.bfloat16)


def table_rows(length):
    inner = log2(GROUP) + 1
    groups = TILE // GROUP
    states = log2(length // (2 * TILE))
    return {
        "inner": 0,
        "group": inner,
        "sibling": inner + groups,
        "value": inner + groups + 1,
        "state": inner + groups + 2,
        "size": inner + groups + 2 + states,
    }


def table_kernel(ld_ref, lw_ref, tab_ref, far_ref):
    heads, length = ld_ref.shape
    levels = lw_ref.shape[0]
    pairs = length // (2 * TILE)
    rows = table_rows(length)
    inner = log2(GROUP) + 1
    tile_level = log2(TILE)
    locals_, middles, totals = tile_decays(ld_ref[...])
    block = lax.broadcasted_iota(jnp.int32, (heads, TILE), 1) // GROUP
    zero = jnp.zeros((heads, TILE), jnp.float32)
    pair_total = []
    running = zero
    for pair in range(pairs):
        low = 2 * pair
        for tile in (low, low + 1):
            lanes = pl.ds(tile * TILE, TILE)
            weight = [lw_ref[level, :, lanes].astype(jnp.float32) for level in range(levels)]
            local = locals_[tile]
            gap = jnp.exp(local - middles[tile])
            scaled = [weight[level] * gap for level in range(tile_level + 1)]
            for level in range(inner):
                tab_ref[rows["inner"] + level, tile] = scaled[level]
            for group in range(TILE // GROUP):
                base = zero
                differ = block ^ group
                for level in range(inner, tile_level + 1):
                    least = 1 << (level - inner)
                    here = (differ >= least) & (differ < 2 * least) & (block > group)
                    base = jnp.where(here, scaled[level], base)
                tab_ref[rows["group"] + group, tile] = base
            tab_ref[rows["value"], tile] = jnp.exp(middles[tile] - local)
            if tile == low:
                tab_ref[rows["sibling"], tile] = zero
            else:
                tab_ref[rows["sibling"], tile] = weight[tile_level + 1] * jnp.exp(
                    local + totals[low] - middles[low]
                )
                local = local + totals[low]
            for bit in range(log2(pairs)):
                since = zero
                for other in range(pair >> bit << bit, pair):
                    since = since + pair_total[other]
                tab_ref[rows["state"] + bit, tile] = weight[tile_level + 2 + bit] * jnp.exp(
                    local + since
                )
            whole_decay = jnp.exp(local + running)
            first = log2(length) + 1
            for level in range(first, levels):
                far_ref[level - first, tile] = weight[level] * whole_decay
        pair_total.append(totals[low] + totals[low + 1])
        running = running + pair_total[-1]


def near_kernel(first_head, vt_ref, st_ref, tab_ref, kc_ref, qt_ref, *refs):
    near_ref, sc, mix, rest = refs[-4:]
    length = vt_ref.shape[1]
    width = vt_ref.shape[0] // STEP
    pairs = length // (2 * TILE)
    rows = table_rows(length)
    inner = log2(GROUP) + 1
    row = lax.broadcasted_iota(jnp.int32, (GROUP, TILE), 0)
    lane = lax.broadcasted_iota(jnp.int32, (GROUP, TILE), 1)
    within = lane % GROUP
    differ = row ^ within
    keys = state_keys(pairs)

    @pl.when(pl.program_id(0) == 0)
    def _():
        for pair in range(pairs):
            at = 2 * pair * TILE
            sc[pair] = jnp.dot(
                kc_ref[at : at + 2 * TILE, :],
                qt_ref[:, at : at + 2 * TILE],
                preferred_element_type=jnp.float32,
            ).astype(jnp.bfloat16)
            for place in range(STEP):
                mix[place, pair, TILE:, 0:TILE] = jnp.zeros((TILE, TILE), jnp.bfloat16)

    def one_head(place):
        head = first_head + pl.program_id(0) * STEP + place
        own = slice(place * width, (place + 1) * width)

        def table(order, tile):
            return tab_ref[order, tile, pl.ds(head, 1), :]

        for pair in range(pairs):
            at = 2 * pair * TILE
            for side in range(2):
                tile = 2 * pair + side
                diagonal = jnp.where(differ == 0, table(rows["inner"], tile), 0.0)
                for level in range(1, inner):
                    here = (differ >= 1 << (level - 1)) & (differ < 1 << level) & (row < within)
                    diagonal = jnp.where(here, table(rows["inner"] + level, tile), diagonal)
                lanes = slice(side * TILE, (side + 1) * TILE)
                for group in range(TILE // GROUP):
                    base = table(rows["group"] + group, tile)
                    weight = jnp.where(lane // GROUP == group, diagonal, base).astype(jnp.bfloat16)
                    start = side * TILE + group * GROUP
                    mix[place, pair, start : start + GROUP, lanes] = (
                        sc[pair, start : start + GROUP, lanes] * weight
                    )
            mix[place, pair, 0:TILE, TILE:] = sc[pair, 0:TILE, TILE:] * table(
                rows["sibling"], 2 * pair + 1
            ).astype(jnp.bfloat16)
            value = vt_ref[own, at : at + 2 * TILE] * pair_row(
                tab_ref.at[rows["value"]], head, pair
            ).astype(jnp.bfloat16)
            summed = jnp.dot(value, mix[place, pair], preferred_element_type=jnp.float32)
            active = [bit for bit in range(log2(pairs)) if pair >> bit & 1]
            if active:
                held = []
                for order, bit in enumerate(active):
                    scale = pair_row(tab_ref.at[rows["state"] + bit], head, pair).astype(jnp.bfloat16)
                    rest[place, pair, order * TILE : (order + 1) * TILE, :] = (
                        qt_ref[:, at : at + 2 * TILE] * scale
                    )
                    held.append(st_ref[keys.index((bit, pair >> bit + 1 << bit + 1)), own, :])
                summed = summed + jnp.dot(
                    jnp.concatenate(held, axis=1),
                    rest[place, pair, 0 : len(active) * TILE, :],
                    preferred_element_type=jnp.float32,
                )
            near_ref[own, at : at + 2 * TILE] = summed.astype(jnp.bfloat16)

    for place in range(STEP):
        one_head(place)


def far_kernel(place_ref, near_ref, own_ref, high_ref, far_ref, qt_ref, off_ref, gain_ref, *refs):
    out_ref, rest = refs[-2:]
    bits = far_ref.shape[0]
    length = qt_ref.shape[1]
    width = near_ref.shape[0] // STEP
    for place in range(STEP):
        own = slice(place * width, (place + 1) * width)
        head = (place_ref[0] + pl.program_id(0)) * STEP + place
        held = jnp.concatenate(
            [own_ref[own, :]] + [high_ref[bit, own, :] for bit in range(bits - 1)], axis=1
        )
        gain = jnp.broadcast_to(gain_ref[:, own], (TILE, TILE)).T
        factors = []
        for bit in range(bits):
            factor = jnp.exp(off_ref[bit, pl.ds(head, 1), :])
            factors.append(jnp.concatenate([factor, factor], axis=1))
        for pair in range(length // (2 * TILE)):
            at = 2 * pair * TILE
            for bit in range(bits):
                row = (pair_row(far_ref.at[bit], head, pair) * factors[bit]).astype(jnp.bfloat16)
                rest[place, pair, bit * TILE : (bit + 1) * TILE, :] = qt_ref[:, at : at + 2 * TILE] * row
            summed = near_ref[own, at : at + 2 * TILE].astype(jnp.float32) + jnp.dot(
                held, rest[place, pair], preferred_element_type=jnp.float32
            )
            mean = jnp.mean(summed * summed, axis=0, keepdims=True)
            normed = summed * lax.rsqrt(mean + EPSILON)
            for side in range(2):
                part = normed[:, side * TILE : (side + 1) * TILE] * gain
                start = at + side * TILE
                out_ref[start : start + TILE, own] = part.astype(jnp.bfloat16).T


def send(x, by, size):
    return lax.ppermute(x, "seq", [(i, i ^ by) for i in range(size)])


def shift(x, by, size):
    return lax.ppermute(x, "seq", [(i, i + by) for i in range(size - by)])


def at_rows(x, first, count):
    return lax.dynamic_slice_in_dim(x, first, count, 0)


def grow(decay, first, count, width):
    return jnp.repeat(jnp.exp(at_rows(decay, first, count)), width)[:, None]


def on_device(
    query_inputs, key_inputs, value_inputs, log_decay, level_weight, conv_weight, norm_gain
):
    length, state_dim = query_inputs.shape
    heads = log_decay.shape[0]
    values_dim = value_inputs.shape[1]
    width = values_dim // heads
    taps = conv_weight.shape[0]
    rim = taps - 1
    size = lax.axis_size("seq")
    bits = log2(size)
    pairs = length // (2 * TILE)
    keys = state_keys(pairs)
    half, quarter = values_dim // 2, values_dim // 4
    half_heads, quarter_heads = heads // 2, heads // 4
    tail = 4 * heads
    index = lax.axis_index("seq")
    core, side, plane = index & 1, index >> 1 & 1, index >> 2
    planes = size // 4
    rows = table_rows(length)
    calls = NEAR_CALLS if heads % NEAR_CALLS == 0 else 1
    each = heads // calls
    zero = jnp.zeros((heads,), jnp.float32)
    upper_core, upper_side = core == 1, side == 1

    own_rim = jnp.concatenate(
        [query_inputs[length - rim :], key_inputs[length - rim :], value_inputs[length - rim :]],
        axis=1,
    )
    rims = shift(own_rim, 1, size)

    tab, far_tab = pl.pallas_call(
        table_kernel,
        out_shape=[
            shape_of((rows["size"], length // TILE, heads, TILE), jnp.float32),
            shape_of((bits, length // TILE, heads, TILE), jnp.float32),
        ],
        cost_estimate=pl.CostEstimate(flops=10**9, bytes_accessed=3 * 10**6, transcendentals=0),
        name="tables",
    )(log_decay, level_weight)

    vt, st, group, qt, kc = pl.pallas_call(
        state_kernel,
        grid=(heads // STEP,),
        in_specs=[
            whole(query_inputs),
            whole(key_inputs),
            pl.BlockSpec((length, STEP * width), lambda i: (0, i)),
            pl.BlockSpec((rim, state_dim), lambda i: (0, 0)),
            pl.BlockSpec((rim, state_dim), lambda i: (0, 1)),
            pl.BlockSpec((rim, STEP * width), lambda i: (0, 2 * state_dim // (STEP * width) + i)),
            pl.BlockSpec((taps, state_dim), lambda i: (0, 0)),
            pl.BlockSpec((taps, state_dim), lambda i: (0, 1)),
            pl.BlockSpec((taps, STEP * width), lambda i: (0, 2 * state_dim // (STEP * width) + i)),
            whole(log_decay),
        ],
        out_specs=[
            pl.BlockSpec((STEP * width, length), lambda i: (i, 0)),
            pl.BlockSpec((len(keys), STEP * width, state_dim), lambda i: (0, i, 0)),
            pl.BlockSpec((values_dim + tail, state_dim), lambda i: (0, 0)),
            pl.BlockSpec((state_dim, length), lambda i: (0, 0)),
            pl.BlockSpec((length, state_dim), lambda i: (0, 0)),
        ],
        out_shape=[
            shape_of((values_dim, length), jnp.bfloat16),
            shape_of((len(keys), values_dim, state_dim), jnp.bfloat16),
            shape_of((values_dim + tail, state_dim), jnp.bfloat16),
            shape_of((state_dim, length), jnp.bfloat16),
            shape_of((length, state_dim), jnp.bfloat16),
        ],
        scratch_shapes=[
            pltpu.VMEM((STEP, length + 8, TILE), jnp.float32),
            pltpu.VMEM((length // TILE, heads, TILE), jnp.float32),
            pltpu.VMEM((pairs, heads, TILE), jnp.float32),
        ],
        cost_estimate=pl.CostEstimate(flops=10**9, bytes_accessed=9 * 10**6, transcendentals=0),
        name="state",
    )(
        query_inputs, key_inputs, value_inputs, rims, rims, rims,
        conv_weight, conv_weight, conv_weight, log_decay,
    )

    near = None
    for call in range(calls):
        first = call * each // STEP
        before = [] if near is None else [near]
        near = pl.pallas_call(
            functools.partial(near_kernel, call * each),
            grid=(each // STEP,),
            in_specs=[
                pl.BlockSpec((STEP * width, length), lambda i, first=first: (first + i, 0)),
                pl.BlockSpec(
                    (len(keys), STEP * width, state_dim), lambda i, first=first: (0, first + i, 0)
                ),
                whole(tab),
                whole(kc),
                whole(qt),
            ]
            + [pl.BlockSpec(memory_space=pl.ANY) for _ in before],
            out_specs=pl.BlockSpec((STEP * width, length), lambda i, first=first: (first + i, 0)),
            out_shape=shape_of((values_dim, length), jnp.bfloat16),
            scratch_shapes=[
                pltpu.VMEM((pairs, 2 * TILE, 2 * TILE), jnp.bfloat16),
                pltpu.VMEM((STEP, pairs, 2 * TILE, 2 * TILE), jnp.bfloat16),
                pltpu.VMEM((STEP, pairs, log2(pairs) * state_dim, 2 * TILE), jnp.bfloat16),
            ],
            input_output_aliases={5: 0} if before else {},
            cost_estimate=pl.CostEstimate(flops=10**9, bytes_accessed=4 * 10**6, transcendentals=0),
            name="near",
        )(vt, st, tab, kc, qt, *before)

    other = send(group, 1, size)
    total = sum_terms(group[values_dim:])[:, 0]
    other_total = sum_terms(other[values_dim:])[:, 0]
    first_head = core * half_heads
    own_half = at_rows(group, core * half, half).astype(jnp.float32)
    other_half = at_rows(other, core * half, half).astype(jnp.float32)
    chip = jnp.where(
        upper_core,
        own_half + grow(total, first_head, half_heads, width) * other_half,
        other_half + grow(other_total, first_head, half_heads, width) * own_half,
    ).astype(jnp.bfloat16)
    chip_total = total + other_total
    in_chip = jnp.where(upper_core, other_total, zero)
    offsets = [jnp.where(upper_core, zero, NEVER), jnp.where(upper_side, in_chip, NEVER)]

    def with_total(state, decay):
        wide = jnp.broadcast_to(decay[:, None], (heads, state_dim))
        return jnp.concatenate([state, three_terms(wide)], axis=0)

    mine = at_rows(chip, side * quarter, quarter)
    theirs = at_rows(chip, (1 - side) * quarter, quarter)
    got = send(with_total(theirs, chip_total), 2, size)
    got_rest = send(mine, 2, size)
    got_mine, got_total = got[:quarter], sum_terms(got[quarter:])[:, 0]
    my_head = first_head + side * quarter_heads
    mine_wide, got_wide = mine.astype(jnp.float32), got_mine.astype(jnp.float32)
    flat = jnp.where(
        upper_side,
        mine_wide + grow(chip_total, my_head, quarter_heads, width) * got_wide,
        got_wide + grow(got_total, my_head, quarter_heads, width) * mine_wide,
    ).astype(jnp.bfloat16)
    in_plane = in_chip + jnp.where(upper_side, got_total, zero)

    message = with_total(flat, chip_total + got_total)
    came = []
    for by in range(1, planes):
        came.append(shift(message, 4 * by, size))
    parts = []
    for bit in range(log2(planes)):
        summed = jnp.zeros((quarter, state_dim), jnp.float32)
        between = zero
        upper = plane >> bit & 1 == 1
        for by in range(1, planes):
            source = plane - by
            here = (
                upper
                & (source >= 0)
                & (source >> (bit + 1) == plane >> (bit + 1))
                & (source >> bit & 1 == 0)
            )
            factor = grow(jnp.where(here, between, NEVER), my_head, quarter_heads, width)
            summed = summed + factor * came[by - 1][:quarter].astype(jnp.float32)
            between = between + sum_terms(came[by - 1][quarter:])[:, 0]
        parts.append(summed.astype(jnp.bfloat16))
        offsets.append(jnp.where(upper, in_plane, NEVER))

    halves = [jnp.concatenate([got_rest, got_mine], axis=0)[None]]
    if parts:
        part = jnp.stack(parts)
        swapped = send(part, 2, size)
        halves.append(
            jnp.where(
                upper_side,
                jnp.concatenate([swapped, part], axis=1),
                jnp.concatenate([part, swapped], axis=1),
            )
        )
    high = jnp.concatenate(halves, axis=0)
    high_other = send(high, 1, size)

    off = jnp.broadcast_to(jnp.stack(offsets)[:, :, None], (bits, heads, TILE))
    gain = norm_gain.reshape(1, values_dim)
    out = None
    for first, states in ((core, high), (1 - core, high_other)):
        before = [] if out is None else [out]
        out = pl.pallas_call(
            far_kernel,
            grid_spec=pltpu.PrefetchScalarGridSpec(
                num_scalar_prefetch=1,
                grid=(half_heads // STEP,),
                in_specs=[
                    pl.BlockSpec((STEP * width, length), lambda i, s: (s[0] + i, 0)),
                    pl.BlockSpec((STEP * width, state_dim), lambda i, s: (s[0] + i, 0)),
                    pl.BlockSpec((bits - 1, STEP * width, state_dim), lambda i, s: (0, i, 0)),
                    pl.BlockSpec(far_tab.shape, lambda i, s: (0, 0, 0, 0)),
                    pl.BlockSpec(qt.shape, lambda i, s: (0, 0)),
                    pl.BlockSpec(off.shape, lambda i, s: (0, 0, 0)),
                    pl.BlockSpec((1, STEP * width), lambda i, s: (0, s[0] + i)),
                ]
                + [pl.BlockSpec(memory_space=pl.ANY) for _ in before],
                out_specs=pl.BlockSpec((length, STEP * width), lambda i, s: (0, s[0] + i)),
                scratch_shapes=[pltpu.VMEM((STEP, pairs, bits * state_dim, 2 * TILE), jnp.bfloat16)],
            ),
            out_shape=shape_of((length, values_dim), jnp.bfloat16),
            input_output_aliases={8: 0} if before else {},
            cost_estimate=pl.CostEstimate(flops=10**9, bytes_accessed=6 * 10**6, transcendentals=0),
            name="far",
        )((first * half_heads // STEP)[None], near, other, states, far_tab, qt, off, gain, *before)
    return out


def solution(mesh):
    return jax.shard_map(
        on_device,
        mesh=mesh,
        in_specs=(
            P(("grp", "seq"), None),
            P(("grp", "seq"), None),
            P(("grp", "seq"), None),
            P(None, ("grp", "seq")),
            P(None, None, ("grp", "seq")),
            P(),
            P(),
        ),
        out_specs=P(("grp", "seq"), None),
        check_vma=False,
    )
```

time: 442 us -> 88.2 us (0.20)
  the two profiles are of different devices: /device:TPU:0 before, /device:TPU:17 now
where the time goes in v1:
time: 88.2 us; the launch traced here: 87.3 us
  Pallas kernels  35.5 us (40%)
  waiting for transfers between devices  27.8 us (32%)
  starting transfers between devices  14.3 us (16%)
  local copies, waits for them, and re-layouts  5.81 us (7%)
  other arithmetic  3.55 us (4%)
    ppermute x5, waiting for transfers between devices, send(): return lax.ppermute(x, 'seq', [(i, i ^ by) for i in range(size)])  14.3 us
    ppermute x4, waiting for transfers between devices, shift(): return lax.ppermute(x, 'seq', [(i, i + by) for i in range(size - by)])  13.6 us
    pallas_call x2, Pallas kernels, on_device(): pl.pallas_call(functools.partial(near_kernel, call * each), grid=(each //...  11.5 us
    pallas_call x2, Pallas kernels, on_device(): pl.pallas_call(far_kernel, grid_spec=pltpu.PrefetchScalarGridSpec(num_sca...  11.1 us
    pallas_call x1, Pallas kernels, on_device(): pl.pallas_call(state_kernel, grid=(heads // STEP,), in_specs=[whole(query...  10.3 us
    ppermute x4, starting transfers between devices, shift(): return lax.ppermute(x, 'seq', [(i, i + by) for i in range(size - by)])  8.87 us
    ppermute x5, starting transfers between devices, send(): return lax.ppermute(x, 'seq', [(i, i ^ by) for i in range(size)])  5.47 us
    pallas_call x1, Pallas kernels, on_device(): pl.pallas_call(table_kernel, out_shape=[shape_of((rows['size'], length //...  2.61 us
  transfers between devices with their start and end apart: 9, of which 6 were waited for; matrix products, arithmetic and copies ran while one was open for 3% of the time, Pallas kernels for 22%

profile of v1, /device:TPU:17, one launch (start us, length us, event | category | flops | bytes accessed | tf_op | source)
XLA Modules:
  0.0 87.3 jit_solution(15441197326655708497)
XLA Ops:
  0.0 0.8 slice.111
  0.8 0.7 slice.110
  1.5 0.7 slice.109
  2.2 3.7 %collective-permute-start = (bf16[3,2304]{1,0:T(4,128)(2,1)S(1)}, bf16[3,2304]{1,0:T(4,128)(2,1)S(1)}, u32[]{:S(2)}, u32[]{:S(2)}) collective-permute-start(bf16[3,2304]{1,0:T(4,128)(2,1)S(1)} %pad_maximum_fusion.2), channel_id=1, source_target_pairs={{0,1},{1,2},{2,3},{3,4},{4,5},{5,6},{6,7},{7,8},{8,9},{9,10},{10,1... | collective-permute-start | bytes 41480 | tf_op jit(solution)/shard_map/ppermute | solution.py:343
  5.9 0.9 collective-permute-done.rq_ref.rk_ref.rv_ref
  6.8 0.6 copy-done.3
  7.3 10.3 %state.1 = (bf16[2048,1024]{1,0:T(8,128)(2,1)}, bf16[3,2048,128]{2,1,0:T(8,128)(2,1)}, bf16[2112,128]{1,0:T(8,128)(2,1)}, bf16[128,1024]{1,0:T(8,128)(2,1)}, bf16[1024,128]{1,0:T(8,128)(2,1)}) custom-call(bf16[1024,128]{1,0:T(8,128)(2,1)} %q_ref.1, bf16[1024,128]{1,0:T(8,128)(2,1)} %k_ref.1, bf16[1024,2048]{1,0:T(8,128)(2,1)} %v_ref.1, ...), custom_call_target="tpu_custom_call" | custom-call | flops 1000000000 | bytes 9000000 | tf_op jit(solution)/shard_map/state/pallas_call | solution.py:395
  17.7 2.1 %collective-permute-start.1 = (bf16[2112,128]{1,0:T(8,128)(2,1)}, bf16[2112,128]{1,0:T(8,128)(2,1)S(1)}, u32[]{:S(2)}, u32[]{:S(2)}) collective-permute-start(bf16[2112,128]{1,0:T(8,128)(2,1)} %get-tuple-element.17), channel_id=1, source_target_pairs={{0,1},{1,0},{2,3},{3,2},{4,5},{5,4},{6,7},{7,6},{8,9},{9,8},{10,11... | collective-permute-start | bytes 1622024 | tf_op jit(solution)/shard_map/ppermute | solution.py:339
  19.8 0.7 slice_convert_fusion.4
  20.5 1.0 %collective-permute-done.1.own_ref = bf16[2112,128]{1,0:T(8,128)(2,1)S(1)} collective-permute-done((bf16[2112,128]{1,0:T(8,128)(2,1)}, bf16[2112,128]{1,0:T(8,128)(2,1)S(1)}, u32[]{:S(2)}, u32[]{:S(2)}) %collective-permute-start.1) | collective-permute-done | bytes 540704 | tf_op jit(solution)/shard_map/ppermute | solution.py:339
  22.0 1.3 %fusion.1 = bf16[1024,128]{1,0:T(8,128)(2,1)S(1)} fusion(f32[1024]{0:T(1024)S(1)} %broadcast_bitcast_fusion, bf16[2112,128]{1,0:T(8,128)(2,1)S(1)} %collective-permute-done.1.own_ref, s32[]{:T(128)S(6)} %select_n.191, f32[1024]{0:T(1024)S(1)} %broadcast_bitcast_fusion.1, bf16[2112,128]{1,0:T(8,128)(2,1)} %get-tuple-element.17, pred[]{:T(512)S(6)} %eq.48), kind=kLoop, calls=%fused_computation.6 | loop fusion | flops 1048576 | bytes 794629 | tf_op jit(solution)/shard_map/convert_element_type | solution.py:475
  23.6 0.4 collective-permute-start.3
  24.2 4.5 %collective-permute-done.3 = bf16[576,128]{1,0:T(8,128)(2,1)S(1)} collective-permute-done((bf16[576,128]{1,0:T(8,128)(2,1)S(1)}, bf16[576,128]{1,0:T(8,128)(2,1)S(1)}, u32[]{:S(2)}, u32[]{:S(2)}) %collective-permute-start.3) | collective-permute-done | bytes 147488 | tf_op jit(solution)/shard_map/ppermute | solution.py:339
  29.0 0.2 fusion.12
  29.5 1.3 %collective-permute-start.5 = (bf16[576,128]{1,0:T(8,128)(2,1)S(1)}, bf16[576,128]{1,0:T(8,128)(2,1)S(1)}, u32[]{:S(2)}, u32[]{:S(2)}) collective-permute-start(bf16[576,128]{1,0:T(8,128)(2,1)S(1)} %constant_dynamic-update-slice_fusion.4), channel_id=1, source_target_pairs={{0,8},{1,9},{2,10},{3,11},{4,12},{5,13},{6,14},{7,15},{16,24},{17,... | collective-permute-start | bytes 442376 | tf_op jit(solution)/shard_map/ppermute | solution.py:343
  30.9 3.2 %collective-permute-start.4 = (bf16[576,128]{1,0:T(8,128)(2,1)S(1)}, bf16[576,128]{1,0:T(8,128)(2,1)S(1)}, u32[]{:S(2)}, u32[]{:S(2)}) collective-permute-start(bf16[576,128]{1,0:T(8,128)(2,1)S(1)} %constant_dynamic-update-slice_fusion.4), channel_id=1, source_target_pairs={{0,4},{1,5},{2,6},{3,7},{4,8},{5,9},{6,10},{7,11},{8,12},{9,13},{1... | collective-permute-start | bytes 442376 | tf_op jit(solution)/shard_map/ppermute | solution.py:343
  34.1 0.7 collective-permute-start.6
  34.8 1.5 %collective-permute-done.5 = bf16[576,128]{1,0:T(8,128)(2,1)S(1)} collective-permute-done((bf16[576,128]{1,0:T(8,128)(2,1)S(1)}, bf16[576,128]{1,0:T(8,128)(2,1)S(1)}, u32[]{:S(2)}, u32[]{:S(2)}) %collective-permute-start.5) | collective-permute-done | bytes 147488 | tf_op jit(solution)/shard_map/ppermute | solution.py:343
  36.4 11.2 %collective-permute-done.4 = bf16[576,128]{1,0:T(8,128)(2,1)S(1)} collective-permute-done((bf16[576,128]{1,0:T(8,128)(2,1)S(1)}, bf16[576,128]{1,0:T(8,128)(2,1)S(1)}, u32[]{:S(2)}, u32[]{:S(2)}) %collective-permute-start.4) | collective-permute-done | bytes 147488 | tf_op jit(solution)/shard_map/ppermute | solution.py:343
  47.8 0.2 exponential_reduce_fusion.5
  48.2 0.3 fusion.11
  48.6 0.4 collective-permute-start.7
  49.0 1.1 %collective-permute-start.2 = (bf16[512,128]{1,0:T(8,128)(2,1)S(1)}, bf16[512,128]{1,0:T(8,128)(2,1)S(1)}, u32[]{:S(2)}, u32[]{:S(2)}) collective-permute-start(bf16[512,128]{1,0:T(8,128)(2,1)S(1)} %get-tuple-element.31), channel_id=1, source_target_pairs={{0,2},{1,3},{2,0},{3,1},{4,6},{5,7},{6,4},{7,5},{8,10},{9,11},{10,... | collective-permute-start | bytes 393224 | tf_op jit(solution)/shard_map/ppermute | solution.py:339
  50.1 8.7 %collective-permute-done.2 = bf16[512,128]{1,0:T(8,128)(2,1)S(1)} collective-permute-done((bf16[512,128]{1,0:T(8,128)(2,1)S(1)}, bf16[512,128]{1,0:T(8,128)(2,1)S(1)}, u32[]{:S(2)}, u32[]{:S(2)}) %collective-permute-start.2) | collective-permute-done | bytes 131104 | tf_op jit(solution)/shard_map/ppermute | solution.py:339
  59.1 1.4 %collective-permute-start.8 = (bf16[3,1024,128]{2,1,0:T(8,128)(2,1)S(1)}, bf16[3,1024,128]{2,1,0:T(8,128)(2,1)S(1)}, u32[]{:S(2)}, u32[]{:S(2)}) collective-permute-start(bf16[3,1024,128]{2,1,0:T(8,128)(2,1)S(1)} %pad_maximum_fusion.high_ref), channel_id=1, source_target_pairs={{0,1},{1,0},{2,3},{3,2},{4,5},{5,4},{6,7},{7,6},{8,9},{9,8},{10,11... | collective-permute-start | bytes 2359304 | tf_op jit(solution)/shard_map/ppermute | solution.py:339
  60.5 2.6 %tables.1 = (f32[17,8,16,128]{3,2,1,0:T(8,128)}, f32[4,8,16,128]{3,2,1,0:T(8,128)}) custom-call(f32[16,1024]{1,0:T(8,128)} %ld_ref.3, bf16[15,16,1024]{2,1,0:T(8,128)(2,1)} %lw_ref.1), custom_call_target="tpu_custom_call" | custom-call | flops 1000000000 | bytes 3000000 | tf_op jit(solution)/shard_map/tables/pallas_call | solution.py:385
  63.1 5.7 %near.2.refs_0_ = bf16[2048,1024]{1,0:T(8,128)(2,1)} custom-call(bf16[2048,1024]{1,0:T(8,128)(2,1)} %get-tuple-element.12.vt_ref, bf16[3,2048,128]{2,1,0:T(8,128)(2,1)} %get-tuple-element.13.st_ref, f32[17,8,16,128]{3,2,1,0:T(8,128)} %get-tuple-element.14.tab_ref, bf16[1024,128]{1,0:T(8,128)(2,1)} %get-tuple-element.15.kc_ref, ...), custom_call_target="tpu_custom_call" | custom-call | flops 1000000000 | bytes 4000000 | tf_op jit(solution)/shard_map/near/pallas_call | solution.py:440
  68.8 5.7 %near.3.near_ref = bf16[2048,1024]{1,0:T(8,128)(2,1)} custom-call(bf16[2048,1024]{1,0:T(8,128)(2,1)} %get-tuple-element.12.vt_ref, bf16[3,2048,128]{2,1,0:T(8,128)(2,1)} %get-tuple-element.13.st_ref, f32[17,8,16,128]{3,2,1,0:T(8,128)} %get-tuple-element.14.tab_ref, bf16[1024,128]{1,0:T(8,128)(2,1)} %get-tuple-element.15.kc_ref, ...), custom_call_target="tpu_custom_call", output_to_operand_aliasing={{}: (5, {})} | custom-call | flops 1000000000 | bytes 4000000 | tf_op jit(solution)/shard_map/near/pallas_call | solution.py:440
  74.7 0.7 broadcast_in_dim.97.off_ref
  75.3 5.5 %far.2.refs_0_ = bf16[1024,2048]{1,0:T(8,128)(2,1)} custom-call(s32[1]{0:T(128)} %bitcast.13.place_ref, bf16[2048,1024]{1,0:T(8,128)(2,1)} %near.3.near_ref, bf16[2112,128]{1,0:T(8,128)(2,1)} %copy-done, bf16[3,1024,128]{2,1,0:T(8,128)(2,1)} %copy-done.1, f32[4,8,16,128]{3,2,1,0:T(8,128)} %get-tuple-element.18.far_ref, ...), custom_call_target="tpu_custom_call" | custom-call | flops 1000000000 | bytes 6000000 | tf_op jit(solution)/shard_map/far/pallas_call | solution.py:540
  80.9 0.9 %copy-done.2 = bf16[3,1024,128]{2,1,0:T(8,128)(2,1)} copy-done((bf16[3,1024,128]{2,1,0:T(8,128)(2,1)}, bf16[3,1024,128]{2,1,0:T(8,128)(2,1)S(1)}, u32[]{:S(2)}) %copy-start.2) | copy-done | bytes 786456
  81.8 5.6 %far.3 = bf16[1024,2048]{1,0:T(8,128)(2,1)} custom-call(s32[1]{0:T(128)} %bitcast.place_ref, bf16[2048,1024]{1,0:T(8,128)(2,1)} %near.3.near_ref, bf16[2112,128]{1,0:T(8,128)(2,1)} %copy-done, bf16[3,1024,128]{2,1,0:T(8,128)(2,1)} %copy-done.2, f32[4,8,16,128]{3,2,1,0:T(8,128)} %get-tuple-element.18.far_ref, ...), custom_call_target="tpu_custom_call", output_to_operand_aliasing={{}: (8, {})} | custom-call | flops 1000000000 | bytes 6000000 | tf_op jit(solution)/shard_map/far/pallas_call | solution.py:540
  (51 shorter events, 2.3 us)
Async XLA Ops:
  2.2 4.6 %collective-permute-start = (bf16[3,2304]{1,0:T(4,128)(2,1)S(1)}, bf16[3,2304]{1,0:T(4,128)(2,1)S(1)}, u32[]{:S(2)}, u32[]{:S(2)}) collective-permute-start(bf16[3,2304]{1,0:T(4,128)(2,1)S(1)} %pad_maximum_fusion.2), channel_id=1, source_target_pairs={{0,1},{1,2},{2,3},{3,4},{4,5},{5,6},{6,7},{7,8},{8,9},{9,10},{10,1... | collective-permute-start | bytes 41480 | tf_op jit(solution)/shard_map/ppermute | solution.py:343
  6.7 0.6 copy-start.3
  17.7 3.9 %collective-permute-start.1 = (bf16[2112,128]{1,0:T(8,128)(2,1)}, bf16[2112,128]{1,0:T(8,128)(2,1)S(1)}, u32[]{:S(2)}, u32[]{:S(2)}) collective-permute-start(bf16[2112,128]{1,0:T(8,128)(2,1)} %get-tuple-element.17), channel_id=1, source_target_pairs={{0,1},{1,0},{2,3},{3,2},{4,5},{5,4},{6,7},{7,6},{8,9},{9,8},{10,11... | collective-permute-start | bytes 1622024 | tf_op jit(solution)/shard_map/ppermute | solution.py:339
  21.6 41.6 %copy-start = (bf16[2112,128]{1,0:T(8,128)(2,1)}, bf16[2112,128]{1,0:T(8,128)(2,1)S(1)}, u32[]{:S(2)}) copy-start(bf16[2112,128]{1,0:T(8,128)(2,1)S(1)} %collective-permute-done.1.own_ref) | copy-start | bytes 1622020
  23.6 5.1 %collective-permute-start.3 = (bf16[576,128]{1,0:T(8,128)(2,1)S(1)}, bf16[576,128]{1,0:T(8,128)(2,1)S(1)}, u32[]{:S(2)}, u32[]{:S(2)}) collective-permute-start(bf16[576,128]{1,0:T(8,128)(2,1)S(1)} %constant_dynamic-update-slice_fusion), channel_id=1, source_target_pairs={{0,2},{1,3},{2,0},{3,1},{4,6},{5,7},{6,4},{7,5},{8,10},{9,11},{10,... | collective-permute-start | bytes 442376 | tf_op jit(solution)/shard_map/ppermute | solution.py:339
  29.5 6.9 %collective-permute-start.5 = (bf16[576,128]{1,0:T(8,128)(2,1)S(1)}, bf16[576,128]{1,0:T(8,128)(2,1)S(1)}, u32[]{:S(2)}, u32[]{:S(2)}) collective-permute-start(bf16[576,128]{1,0:T(8,128)(2,1)S(1)} %constant_dynamic-update-slice_fusion.4), channel_id=1, source_target_pairs={{0,8},{1,9},{2,10},{3,11},{4,12},{5,13},{6,14},{7,15},{16,24},{17,... | collective-permute-start | bytes 442376 | tf_op jit(solution)/shard_map/ppermute | solution.py:343
  30.9 16.6 %collective-permute-start.4 = (bf16[576,128]{1,0:T(8,128)(2,1)S(1)}, bf16[576,128]{1,0:T(8,128)(2,1)S(1)}, u32[]{:S(2)}, u32[]{:S(2)}) collective-permute-start(bf16[576,128]{1,0:T(8,128)(2,1)S(1)} %constant_dynamic-update-slice_fusion.4), channel_id=1, source_target_pairs={{0,4},{1,5},{2,6},{3,7},{4,8},{5,9},{6,10},{7,11},{8,12},{9,13},{1... | collective-permute-start | bytes 442376 | tf_op jit(solution)/shard_map/ppermute | solution.py:343
  34.1 14.0 %collective-permute-start.6 = (bf16[576,128]{1,0:T(8,128)(2,1)S(1)}, bf16[576,128]{1,0:T(8,128)(2,1)S(1)}, u32[]{:S(2)}, u32[]{:S(2)}) collective-permute-start(bf16[576,128]{1,0:T(8,128)(2,1)S(1)} %constant_dynamic-update-slice_fusion.4), channel_id=1, source_target_pairs={{0,12},{1,13},{2,14},{3,15},{16,28},{17,29},{18,30},{19,31}} | collective-permute-start | bytes 442376 | tf_op jit(solution)/shard_map/ppermute | solution.py:343
  48.6 10.3 %collective-permute-start.7 = (bf16[2,512,128]{2,1,0:T(8,128)(2,1)S(1)}, bf16[2,512,128]{2,1,0:T(8,128)(2,1)S(1)}, u32[]{:S(2)}, u32[]{:S(2)}) collective-permute-start(bf16[2,512,128]{2,1,0:T(8,128)(2,1)S(1)} %pad_maximum_fusion.1), channel_id=1, source_target_pairs={{0,2},{1,3},{2,0},{3,1},{4,6},{5,7},{6,4},{7,5},{8,10},{9,11},{10,... | collective-permute-start | bytes 786440 | tf_op jit(solution)/shard_map/ppermute | solution.py:339
  49.0 9.8 %collective-permute-start.2 = (bf16[512,128]{1,0:T(8,128)(2,1)S(1)}, bf16[512,128]{1,0:T(8,128)(2,1)S(1)}, u32[]{:S(2)}, u32[]{:S(2)}) collective-permute-start(bf16[512,128]{1,0:T(8,128)(2,1)S(1)} %get-tuple-element.31), channel_id=1, source_target_pairs={{0,2},{1,3},{2,0},{3,1},{4,6},{5,7},{6,4},{7,5},{8,10},{9,11},{10,... | collective-permute-start | bytes 393224 | tf_op jit(solution)/shard_map/ppermute | solution.py:339
  59.1 9.8 %copy-start.1 = (bf16[3,1024,128]{2,1,0:T(8,128)(2,1)}, bf16[3,1024,128]{2,1,0:T(8,128)(2,1)S(1)}, u32[]{:S(2)}) copy-start(bf16[3,1024,128]{2,1,0:T(8,128)(2,1)S(1)} %pad_maximum_fusion.high_ref) | copy-start | bytes 2359300
  59.1 21.8 %collective-permute-start.8 = (bf16[3,1024,128]{2,1,0:T(8,128)(2,1)S(1)}, bf16[3,1024,128]{2,1,0:T(8,128)(2,1)S(1)}, u32[]{:S(2)}, u32[]{:S(2)}) collective-permute-start(bf16[3,1024,128]{2,1,0:T(8,128)(2,1)S(1)} %pad_maximum_fusion.high_ref), channel_id=1, source_target_pairs={{0,1},{1,0},{2,3},{3,2},{4,5},{5,4},{6,7},{7,6},{8,9},{9,8},{10,11... | collective-permute-start | bytes 2359304 | tf_op jit(solution)/shard_map/ppermute | solution.py:339
  80.9 0.9 %copy-start.2 = (bf16[3,1024,128]{2,1,0:T(8,128)(2,1)}, bf16[3,1024,128]{2,1,0:T(8,128)(2,1)S(1)}, u32[]{:S(2)}) copy-start(bf16[3,1024,128]{2,1,0:T(8,128)(2,1)S(1)} %collective-permute-done.8.high_ref) | copy-start | bytes 2359300

commit v2 on v1

--- a/solution.py
+++ b/solution.py
@@ -11,9 +11,8 @@
 EPSILON = 1e-05
 TILE = 128
 GROUP = 16
-NEAR_CALLS = 2
+NEAR_CALLS = (4, 12)
 STEP = 2
-NEVER = -1e30
 
 
 def log2(value):
@@ -27,6 +26,14 @@
 
 def shape_of(shape, dtype):
     return jax.ShapeDtypeStruct(shape, dtype)
+
+
+RESIDENT = pl.BlockSpec(memory_space=pltpu.VMEM)
+PARAMS = pltpu.CompilerParams(vmem_limit_bytes=24 << 20)
+
+
+def rows_of(head, width):
+    return pl.ds(pl.multiple_of(head * width, width), width)
 
 
 def tile_decays(log_decay):
@@ -139,7 +146,7 @@
             sides = []
             for start in (at, at + TILE):
                 done = conv_tile(buf.at[place], weight, start).astype(jnp.bfloat16).T
-                vt_ref[lanes, start : start + TILE] = done
+                vt_ref[rows_of(head, width), start : start + TILE] = done
                 sides.append(done)
             row = pair_row(scale, head, pair).astype(jnp.bfloat16)
             states[(0, pair)] = jnp.dot(
@@ -156,9 +163,8 @@
                     factor = factor * decay[later]
                 states[(bit + 1, first)] = keep + factor * states[(bit, first)]
         for order, key in enumerate(state_keys(pairs)):
-            st_ref[order, lanes, :] = states[key].astype(jnp.bfloat16)
-        at = pl.multiple_of(head * width, width)
-        g_ref[pl.ds(at, width), :] = states[(log2(pairs), 0)].astype(jnp.bfloat16)
+            st_ref[order, rows_of(head, width), :] = states[key].astype(jnp.bfloat16)
+        g_ref[rows_of(head, width), :] = states[(log2(pairs), 0)].astype(jnp.bfloat16)
 
 
 def table_rows(length):
@@ -228,10 +234,26 @@
         running = running + pair_total[-1]
 
 
-def near_kernel(first_head, vt_ref, st_ref, tab_ref, kc_ref, qt_ref, *refs):
-    near_ref, sc, mix, rest = refs[-4:]
+def rim_kernel(place_ref, q_ref, k_ref, v_ref, out_ref):
+    rows, state_dim = out_ref.shape[0], q_ref.shape[1]
+    last = slice(q_ref.shape[0] - rows, q_ref.shape[0])
+    out_ref[:, 0:state_dim] = q_ref[last, :]
+    out_ref[:, state_dim : 2 * state_dim] = k_ref[last, :]
+    out_ref[:, 2 * state_dim :] = v_ref[last, :]
+
+
+def score_kernel(qt_ref, kc_ref, sc_ref):
+    for pair in range(sc_ref.shape[0]):
+        at = 2 * pair * TILE
+        sc_ref[pair] = jnp.dot(
+            kc_ref[at : at + 2 * TILE, :],
+            qt_ref[:, at : at + 2 * TILE],
+            preferred_element_type=jnp.float32,
+        ).astype(jnp.bfloat16)
+
+
+def near_kernel(first_head, width, vt_ref, st_ref, tab_ref, sc, qt_ref, near_ref, mix, rest):
     length = vt_ref.shape[1]
-    width = vt_ref.shape[0] // STEP
     pairs = length // (2 * TILE)
     rows = table_rows(length)
     inner = log2(GROUP) + 1
@@ -244,18 +266,12 @@
     @pl.when(pl.program_id(0) == 0)
     def _():
         for pair in range(pairs):
-            at = 2 * pair * TILE
-            sc[pair] = jnp.dot(
-                kc_ref[at : at + 2 * TILE, :],
-                qt_ref[:, at : at + 2 * TILE],
-                preferred_element_type=jnp.float32,
-            ).astype(jnp.bfloat16)
             for place in range(STEP):
                 mix[place, pair, TILE:, 0:TILE] = jnp.zeros((TILE, TILE), jnp.bfloat16)
 
     def one_head(place):
         head = first_head + pl.program_id(0) * STEP + place
-        own = slice(place * width, (place + 1) * width)
+        own = rows_of(head, width)
 
         def table(order, tile):
             return tab_ref[order, tile, pl.ds(head, 1), :]
@@ -303,30 +319,51 @@
         one_head(place)
 
 
-def far_kernel(place_ref, near_ref, own_ref, high_ref, far_ref, qt_ref, off_ref, gain_ref, *refs):
-    out_ref, rest = refs[-2:]
-    bits = far_ref.shape[0]
+def add_far(levels, head, width, near_ref, buckets, far_ref, qt_ref, off_ref, rest, finish):
     length = qt_ref.shape[1]
-    width = near_ref.shape[0] // STEP
+    held = jnp.concatenate(buckets, axis=1)
+    factors = []
+    for level in levels:
+        factor = off_ref[level, pl.ds(head, 1), :]
+        factors.append(jnp.concatenate([factor, factor], axis=1))
+    for pair in range(length // (2 * TILE)):
+        at = 2 * pair * TILE
+        for order, level in enumerate(levels):
+            row = (pair_row(far_ref.at[level], head, pair) * factors[order]).astype(jnp.bfloat16)
+            rest[pair, order * TILE : (order + 1) * TILE, :] = qt_ref[:, at : at + 2 * TILE] * row
+        summed = near_ref[rows_of(head, width), at : at + 2 * TILE].astype(jnp.float32) + jnp.dot(
+            held, rest[pair], preferred_element_type=jnp.float32
+        )
+        finish(at, summed)
+
+
+def mid_kernel(
+    width, place_ref, near_ref, chip_ref, low_ref, low_other_ref, far_ref, qt_ref, off_ref, out_ref, rest
+):
+    step, steps = pl.program_id(0), pl.num_programs(0)
     for place in range(STEP):
         own = slice(place * width, (place + 1) * width)
-        head = (place_ref[0] + pl.program_id(0)) * STEP + place
-        held = jnp.concatenate(
-            [own_ref[own, :]] + [high_ref[bit, own, :] for bit in range(bits - 1)], axis=1
+        head = lax.rem(place_ref[0] * (steps // 2) + step, steps) * STEP + place
+        low = jnp.where(step < steps // 2, low_ref[own, :], low_other_ref[own, :])
+
+        def finish(at, summed, head=head):
+            out_ref[rows_of(head, width), at : at + 2 * TILE] = summed.astype(jnp.bfloat16)
+
+        add_far(
+            (0, 1), head, width, near_ref, [chip_ref[own, :], low], far_ref, qt_ref, off_ref, rest.at[place], finish
         )
+
+
+def far_kernel(width, other, place_ref, near_ref, high_ref, far_ref, qt_ref, off_ref, gain_ref, *refs):
+    out_ref, rest = refs[-2:]
+    count = high_ref.shape[0]
+    for place in range(STEP):
+        own = slice(place * width, (place + 1) * width)
+        core = 1 - place_ref[0] if other else place_ref[0]
+        head = (core * pl.num_programs(0) + pl.program_id(0)) * STEP + place
         gain = jnp.broadcast_to(gain_ref[:, own], (TILE, TILE)).T
-        factors = []
-        for bit in range(bits):
-            factor = jnp.exp(off_ref[bit, pl.ds(head, 1), :])
-            factors.append(jnp.concatenate([factor, factor], axis=1))
-        for pair in range(length // (2 * TILE)):
-            at = 2 * pair * TILE
-            for bit in range(bits):
-                row = (pair_row(far_ref.at[bit], head, pair) * factors[bit]).astype(jnp.bfloat16)
-                rest[place, pair, bit * TILE : (bit + 1) * TILE, :] = qt_ref[:, at : at + 2 * TILE] * row
-            summed = near_ref[own, at : at + 2 * TILE].astype(jnp.float32) + jnp.dot(
-                held, rest[place, pair], preferred_element_type=jnp.float32
-            )
+
+        def finish(at, summed, own=own, gain=gain):
             mean = jnp.mean(summed * summed, axis=0, keepdims=True)
             normed = summed * lax.rsqrt(mean + EPSILON)
             for side in range(2):
@@ -334,6 +371,126 @@
                 start = at + side * TILE
                 out_ref[start : start + TILE, own] = part.astype(jnp.bfloat16).T
 
+        add_far(
+            tuple(range(2, 2 + count)),
+            head,
+            width,
+            near_ref,
+            [high_ref[level, own, :] for level in range(count)],
+            far_ref,
+            qt_ref,
+            off_ref,
+            rest.at[place],
+            finish,
+        )
+
+
+def core_kernel(width, place_ref, own_ref, other_ref, theirs_ref, mine_ref, keep_ref, factor):
+    heads = keep_ref.shape[1]
+    states = heads * width
+    quarter = heads // 4
+    core, side = place_ref[0], place_ref[1]
+    upper = core == 1
+    own_total = sum_terms(own_ref[states:, :])
+    other_total = sum_terms(other_ref[states:, :])
+    factor[...] = jnp.exp(jnp.where(upper, own_total, other_total))
+    keep_ref[0] = own_total + other_total
+    keep_ref[1] = jnp.where(upper, other_total, 0.0)
+    for out_ref, column in ((theirs_ref, 1 - side), (mine_ref, side)):
+        for order in range(quarter):
+            head = (core * 2 + column) * quarter + order
+            own = own_ref[rows_of(head, width), :].astype(jnp.float32)
+            other = other_ref[rows_of(head, width), :].astype(jnp.float32)
+            scale = factor[pl.ds(head, 1), :]
+            last, first = jnp.where(upper, own, other), jnp.where(upper, other, own)
+            out_ref[order * width : (order + 1) * width, :] = (last + scale * first).astype(jnp.bfloat16)
+    theirs_ref[quarter * width :, :] = three_terms(own_total + other_total)
+
+
+def side_kernel(width, place_ref, got_ref, mine_ref, chip_ref, message_ref, keep_ref, factor):
+    heads = keep_ref.shape[1]
+    quarter = heads // 4
+    core, side = place_ref[0], place_ref[1]
+    upper = side == 1
+    chip_total = chip_ref[0]
+    got_total = sum_terms(got_ref[quarter * width :, :])
+    factor[...] = jnp.exp(jnp.where(upper, chip_total, got_total))
+    keep_ref[0] = chip_ref[1]
+    keep_ref[1] = chip_ref[1] + jnp.where(upper, got_total, 0.0)
+    for order in range(quarter):
+        rows = slice(order * width, (order + 1) * width)
+        mine, got = mine_ref[rows, :].astype(jnp.float32), got_ref[rows, :].astype(jnp.float32)
+        scale = factor[pl.ds((core * 2 + side) * quarter + order, 1), :]
+        last, first = jnp.where(upper, mine, got), jnp.where(upper, got, mine)
+        message_ref[rows, :] = (last + scale * first).astype(jnp.bfloat16)
+    message_ref[quarter * width :, :] = three_terms(chip_total + got_total)
+
+
+def plane_kernel(width, place_ref, *refs):
+    far_ref, part_ref, factor = refs[-3:]
+    came, keep_ref = refs[:-4], refs[-4]
+    heads = keep_ref.shape[1]
+    quarter = heads // 4
+    core, side, plane = place_ref[0], place_ref[1], place_ref[2]
+    planes = len(came) + 1
+    totals = [sum_terms(ref[quarter * width :, :]) for ref in came]
+    zero = jnp.zeros_like(totals[0])
+    far_ref[0] = jnp.where(core == 1, jnp.ones_like(zero), 0.0)
+    far_ref[1] = jnp.where(side == 1, jnp.exp(keep_ref[0]), 0.0)
+    in_plane = jnp.exp(keep_ref[1])
+    for bit in range(log2(planes)):
+        upper = (plane >> bit) & 1 == 1
+        far_ref[2 + bit] = jnp.where(upper, in_plane, 0.0)
+        for by in range(1, planes):
+            source = plane ^ by
+            here = upper & (source >> (bit + 1) == plane >> (bit + 1)) & ((source >> bit) & 1 == 0)
+            between = zero
+            for mid in range(1, planes):
+                inside = (plane ^ mid > source) & (plane ^ mid < plane)
+                between = between + jnp.where(inside, totals[mid - 1], 0.0)
+            factor[by - 1] = jnp.where(here, jnp.exp(between), 0.0)
+        for order in range(quarter):
+            rows = slice(order * width, (order + 1) * width)
+            head = (core * 2 + side) * quarter + order
+            summed = None
+            for by in range(1, planes):
+                term = factor[by - 1, pl.ds(head, 1), :] * came[by - 1][rows, :].astype(jnp.float32)
+                summed = term if summed is None else summed + term
+            part_ref[bit, rows, :] = summed.astype(jnp.bfloat16)
+
+
+def stack_kernel(first_ref, last_ref, out_ref):
+    half = first_ref.shape[0]
+    out_ref[0:half, :] = first_ref[...]
+    out_ref[half:, :] = last_ref[0:half, :]
+
+
+def column_kernel(place_ref, part_ref, swapped_ref, out_ref):
+    side = place_ref[1]
+    count, quarter, _ = part_ref.shape
+    for level in range(count):
+        out_ref[level, rows_of(side, quarter), :] = part_ref[level]
+        out_ref[level, rows_of(1 - side, quarter), :] = swapped_ref[level]
+
+
+def glue(kernel, out_shape, scratch=()):
+    scalar = pl.BlockSpec(memory_space=pltpu.SMEM)
+
+    def call(*args, place=None):
+        first = [] if place is None else [place]
+        many = isinstance(out_shape, list)
+        return pl.pallas_call(
+            kernel,
+            in_specs=[scalar for _ in first] + [RESIDENT for _ in args],
+            out_specs=[RESIDENT for _ in out_shape] if many else RESIDENT,
+            out_shape=out_shape,
+            scratch_shapes=list(scratch),
+            compiler_params=PARAMS,
+            cost_estimate=pl.CostEstimate(flops=10**7, bytes_accessed=10**6, transcendentals=0),
+        )(*first, *args)
+
+    return call
+
 
 def send(x, by, size):
     return lax.ppermute(x, "seq", [(i, i ^ by) for i in range(size)])
@@ -341,14 +498,6 @@
 
 def shift(x, by, size):
     return lax.ppermute(x, "seq", [(i, i + by) for i in range(size - by)])
-
-
-def at_rows(x, first, count):
-    return lax.dynamic_slice_in_dim(x, first, count, 0)
-
-
-def grow(decay, first, count, width):
-    return jnp.repeat(jnp.exp(at_rows(decay, first, count)), width)[:, None]
 
 
 def on_device(
@@ -365,29 +514,37 @@
     pairs = length // (2 * TILE)
     keys = state_keys(pairs)
     half, quarter = values_dim // 2, values_dim // 4
-    half_heads, quarter_heads = heads // 2, heads // 4
+    half_heads = heads // 2
     tail = 4 * heads
     index = lax.axis_index("seq")
-    core, side, plane = index & 1, index >> 1 & 1, index >> 2
+    core = index & 1
+    place = jnp.stack([core, index >> 1 & 1, index >> 2]).astype(jnp.int32)
+    half_steps = half_heads // STEP
+    gain = norm_gain.reshape(1, values_dim)
     planes = size // 4
     rows = table_rows(length)
-    calls = NEAR_CALLS if heads % NEAR_CALLS == 0 else 1
-    each = heads // calls
-    zero = jnp.zeros((heads,), jnp.float32)
-    upper_core, upper_side = core == 1, side == 1
-
-    own_rim = jnp.concatenate(
-        [query_inputs[length - rim :], key_inputs[length - rim :], value_inputs[length - rim :]],
-        axis=1,
-    )
+    calls = NEAR_CALLS if sum(NEAR_CALLS) == heads else (heads,)
+
+    last = length // GROUP - 1
+    own_rim = pl.pallas_call(
+        rim_kernel,
+        grid=(1,),
+        in_specs=[pl.BlockSpec(memory_space=pltpu.SMEM)]
+        + [pl.BlockSpec((GROUP, x.shape[1]), lambda i: (last, 0)) for x in (query_inputs, key_inputs, value_inputs)],
+        out_specs=pl.BlockSpec((rim, 2 * state_dim + values_dim), lambda i: (0, 0)),
+        out_shape=shape_of((rim, 2 * state_dim + values_dim), jnp.bfloat16),
+        name="rim",
+    )(place, query_inputs, key_inputs, value_inputs)
     rims = shift(own_rim, 1, size)
 
     tab, far_tab = pl.pallas_call(
         table_kernel,
+        out_specs=[RESIDENT] * 2,
         out_shape=[
-            shape_of((rows["size"], length // TILE, heads, TILE), jnp.float32),
-            shape_of((bits, length // TILE, heads, TILE), jnp.float32),
+            pltpu.VMEM((rows["size"], length // TILE, heads, TILE), jnp.float32),
+            pltpu.VMEM((bits, length // TILE, heads, TILE), jnp.float32),
         ],
+        compiler_params=PARAMS,
         cost_estimate=pl.CostEstimate(flops=10**9, bytes_accessed=3 * 10**6, transcendentals=0),
         name="tables",
     )(log_decay, level_weight)
@@ -407,25 +564,20 @@
             pl.BlockSpec((taps, STEP * width), lambda i: (0, 2 * state_dim // (STEP * width) + i)),
             whole(log_decay),
         ],
-        out_specs=[
-            pl.BlockSpec((STEP * width, length), lambda i: (i, 0)),
-            pl.BlockSpec((len(keys), STEP * width, state_dim), lambda i: (0, i, 0)),
-            pl.BlockSpec((values_dim + tail, state_dim), lambda i: (0, 0)),
-            pl.BlockSpec((state_dim, length), lambda i: (0, 0)),
-            pl.BlockSpec((length, state_dim), lambda i: (0, 0)),
-        ],
+        out_specs=[RESIDENT] * 5,
         out_shape=[
-            shape_of((values_dim, length), jnp.bfloat16),
-            shape_of((len(keys), values_dim, state_dim), jnp.bfloat16),
-            shape_of((values_dim + tail, state_dim), jnp.bfloat16),
-            shape_of((state_dim, length), jnp.bfloat16),
-            shape_of((length, state_dim), jnp.bfloat16),
+            pltpu.VMEM((values_dim, length), jnp.bfloat16),
+            pltpu.VMEM((len(keys), values_dim, state_dim), jnp.bfloat16),
+            pltpu.VMEM((values_dim + tail, state_dim), jnp.bfloat16),
+            pltpu.VMEM((state_dim, length), jnp.bfloat16),
+            pltpu.VMEM((length, state_dim), jnp.bfloat16),
         ],
         scratch_shapes=[
             pltpu.VMEM((STEP, length + 8, TILE), jnp.float32),
             pltpu.VMEM((length // TILE, heads, TILE), jnp.float32),
             pltpu.VMEM((pairs, heads, TILE), jnp.float32),
         ],
+        compiler_params=pltpu.CompilerParams(vmem_limit_bytes=52 << 20),
         cost_estimate=pl.CostEstimate(flops=10**9, bytes_accessed=9 * 10**6, transcendentals=0),
         name="state",
     )(
@@ -433,133 +585,124 @@
         conv_weight, conv_weight, conv_weight, log_decay,
     )
 
-    near = None
-    for call in range(calls):
-        first = call * each // STEP
-        before = [] if near is None else [near]
+    sc = pl.pallas_call(
+        score_kernel,
+        in_specs=[RESIDENT] * 2,
+        out_specs=RESIDENT,
+        out_shape=pltpu.VMEM((pairs, 2 * TILE, 2 * TILE), jnp.bfloat16),
+        compiler_params=PARAMS,
+        cost_estimate=pl.CostEstimate(flops=10**8, bytes_accessed=10**6, transcendentals=0),
+        name="scores",
+    )(qt, kc)
+
+    near = vt
+    for call, each in enumerate(calls):
         near = pl.pallas_call(
-            functools.partial(near_kernel, call * each),
+            functools.partial(near_kernel, sum(calls[:call]), width),
             grid=(each // STEP,),
-            in_specs=[
-                pl.BlockSpec((STEP * width, length), lambda i, first=first: (first + i, 0)),
-                pl.BlockSpec(
-                    (len(keys), STEP * width, state_dim), lambda i, first=first: (0, first + i, 0)
-                ),
-                whole(tab),
-                whole(kc),
-                whole(qt),
-            ]
-            + [pl.BlockSpec(memory_space=pl.ANY) for _ in before],
-            out_specs=pl.BlockSpec((STEP * width, length), lambda i, first=first: (first + i, 0)),
-            out_shape=shape_of((values_dim, length), jnp.bfloat16),
+            in_specs=[RESIDENT] * 5,
+            out_specs=RESIDENT,
+            out_shape=pltpu.VMEM((values_dim, length), jnp.bfloat16),
             scratch_shapes=[
-                pltpu.VMEM((pairs, 2 * TILE, 2 * TILE), jnp.bfloat16),
                 pltpu.VMEM((STEP, pairs, 2 * TILE, 2 * TILE), jnp.bfloat16),
                 pltpu.VMEM((STEP, pairs, log2(pairs) * state_dim, 2 * TILE), jnp.bfloat16),
             ],
-            input_output_aliases={5: 0} if before else {},
+            input_output_aliases={0: 0},
+            compiler_params=PARAMS,
             cost_estimate=pl.CostEstimate(flops=10**9, bytes_accessed=4 * 10**6, transcendentals=0),
             name="near",
-        )(vt, st, tab, kc, qt, *before)
+        )(near, st, tab, sc, qt)
 
     other = send(group, 1, size)
-    total = sum_terms(group[values_dim:])[:, 0]
-    other_total = sum_terms(other[values_dim:])[:, 0]
-    first_head = core * half_heads
-    own_half = at_rows(group, core * half, half).astype(jnp.float32)
-    other_half = at_rows(other, core * half, half).astype(jnp.float32)
-    chip = jnp.where(
-        upper_core,
-        own_half + grow(total, first_head, half_heads, width) * other_half,
-        other_half + grow(other_total, first_head, half_heads, width) * own_half,
-    ).astype(jnp.bfloat16)
-    chip_total = total + other_total
-    in_chip = jnp.where(upper_core, other_total, zero)
-    offsets = [jnp.where(upper_core, zero, NEVER), jnp.where(upper_side, in_chip, NEVER)]
-
-    def with_total(state, decay):
-        wide = jnp.broadcast_to(decay[:, None], (heads, state_dim))
-        return jnp.concatenate([state, three_terms(wide)], axis=0)
-
-    mine = at_rows(chip, side * quarter, quarter)
-    theirs = at_rows(chip, (1 - side) * quarter, quarter)
-    got = send(with_total(theirs, chip_total), 2, size)
+    table = pltpu.VMEM((heads, state_dim), jnp.float32)
+    message_shape = pltpu.VMEM((quarter + tail, state_dim), jnp.bfloat16)
+    theirs, mine, keep = glue(
+        functools.partial(core_kernel, width),
+        [message_shape, pltpu.VMEM((quarter, state_dim), jnp.bfloat16), pltpu.VMEM((2, heads, state_dim), jnp.float32)],
+        [table],
+    )(group, other, place=place)
+
+    got = send(theirs, 2, size)
     got_rest = send(mine, 2, size)
-    got_mine, got_total = got[:quarter], sum_terms(got[quarter:])[:, 0]
-    my_head = first_head + side * quarter_heads
-    mine_wide, got_wide = mine.astype(jnp.float32), got_mine.astype(jnp.float32)
-    flat = jnp.where(
-        upper_side,
-        mine_wide + grow(chip_total, my_head, quarter_heads, width) * got_wide,
-        got_wide + grow(got_total, my_head, quarter_heads, width) * mine_wide,
-    ).astype(jnp.bfloat16)
-    in_plane = in_chip + jnp.where(upper_side, got_total, zero)
-
-    message = with_total(flat, chip_total + got_total)
+    message, keep = glue(
+        functools.partial(side_kernel, width), [message_shape, pltpu.VMEM((2, heads, state_dim), jnp.float32)], [table]
+    )(got, mine, keep, place=place)
+
     came = []
     for by in range(1, planes):
-        came.append(shift(message, 4 * by, size))
-    parts = []
-    for bit in range(log2(planes)):
-        summed = jnp.zeros((quarter, state_dim), jnp.float32)
-        between = zero
-        upper = plane >> bit & 1 == 1
-        for by in range(1, planes):
-            source = plane - by
-            here = (
-                upper
-                & (source >= 0)
-                & (source >> (bit + 1) == plane >> (bit + 1))
-                & (source >> bit & 1 == 0)
-            )
-            factor = grow(jnp.where(here, between, NEVER), my_head, quarter_heads, width)
-            summed = summed + factor * came[by - 1][:quarter].astype(jnp.float32)
-            between = between + sum_terms(came[by - 1][quarter:])[:, 0]
-        parts.append(summed.astype(jnp.bfloat16))
-        offsets.append(jnp.where(upper, in_plane, NEVER))
-
-    halves = [jnp.concatenate([got_rest, got_mine], axis=0)[None]]
-    if parts:
-        part = jnp.stack(parts)
-        swapped = send(part, 2, size)
-        halves.append(
-            jnp.where(
-                upper_side,
-                jnp.concatenate([swapped, part], axis=1),
-                jnp.concatenate([part, swapped], axis=1),
-            )
-        )
-    high = jnp.concatenate(halves, axis=0)
+        came.append(send(message, 4 * by, size))
+
+    low = glue(stack_kernel, pltpu.VMEM((half, state_dim), jnp.bfloat16))(got_rest, got)
+    low_other = send(low, 1, size)
+
+    count = bits - 2
+    far_factor, part = glue(
+        functools.partial(plane_kernel, width),
+        [
+            pltpu.VMEM((bits, heads, state_dim), jnp.float32),
+            pltpu.VMEM((count, quarter, state_dim), jnp.bfloat16),
+        ],
+        [pltpu.VMEM((planes - 1, heads, state_dim), jnp.float32)],
+    )(*came, keep, place=place)
+
+    near = pl.pallas_call(
+        functools.partial(mid_kernel, width),
+        grid_spec=pltpu.PrefetchScalarGridSpec(
+            num_scalar_prefetch=1,
+            grid=(2 * half_steps,),
+            in_specs=[
+                RESIDENT,
+                pl.BlockSpec((STEP * width, state_dim), lambda i, s: (lax.rem(s[0] * half_steps + i, 2 * half_steps), 0)),
+                pl.BlockSpec((STEP * width, state_dim), lambda i, s: (jnp.minimum(i, half_steps - 1), 0)),
+                pl.BlockSpec((STEP * width, state_dim), lambda i, s: (jnp.maximum(i - half_steps, 0), 0)),
+                RESIDENT,
+                RESIDENT,
+                RESIDENT,
+            ],
+            out_specs=RESIDENT,
+            scratch_shapes=[pltpu.VMEM((STEP, pairs, 2 * state_dim, 2 * TILE), jnp.bfloat16)],
+        ),
+        out_shape=pltpu.VMEM((values_dim, length), jnp.bfloat16),
+        input_output_aliases={1: 0},
+        compiler_params=PARAMS,
+        cost_estimate=pl.CostEstimate(flops=10**9, bytes_accessed=6 * 10**6, transcendentals=0),
+        name="mid",
+    )(place, near, other, low, low_other, far_tab, qt, far_factor)
+
+    swapped = send(part, 2, size)
+    high = glue(column_kernel, pltpu.VMEM((count, half, state_dim), jnp.bfloat16))(part, swapped, place=place)
     high_other = send(high, 1, size)
 
-    off = jnp.broadcast_to(jnp.stack(offsets)[:, :, None], (bits, heads, TILE))
-    gain = norm_gain.reshape(1, values_dim)
     out = None
-    for first, states in ((core, high), (1 - core, high_other)):
+    for call, states in enumerate((high, high_other)):
         before = [] if out is None else [out]
+
+        def columns(i, s, other=call):
+            return (0, (1 - s[0] if other else s[0]) * half_steps + i)
+
         out = pl.pallas_call(
-            far_kernel,
+            functools.partial(far_kernel, width, call),
             grid_spec=pltpu.PrefetchScalarGridSpec(
                 num_scalar_prefetch=1,
-                grid=(half_heads // STEP,),
+                grid=(half_steps,),
                 in_specs=[
-                    pl.BlockSpec((STEP * width, length), lambda i, s: (s[0] + i, 0)),
-                    pl.BlockSpec((STEP * width, state_dim), lambda i, s: (s[0] + i, 0)),
-                    pl.BlockSpec((bits - 1, STEP * width, state_dim), lambda i, s: (0, i, 0)),
-                    pl.BlockSpec(far_tab.shape, lambda i, s: (0, 0, 0, 0)),
-                    pl.BlockSpec(qt.shape, lambda i, s: (0, 0)),
-                    pl.BlockSpec(off.shape, lambda i, s: (0, 0, 0)),
-                    pl.BlockSpec((1, STEP * width), lambda i, s: (0, s[0] + i)),
+                    RESIDENT,
+                    pl.BlockSpec((count, STEP * width, state_dim), lambda i, s: (0, i, 0)),
+                    RESIDENT,
+                    RESIDENT,
+                    RESIDENT,
+                    pl.BlockSpec((1, STEP * width), columns),
                 ]
                 + [pl.BlockSpec(memory_space=pl.ANY) for _ in before],
-                out_specs=pl.BlockSpec((length, STEP * width), lambda i, s: (0, s[0] + i)),
-                scratch_shapes=[pltpu.VMEM((STEP, pairs, bits * state_dim, 2 * TILE), jnp.bfloat16)],
+                out_specs=pl.BlockSpec((length, STEP * width), columns),
+                scratch_shapes=[pltpu.VMEM((STEP, pairs, count * state_dim, 2 * TILE), jnp.bfloat16)],
             ),
             out_shape=shape_of((length, values_dim), jnp.bfloat16),
-            input_output_aliases={8: 0} if before else {},
+            input_output_aliases={7: 0} if before else {},
+            compiler_params=PARAMS,
             cost_estimate=pl.CostEstimate(flops=10**9, bytes_accessed=6 * 10**6, transcendentals=0),
             name="far",
-        )((first * half_heads // STEP)[None], near, other, states, far_tab, qt, off, gain, *before)
+        )(place, near, states, far_tab, qt, far_factor, gain, *before)
     return out
 
 

time: 88.2 us -> 78.2 us (0.89)
  the two profiles are of different devices: /device:TPU:17 before, /device:TPU:0 now
where the time goes in v2:
time: 78.2 us; the launch traced here: 77.9 us
  Pallas kernels  35.5 us (45%)
  waiting for transfers between devices  25.5 us (33%)
  starting transfers between devices  15.5 us (20%)
    ppermute x9, waiting for transfers between devices, send(): return lax.ppermute(x, 'seq', [(i, i ^ by) for i in range(size)])  24.5 us
    ppermute x9, starting transfers between devices, send(): return lax.ppermute(x, 'seq', [(i, i ^ by) for i in range(size)])  13 us
    pallas_call x2, Pallas kernels, on_device(): pl.pallas_call(functools.partial(near_kernel, sum(calls[:call]), width),...  10.6 us
    pallas_call x1, Pallas kernels, on_device(): pl.pallas_call(state_kernel, grid=(heads // STEP,), in_specs=[whole(query...  8.95 us
    pallas_call x2, Pallas kernels, on_device(): pl.pallas_call(functools.partial(far_kernel, width, call), grid_spec=pltp...  7.6 us
    pallas_call x1, Pallas kernels, on_device(): pl.pallas_call(functools.partial(mid_kernel, width), grid_spec=pltpu.Pref...  3.44 us
    pallas_call x5, Pallas kernels, call(): pl.pallas_call(kernel, in_specs=[scalar for _ in first] + [RESIDENT for _...  2.61 us
    ppermute x1, starting transfers between devices, shift(): return lax.ppermute(x, 'seq', [(i, i + by) for i in range(size - by)])  2.52 us
  transfers between devices with their start and end apart: 10, of which 7 were waited for; matrix products, arithmetic and copies ran while one was open for 0% of the time, Pallas kernels for 25%

profile of v2, /device:TPU:0, one launch (start us, length us, event | category | flops | bytes accessed | tf_op | source)
XLA Modules:
  0.0 77.9 jit_solution(13649146234284889912)
XLA Ops:
  0.0 0.6 pad_add_fusion.place_ref
  0.6 1.5 %rim.1 = bf16[3,2304]{1,0:T(4,128)(2,1)} custom-call(s32[3]{0:T(128)} %pad_add_fusion.place_ref, bf16[1024,128]{1,0:T(8,128)(2,1)} %q_ref.3, bf16[1024,128]{1,0:T(8,128)(2,1)} %k_ref.3, bf16[1024,2048]{1,0:T(8,128)(2,1)} %v_ref.3), custom_call_target="tpu_custom_call" | custom-call | tf_op jit(solution)/shard_map/rim/pallas_call | solution.py:529
  2.1 2.5 %collective-permute-start = (bf16[3,2304]{1,0:T(4,128)(2,1)}, bf16[3,2304]{1,0:T(4,128)(2,1)S(1)}, u32[]{:S(2)}, u32[]{:S(2)}) collective-permute-start(bf16[3,2304]{1,0:T(4,128)(2,1)} %rim.1), channel_id=1, source_target_pairs={{0,1},{1,2},{2,3},{3,4},{4,5},{5,6},{6,7},{7,8},{8,9},{9,10},{10,1... | collective-permute-start | bytes 41480 | tf_op jit(solution)/shard_map/ppermute | solution.py:500
  4.6 1.0 %collective-permute-done.rq_ref.rk_ref.rv_ref = bf16[3,2304]{1,0:T(4,128)(2,1)S(1)} collective-permute-done((bf16[3,2304]{1,0:T(4,128)(2,1)}, bf16[3,2304]{1,0:T(4,128)(2,1)S(1)}, u32[]{:S(2)}, u32[]{:S(2)}) %collective-permute-start) | collective-permute-done | bytes 13856 | tf_op jit(solution)/shard_map/ppermute | solution.py:500
  5.7 0.6 copy-done.4
  6.3 8.9 %state.1 = (bf16[2048,1024]{1,0:T(8,128)(2,1)S(1)}, bf16[3,2048,128]{2,1,0:T(8,128)(2,1)S(1)}, bf16[2112,128]{1,0:T(8,128)(2,1)S(1)}, bf16[128,1024]{1,0:T(8,128)(2,1)S(1)}, bf16[1024,128]{1,0:T(8,128)(2,1)S(1)}) custom-call(bf16[1024,128]{1,0:T(8,128)(2,1)} %q_ref.3, bf16[1024,128]{1,0:T(8,128)(2,1)} %k_ref.3, bf16[1024,2048]{1,0:T(8,128)(2,1)} %v_ref.3, ...), custom_call_target="tpu_custom_call" | custom-call | flops 1000000000 | bytes 9000000 | tf_op jit(solution)/shard_map/state/pallas_call | solution.py:552
  15.2 2.7 %collective-permute-start.1 = (bf16[2112,128]{1,0:T(8,128)(2,1)S(1)}, bf16[2112,128]{1,0:T(8,128)(2,1)S(1)}, u32[]{:S(2)}, u32[]{:S(2)}) collective-permute-start(bf16[2112,128]{1,0:T(8,128)(2,1)S(1)} %get-tuple-element.24.own_ref), channel_id=1, source_target_pairs={{0,1},{1,0},{2,3},{3,2},{4,5},{5,4},{6,7},{7,6},{8,9},{9,8},{10,11... | collective-permute-start | bytes 1622024 | tf_op jit(solution)/shard_map/ppermute | solution.py:496
  18.0 1.6 %collective-permute-done.1.other_ref.chip_ref = bf16[2112,128]{1,0:T(8,128)(2,1)S(1)} collective-permute-done((bf16[2112,128]{1,0:T(8,128)(2,1)S(1)}, bf16[2112,128]{1,0:T(8,128)(2,1)S(1)}, u32[]{:S(2)}, u32[]{:S(2)}) %collective-permute-start.1) | collective-permute-done | bytes 540704 | tf_op jit(solution)/shard_map/ppermute | solution.py:496
  19.5 0.7 shard_map.73
  20.2 2.6 %collective-permute-start.3 = (bf16[576,128]{1,0:T(8,128)(2,1)S(1)}, bf16[576,128]{1,0:T(8,128)(2,1)S(1)}, u32[]{:S(2)}, u32[]{:S(2)}) collective-permute-start(bf16[576,128]{1,0:T(8,128)(2,1)S(1)} %get-tuple-element.26), channel_id=1, source_target_pairs={{0,2},{1,3},{2,0},{3,1},{4,6},{5,7},{6,4},{7,5},{8,10},{9,11},{10,... | collective-permute-start | bytes 442376 | tf_op jit(solution)/shard_map/ppermute | solution.py:496
  22.8 4.1 %collective-permute-done.3.last_ref.got_ref = bf16[576,128]{1,0:T(8,128)(2,1)S(1)} collective-permute-done((bf16[576,128]{1,0:T(8,128)(2,1)S(1)}, bf16[576,128]{1,0:T(8,128)(2,1)S(1)}, u32[]{:S(2)}, u32[]{:S(2)}) %collective-permute-start.3) | collective-permute-done | bytes 147488 | tf_op jit(solution)/shard_map/ppermute | solution.py:496
  27.0 0.6 shard_map.75
  27.6 4.8 %collective-permute-start.7 = (bf16[576,128]{1,0:T(8,128)(2,1)S(1)}, bf16[576,128]{1,0:T(8,128)(2,1)S(1)}, u32[]{:S(2)}, u32[]{:S(2)}) collective-permute-start(bf16[576,128]{1,0:T(8,128)(2,1)S(1)} %get-tuple-element.29), channel_id=1, source_target_pairs={{0,12},{1,13},{2,14},{3,15},{4,8},{5,9},{6,10},{7,11},{8,4},{9,5},... | collective-permute-start | bytes 442376 | tf_op jit(solution)/shard_map/ppermute | solution.py:496
  32.4 0.6 collective-permute-start.5
  33.0 4.1 %collective-permute-done.7.refs_2_ = bf16[576,128]{1,0:T(8,128)(2,1)S(1)} collective-permute-done((bf16[576,128]{1,0:T(8,128)(2,1)S(1)}, bf16[576,128]{1,0:T(8,128)(2,1)S(1)}, u32[]{:S(2)}, u32[]{:S(2)}) %collective-permute-start.7) | collective-permute-done | bytes 147488 | tf_op jit(solution)/shard_map/ppermute | solution.py:496
  37.1 7.2 %collective-permute-done.6.refs_1_ = bf16[576,128]{1,0:T(8,128)(2,1)S(1)} collective-permute-done((bf16[576,128]{1,0:T(8,128)(2,1)S(1)}, bf16[576,128]{1,0:T(8,128)(2,1)S(1)}, u32[]{:S(2)}, u32[]{:S(2)}) %collective-permute-start.6) | collective-permute-done | bytes 147488 | tf_op jit(solution)/shard_map/ppermute | solution.py:496
  44.3 0.7 shard_map.76
  45.0 0.7 collective-permute-start.8
  45.7 1.4 %collective-permute-start.2 = (bf16[512,128]{1,0:T(8,128)(2,1)S(1)}, bf16[512,128]{1,0:T(8,128)(2,1)S(1)}, u32[]{:S(2)}, u32[]{:S(2)}) collective-permute-start(bf16[512,128]{1,0:T(8,128)(2,1)S(1)} %get-tuple-element.25.mine_ref), channel_id=1, source_target_pairs={{0,2},{1,3},{2,0},{3,1},{4,6},{5,7},{6,4},{7,5},{8,10},{9,11},{10,... | collective-permute-start | bytes 393224 | tf_op jit(solution)/shard_map/ppermute | solution.py:496
  47.1 6.8 %collective-permute-done.8.swapped_ref = bf16[2,512,128]{2,1,0:T(8,128)(2,1)S(1)} collective-permute-done((bf16[2,512,128]{2,1,0:T(8,128)(2,1)S(1)}, bf16[2,512,128]{2,1,0:T(8,128)(2,1)S(1)}, u32[]{:S(2)}, u32[]{:S(2)}) %collective-permute-start.8) | collective-permute-done | bytes 262176 | tf_op jit(solution)/shard_map/ppermute | solution.py:496
  53.9 0.6 shard_map.77.high_ref
  54.5 0.1 collective-permute-start.9
  54.6 0.7 collective-permute-done.2.first_ref
  55.3 0.1 collective-permute-start.4
  55.4 0.4 tables.1
  55.9 0.3 scores.1.sc
  56.1 2.7 %near.2.vt_ref = bf16[2048,1024]{1,0:T(8,128)(2,1)S(1)} custom-call(bf16[2048,1024]{1,0:T(8,128)(2,1)S(1)} %get-tuple-element.19.vt_ref, bf16[3,2048,128]{2,1,0:T(8,128)(2,1)S(1)} %get-tuple-element.20.st_ref, f32[17,8,16,128]{3,2,1,0:T(8,128)S(1)} %get-tuple-element.21.tab_ref, bf16[4,256,256]{2,1,0:T(8,128)(2,1)S(1)} %scores.1.sc, ...), custom_call_target="tpu_custom_call", output_to_operand_aliasing={{}: (0, {})} | custom-call | flops 1000000000 | bytes 4000000 | tf_op jit(solution)/shard_map/near/pallas_call | solution.py:600
  58.8 8.0 %near.3.near_ref = bf16[2048,1024]{1,0:T(8,128)(2,1)S(1)} custom-call(bf16[2048,1024]{1,0:T(8,128)(2,1)S(1)} %near.2.vt_ref, bf16[3,2048,128]{2,1,0:T(8,128)(2,1)S(1)} %get-tuple-element.20.st_ref, f32[17,8,16,128]{3,2,1,0:T(8,128)S(1)} %get-tuple-element.21.tab_ref, bf16[4,256,256]{2,1,0:T(8,128)(2,1)S(1)} %scores.1.sc, ...), custom_call_target="tpu_custom_call", output_to_operand_aliasing={{}: (0, {})} | custom-call | flops 1000000000 | bytes 4000000 | tf_op jit(solution)/shard_map/near/pallas_call | solution.py:600
  66.8 0.0 copy-start.2
  66.8 3.4 %mid.1.near_ref = bf16[2048,1024]{1,0:T(8,128)(2,1)S(1)} custom-call(s32[3]{0:T(128)S(1)} %copy-done.1, bf16[2048,1024]{1,0:T(8,128)(2,1)S(1)} %near.3.near_ref, bf16[2112,128]{1,0:T(8,128)(2,1)S(1)} %collective-permute-done.1.other_ref.chip_ref, bf16[1024,128]{1,0:T(8,128)(2,1)S(1)} %shard_map.74.low_ref, ...), custom_call_target="tpu_custom_call", output_to_operand_aliasing={{}: (1, {})} | custom-call | flops 1000000000 | bytes 6000000 | tf_op jit(solution)/shard_map/mid/pallas_call | solution.py:648
  70.3 3.8 %far.2.refs_0_ = bf16[1024,2048]{1,0:T(8,128)(2,1)} custom-call(s32[3]{0:T(128)S(1)} %copy-done.1, bf16[2048,1024]{1,0:T(8,128)(2,1)S(1)} %mid.1.near_ref, bf16[2,1024,128]{2,1,0:T(8,128)(2,1)S(1)} %shard_map.77.high_ref, f32[4,8,16,128]{3,2,1,0:T(8,128)S(1)} %get-tuple-element.27.far_ref, bf16[128,1024]{1,0:T(8,128)(2,1)S(1)} %get-tuple-element.22.qt_ref, ...), custom_call_target="tpu_custom_call" | custom-call | flops 1000000000 | bytes 6000000 | tf_op jit(solution)/shard_map/far/pallas_call | solution.py:683
  74.1 3.8 %far.3 = bf16[1024,2048]{1,0:T(8,128)(2,1)} custom-call(s32[3]{0:T(128)S(1)} %copy-done.1, bf16[2048,1024]{1,0:T(8,128)(2,1)S(1)} %mid.1.near_ref, bf16[2,1024,128]{2,1,0:T(8,128)(2,1)S(1)} %collective-permute-done.9.high_ref, f32[4,8,16,128]{3,2,1,0:T(8,128)S(1)} %get-tuple-element.27.far_ref, ...), custom_call_target="tpu_custom_call", output_to_operand_aliasing={{}: (7, {})} | custom-call | flops 1000000000 | bytes 6000000 | tf_op jit(solution)/shard_map/far/pallas_call | solution.py:683
  (13 shorter events, 0.0 us)
Async XLA Ops:
  0.6 18.9 %copy-start.1 = (s32[3]{0:T(128)S(1)}, s32[3]{0:T(128)}, u32[]{:S(2)}) copy-start(s32[3]{0:T(128)} %pad_add_fusion.place_ref) | copy-start | bytes 40
  2.1 53.3 %copy-start = (f32[16,1024]{1,0:T(8,128)S(1)}, f32[16,1024]{1,0:T(8,128)}, u32[]{:S(2)}) copy-start(f32[16,1024]{1,0:T(8,128)} %ld_ref.3) | copy-start | bytes 196612
  2.1 53.3 %copy-start.3 = (bf16[15,16,1024]{2,1,0:T(8,128)(2,1)S(1)}, bf16[15,16,1024]{2,1,0:T(8,128)(2,1)}, u32[]{:S(2)}) copy-start(bf16[15,16,1024]{2,1,0:T(8,128)(2,1)} %lw_ref.1) | copy-start | bytes 1474564
  2.1 3.6 %collective-permute-start = (bf16[3,2304]{1,0:T(4,128)(2,1)}, bf16[3,2304]{1,0:T(4,128)(2,1)S(1)}, u32[]{:S(2)}, u32[]{:S(2)}) collective-permute-start(bf16[3,2304]{1,0:T(4,128)(2,1)} %rim.1), channel_id=1, source_target_pairs={{0,1},{1,2},{2,3},{3,4},{4,5},{5,6},{6,7},{7,8},{8,9},{9,10},{10,1... | collective-permute-start | bytes 41480 | tf_op jit(solution)/shard_map/ppermute | solution.py:500
  5.7 0.6 copy-start.4
  15.2 4.3 %collective-permute-start.1 = (bf16[2112,128]{1,0:T(8,128)(2,1)S(1)}, bf16[2112,128]{1,0:T(8,128)(2,1)S(1)}, u32[]{:S(2)}, u32[]{:S(2)}) collective-permute-start(bf16[2112,128]{1,0:T(8,128)(2,1)S(1)} %get-tuple-element.24.own_ref), channel_id=1, source_target_pairs={{0,1},{1,0},{2,3},{3,2},{4,5},{5,4},{6,7},{7,6},{8,9},{9,8},{10,11... | collective-permute-start | bytes 1622024 | tf_op jit(solution)/shard_map/ppermute | solution.py:496
  20.2 6.8 %collective-permute-start.3 = (bf16[576,128]{1,0:T(8,128)(2,1)S(1)}, bf16[576,128]{1,0:T(8,128)(2,1)S(1)}, u32[]{:S(2)}, u32[]{:S(2)}) collective-permute-start(bf16[576,128]{1,0:T(8,128)(2,1)S(1)} %get-tuple-element.26), channel_id=1, source_target_pairs={{0,2},{1,3},{2,0},{3,1},{4,6},{5,7},{6,4},{7,5},{8,10},{9,11},{10,... | collective-permute-start | bytes 442376 | tf_op jit(solution)/shard_map/ppermute | solution.py:496
  27.6 9.5 %collective-permute-start.7 = (bf16[576,128]{1,0:T(8,128)(2,1)S(1)}, bf16[576,128]{1,0:T(8,128)(2,1)S(1)}, u32[]{:S(2)}, u32[]{:S(2)}) collective-permute-start(bf16[576,128]{1,0:T(8,128)(2,1)S(1)} %get-tuple-element.29), channel_id=1, source_target_pairs={{0,12},{1,13},{2,14},{3,15},{4,8},{5,9},{6,10},{7,11},{8,4},{9,5},... | collective-permute-start | bytes 442376 | tf_op jit(solution)/shard_map/ppermute | solution.py:496
  32.4 11.9 %collective-permute-start.6 = (bf16[576,128]{1,0:T(8,128)(2,1)S(1)}, bf16[576,128]{1,0:T(8,128)(2,1)S(1)}, u32[]{:S(2)}, u32[]{:S(2)}) collective-permute-start(bf16[576,128]{1,0:T(8,128)(2,1)S(1)} %get-tuple-element.29), channel_id=1, source_target_pairs={{0,8},{1,9},{2,10},{3,11},{4,12},{5,13},{6,14},{7,15},{8,0},{9,1},... | collective-permute-start | bytes 442376 | tf_op jit(solution)/shard_map/ppermute | solution.py:496
  32.4 11.9 %collective-permute-start.5 = (bf16[576,128]{1,0:T(8,128)(2,1)S(1)}, bf16[576,128]{1,0:T(8,128)(2,1)S(1)}, u32[]{:S(2)}, u32[]{:S(2)}) collective-permute-start(bf16[576,128]{1,0:T(8,128)(2,1)S(1)} %get-tuple-element.29), channel_id=1, source_target_pairs={{0,4},{1,5},{2,6},{3,7},{4,0},{5,1},{6,2},{7,3},{8,12},{9,13},{10,... | collective-permute-start | bytes 442376 | tf_op jit(solution)/shard_map/ppermute | solution.py:496
  45.0 8.8 %collective-permute-start.8 = (bf16[2,512,128]{2,1,0:T(8,128)(2,1)S(1)}, bf16[2,512,128]{2,1,0:T(8,128)(2,1)S(1)}, u32[]{:S(2)}, u32[]{:S(2)}) collective-permute-start(bf16[2,512,128]{2,1,0:T(8,128)(2,1)S(1)} %get-tuple-element.32.part_ref), channel_id=1, source_target_pairs={{0,2},{1,3},{2,0},{3,1},{4,6},{5,7},{6,4},{7,5},{8,10},{9,11},{10,... | collective-permute-start | bytes 786440 | tf_op jit(solution)/shard_map/ppermute | solution.py:496
  45.7 9.6 %collective-permute-start.2 = (bf16[512,128]{1,0:T(8,128)(2,1)S(1)}, bf16[512,128]{1,0:T(8,128)(2,1)S(1)}, u32[]{:S(2)}, u32[]{:S(2)}) collective-permute-start(bf16[512,128]{1,0:T(8,128)(2,1)S(1)} %get-tuple-element.25.mine_ref), channel_id=1, source_target_pairs={{0,2},{1,3},{2,0},{3,1},{4,6},{5,7},{6,4},{7,5},{8,10},{9,11},{10,... | collective-permute-start | bytes 393224 | tf_op jit(solution)/shard_map/ppermute | solution.py:496
  54.5 19.6 %collective-permute-start.9 = (bf16[2,1024,128]{2,1,0:T(8,128)(2,1)S(1)}, bf16[2,1024,128]{2,1,0:T(8,128)(2,1)S(1)}, u32[]{:S(2)}, u32[]{:S(2)}) collective-permute-start(bf16[2,1024,128]{2,1,0:T(8,128)(2,1)S(1)} %shard_map.77.high_ref), channel_id=1, source_target_pairs={{0,1},{1,0},{2,3},{3,2},{4,5},{5,4},{6,7},{7,6},{8,9},{9,8},{10,11... | collective-permute-start | bytes 1572872 | tf_op jit(solution)/shard_map/ppermute | solution.py:496
  55.3 11.5 %collective-permute-start.4 = (bf16[1024,128]{1,0:T(8,128)(2,1)S(1)}, bf16[1024,128]{1,0:T(8,128)(2,1)S(1)}, u32[]{:S(2)}, u32[]{:S(2)}) collective-permute-start(bf16[1024,128]{1,0:T(8,128)(2,1)S(1)} %shard_map.74.low_ref), channel_id=1, source_target_pairs={{0,1},{1,0},{2,3},{3,2},{4,5},{5,4},{6,7},{7,6},{8,9},{9,8},{10,11... | collective-permute-start | bytes 786440 | tf_op jit(solution)/shard_map/ppermute | solution.py:496
  66.8 3.5 %copy-start.2 = (f32[2048]{0:T(1024)S(1)}, f32[2048]{0:T(1024)}, u32[]{:S(2)}) copy-start(f32[2048]{0:T(1024)} %param.13) | copy-start | bytes 24580

commit v3 on v2

--- a/solution.py
+++ b/solution.py
@@ -11,17 +11,12 @@
 EPSILON = 1e-05
 TILE = 128
 GROUP = 16
-NEAR_CALLS = (4, 12)
+NEAR_CALLS = (4, 6, 6)
 STEP = 2
 
 
 def log2(value):
     return value.bit_length() - 1
-
-
-def whole(array):
-    rank = array.ndim
-    return pl.BlockSpec(array.shape, lambda i: (0,) * rank)
 
 
 def shape_of(shape, dtype):
@@ -103,18 +98,26 @@
 
 
 def state_kernel(
-    q_ref, k_ref, v_ref, rq_ref, rk_ref, rv_ref, wq_ref, wk_ref, wv_ref, ld_ref,
-    vt_ref, st_ref, g_ref, qt_ref, kc_ref,
-    buf, scale, total,
+    k_ref, v_ref, rim_ref, wk_ref, wv_ref, ld_ref,
+    vt_ref, st_ref, g_ref, kc_ref,
+    buf, scale, total, values, sems,
 ):
     step = pl.program_id(0)
     heads = ld_ref.shape[0]
     length = v_ref.shape[0]
-    width = v_ref.shape[1] // STEP
+    width = v_ref.shape[1] // heads
+    state_dim = k_ref.shape[1]
     pairs = length // (2 * TILE)
+    steps = heads // STEP
+
+    def fetch(order):
+        lanes = slice(order * STEP * width, (order + 1) * STEP * width)
+        return pltpu.make_async_copy(v_ref.at[:, lanes], values.at[order], sems.at[order])
 
     @pl.when(step == 0)
     def _():
+        for order in range(steps):
+            fetch(order).start()
         local, _, totals = tile_decays(ld_ref[...])
         summed = None
         for pair in range(pairs):
@@ -125,17 +128,21 @@
             total[pair] = jnp.exp(both)
             summed = both if summed is None else summed + both
         g_ref[pl.ds(heads * width, 4 * heads), :] = three_terms(summed)
-        fill(buf.at[0], q_ref, rq_ref)
-        fill(buf.at[1], k_ref, rk_ref)
+        fill(buf.at[0], k_ref, rim_ref.at[:, state_dim : 2 * state_dim])
         for tile in range(length // TILE):
             at = tile * TILE
-            done = conv_tile(buf.at[0], 0.5 * wq_ref[...], at).astype(jnp.bfloat16)
-            qt_ref[:, at : at + TILE] = done.T
-            kc_ref[at : at + TILE, :] = conv_tile(buf.at[1], 0.5 * wk_ref[...], at).astype(jnp.bfloat16)
+            kc_ref[at : at + TILE, :] = conv_tile(buf.at[0], 0.5 * wk_ref[...], at).astype(jnp.bfloat16)
+
+    for order in range(steps):
+
+        @pl.when(step == order)
+        def _(order=order):
+            fetch(order).wait()
 
     for place in range(STEP):
         lanes = slice(place * width, (place + 1) * width)
-        fill(buf.at[place], v_ref.at[:, lanes], rv_ref.at[:, lanes])
+        rim_lanes = pl.ds(pl.multiple_of(2 * state_dim + (step * STEP + place) * width, width), width)
+        fill(buf.at[place], values.at[step, :, lanes], rim_ref.at[:, rim_lanes])
     for place in range(STEP):
         head = step * STEP + place
         lanes = slice(place * width, (place + 1) * width)
@@ -181,7 +188,11 @@
     }
 
 
-def table_kernel(ld_ref, lw_ref, tab_ref, far_ref):
+def table_kernel(ld_ref, lw_ref, tab_ref, far_ref, place_ref):
+    index = lax.axis_index("seq")
+    place_ref[0] = index & 1
+    place_ref[1] = index >> 1 & 1
+    place_ref[2] = index >> 2
     heads, length = ld_ref.shape
     levels = lw_ref.shape[0]
     pairs = length // (2 * TILE)
@@ -234,15 +245,31 @@
         running = running + pair_total[-1]
 
 
-def rim_kernel(place_ref, q_ref, k_ref, v_ref, out_ref):
+def rim_kernel(q_ref, k_ref, v_ref, out_ref, last, sems):
     rows, state_dim = out_ref.shape[0], q_ref.shape[1]
-    last = slice(q_ref.shape[0] - rows, q_ref.shape[0])
-    out_ref[:, 0:state_dim] = q_ref[last, :]
-    out_ref[:, state_dim : 2 * state_dim] = k_ref[last, :]
-    out_ref[:, 2 * state_dim :] = v_ref[last, :]
-
-
-def score_kernel(qt_ref, kc_ref, sc_ref):
+    tail = pl.ds(q_ref.shape[0] - GROUP, GROUP)
+    lanes = (
+        slice(0, state_dim),
+        slice(state_dim, 2 * state_dim),
+        slice(2 * state_dim, 2 * state_dim + v_ref.shape[1]),
+    )
+    copies = [
+        pltpu.make_async_copy(ref.at[tail, :], last.at[:, at], sems.at[order])
+        for order, (ref, at) in enumerate(zip((q_ref, k_ref, v_ref), lanes, strict=True))
+    ]
+    for copy in copies:
+        copy.start()
+    for copy in copies:
+        copy.wait()
+    out_ref[...] = last[GROUP - rows :, :]
+
+
+def score_kernel(q_ref, rim_ref, w_ref, kc_ref, qt_ref, sc_ref, buf):
+    length, state_dim = q_ref.shape
+    fill(buf, q_ref, rim_ref.at[:, 0:state_dim])
+    weight = 0.5 * w_ref[:, 0:state_dim]
+    for at in range(0, length, TILE):
+        qt_ref[:, at : at + TILE] = conv_tile(buf, weight, at).astype(jnp.bfloat16).T
     for pair in range(sc_ref.shape[0]):
         at = 2 * pair * TILE
         sc_ref[pair] = jnp.dot(
@@ -441,6 +468,8 @@
     for bit in range(log2(planes)):
         upper = (plane >> bit) & 1 == 1
         far_ref[2 + bit] = jnp.where(upper, in_plane, 0.0)
+        if bit == 0:
+            continue
         for by in range(1, planes):
             source = plane ^ by
             here = upper & (source >> (bit + 1) == plane >> (bit + 1)) & ((source >> bit) & 1 == 0)
@@ -456,7 +485,7 @@
             for by in range(1, planes):
                 term = factor[by - 1, pl.ds(head, 1), :] * came[by - 1][rows, :].astype(jnp.float32)
                 summed = term if summed is None else summed + term
-            part_ref[bit, rows, :] = summed.astype(jnp.bfloat16)
+            part_ref[bit - 1, rows, :] = summed.astype(jnp.bfloat16)
 
 
 def stack_kernel(first_ref, last_ref, out_ref):
@@ -465,12 +494,15 @@
     out_ref[half:, :] = last_ref[0:half, :]
 
 
-def column_kernel(place_ref, part_ref, swapped_ref, out_ref):
+def column_kernel(place_ref, next_ref, next_swapped_ref, part_ref, swapped_ref, out_ref):
     side = place_ref[1]
     count, quarter, _ = part_ref.shape
+    mine, theirs = rows_of(side, quarter), rows_of(1 - side, quarter)
+    out_ref[0, mine, :] = next_ref[0:quarter, :]
+    out_ref[0, theirs, :] = next_swapped_ref[0:quarter, :]
     for level in range(count):
-        out_ref[level, rows_of(side, quarter), :] = part_ref[level]
-        out_ref[level, rows_of(1 - side, quarter), :] = swapped_ref[level]
+        out_ref[level + 1, mine, :] = part_ref[level]
+        out_ref[level + 1, theirs, :] = swapped_ref[level]
 
 
 def glue(kernel, out_shape, scratch=()):
@@ -516,84 +548,85 @@
     half, quarter = values_dim // 2, values_dim // 4
     half_heads = heads // 2
     tail = 4 * heads
-    index = lax.axis_index("seq")
-    core = index & 1
-    place = jnp.stack([core, index >> 1 & 1, index >> 2]).astype(jnp.int32)
     half_steps = half_heads // STEP
     gain = norm_gain.reshape(1, values_dim)
     planes = size // 4
     rows = table_rows(length)
+    value_inputs = pltpu.with_memory_space_constraint(value_inputs, pltpu.HBM)
     calls = NEAR_CALLS if sum(NEAR_CALLS) == heads else (heads,)
 
-    last = length // GROUP - 1
+    rim_width = 2 * state_dim + values_dim
     own_rim = pl.pallas_call(
         rim_kernel,
-        grid=(1,),
-        in_specs=[pl.BlockSpec(memory_space=pltpu.SMEM)]
-        + [pl.BlockSpec((GROUP, x.shape[1]), lambda i: (last, 0)) for x in (query_inputs, key_inputs, value_inputs)],
-        out_specs=pl.BlockSpec((rim, 2 * state_dim + values_dim), lambda i: (0, 0)),
-        out_shape=shape_of((rim, 2 * state_dim + values_dim), jnp.bfloat16),
+        in_specs=[pl.BlockSpec(memory_space=pltpu.HBM)] * 3,
+        out_specs=RESIDENT,
+        out_shape=pltpu.VMEM((rim, rim_width), jnp.bfloat16),
+        scratch_shapes=[
+            pltpu.VMEM((GROUP, rim_width), jnp.bfloat16),
+            pltpu.SemaphoreType.DMA((3,)),
+        ],
+        compiler_params=pltpu.CompilerParams(vmem_limit_bytes=62 << 20),
         name="rim",
-    )(place, query_inputs, key_inputs, value_inputs)
+    )(query_inputs, key_inputs, value_inputs)
     rims = shift(own_rim, 1, size)
 
-    tab, far_tab = pl.pallas_call(
+    tab, far_tab, place = pl.pallas_call(
         table_kernel,
-        out_specs=[RESIDENT] * 2,
+        in_specs=[RESIDENT] * 2,
+        out_specs=[RESIDENT] * 2 + [pl.BlockSpec(memory_space=pltpu.SMEM)],
         out_shape=[
             pltpu.VMEM((rows["size"], length // TILE, heads, TILE), jnp.float32),
             pltpu.VMEM((bits, length // TILE, heads, TILE), jnp.float32),
+            shape_of((3,), jnp.int32),
         ],
         compiler_params=PARAMS,
         cost_estimate=pl.CostEstimate(flops=10**9, bytes_accessed=3 * 10**6, transcendentals=0),
         name="tables",
     )(log_decay, level_weight)
 
-    vt, st, group, qt, kc = pl.pallas_call(
+    vt, st, group, kc = pl.pallas_call(
         state_kernel,
         grid=(heads // STEP,),
         in_specs=[
-            whole(query_inputs),
-            whole(key_inputs),
-            pl.BlockSpec((length, STEP * width), lambda i: (0, i)),
-            pl.BlockSpec((rim, state_dim), lambda i: (0, 0)),
-            pl.BlockSpec((rim, state_dim), lambda i: (0, 1)),
-            pl.BlockSpec((rim, STEP * width), lambda i: (0, 2 * state_dim // (STEP * width) + i)),
-            pl.BlockSpec((taps, state_dim), lambda i: (0, 0)),
+            RESIDENT,
+            pl.BlockSpec(memory_space=pl.ANY),
+            RESIDENT,
             pl.BlockSpec((taps, state_dim), lambda i: (0, 1)),
             pl.BlockSpec((taps, STEP * width), lambda i: (0, 2 * state_dim // (STEP * width) + i)),
-            whole(log_decay),
+            RESIDENT,
         ],
-        out_specs=[RESIDENT] * 5,
+        out_specs=[RESIDENT] * 4,
         out_shape=[
             pltpu.VMEM((values_dim, length), jnp.bfloat16),
             pltpu.VMEM((len(keys), values_dim, state_dim), jnp.bfloat16),
             pltpu.VMEM((values_dim + tail, state_dim), jnp.bfloat16),
-            pltpu.VMEM((state_dim, length), jnp.bfloat16),
             pltpu.VMEM((length, state_dim), jnp.bfloat16),
         ],
         scratch_shapes=[
             pltpu.VMEM((STEP, length + 8, TILE), jnp.float32),
             pltpu.VMEM((length // TILE, heads, TILE), jnp.float32),
             pltpu.VMEM((pairs, heads, TILE), jnp.float32),
+            pltpu.VMEM((heads // STEP, length, STEP * width), jnp.bfloat16),
+            pltpu.SemaphoreType.DMA((heads // STEP,)),
         ],
-        compiler_params=pltpu.CompilerParams(vmem_limit_bytes=52 << 20),
+        compiler_params=PARAMS,
         cost_estimate=pl.CostEstimate(flops=10**9, bytes_accessed=9 * 10**6, transcendentals=0),
         name="state",
-    )(
-        query_inputs, key_inputs, value_inputs, rims, rims, rims,
-        conv_weight, conv_weight, conv_weight, log_decay,
-    )
-
-    sc = pl.pallas_call(
+    )(key_inputs, value_inputs, rims, conv_weight, conv_weight, log_decay)
+
+    qt, sc = pl.pallas_call(
         score_kernel,
-        in_specs=[RESIDENT] * 2,
-        out_specs=RESIDENT,
-        out_shape=pltpu.VMEM((pairs, 2 * TILE, 2 * TILE), jnp.bfloat16),
+        in_specs=[RESIDENT] * 4,
+        out_specs=[RESIDENT] * 2,
+        out_shape=[
+            pltpu.VMEM((state_dim, length), jnp.bfloat16),
+            pltpu.VMEM((pairs, 2 * TILE, 2 * TILE), jnp.bfloat16),
+        ],
+        scratch_shapes=[pltpu.VMEM((length + 8, TILE), jnp.float32)],
         compiler_params=PARAMS,
         cost_estimate=pl.CostEstimate(flops=10**8, bytes_accessed=10**6, transcendentals=0),
         name="scores",
-    )(qt, kc)
+    )(query_inputs, rims, conv_weight, kc)
 
     near = vt
     for call, each in enumerate(calls):
@@ -632,16 +665,15 @@
     for by in range(1, planes):
         came.append(send(message, 4 * by, size))
 
+    next_swapped = send(came[0], 2, size)
+
     low = glue(stack_kernel, pltpu.VMEM((half, state_dim), jnp.bfloat16))(got_rest, got)
     low_other = send(low, 1, size)
 
     count = bits - 2
     far_factor, part = glue(
         functools.partial(plane_kernel, width),
-        [
-            pltpu.VMEM((bits, heads, state_dim), jnp.float32),
-            pltpu.VMEM((count, quarter, state_dim), jnp.bfloat16),
-        ],
+        [pltpu.VMEM((bits, heads, state_dim), jnp.float32), pltpu.VMEM((count - 1, quarter, state_dim), jnp.bfloat16)],
         [pltpu.VMEM((planes - 1, heads, state_dim), jnp.float32)],
     )(*came, keep, place=place)
 
@@ -670,7 +702,9 @@
     )(place, near, other, low, low_other, far_tab, qt, far_factor)
 
     swapped = send(part, 2, size)
-    high = glue(column_kernel, pltpu.VMEM((count, half, state_dim), jnp.bfloat16))(part, swapped, place=place)
+    high = glue(column_kernel, pltpu.VMEM((count, half, state_dim), jnp.bfloat16))(
+        came[0], next_swapped, part, swapped, place=place
+    )
     high_other = send(high, 1, size)
 
     out = None

time: 78.2 us -> 69.9 us (0.89)
  waiting for transfers between devices: 25.5 us -> 19.1 us
  Pallas kernels: 35.5 us -> 33.8 us
  starting transfers between devices: 15.5 us -> 16.7 us
    ppermute x9 -> x10, waiting for transfers between devices: 24.5 us -> 18.2 us  [send(): return lax.ppermute(x, 'seq', [(i, i ^ by) for i in range(size)])]
    pallas_call x4, Pallas kernels: 11.2 us -> 9.39 us  [the longest x1 7.26 us: on_device(): pl.pallas_call(state_kernel, grid=(heads // STEP,), in_specs=[RESIDENT, p...]
    ppermute x9 -> x10, starting transfers between devices: 13 us -> 14.3 us  [send(): return lax.ppermute(x, 'seq', [(i, i ^ by) for i in range(size)])]
    pallas_call x2 -> x3, Pallas kernels: 10.6 us -> 10.8 us  [on_device(): pl.pallas_call(functools.partial(near_kernel, sum(calls[:call]), width),...]
  transfers between devices with their start and end apart: 10 -> 11, of which waited for: 7 -> 7; matrix products, arithmetic and copies ran while one was open for 0% -> 0% of each run, Pallas kernels for 25% -> 29%
where the time goes in v3:
time: 69.9 us; the launch traced here: 69.7 us
  Pallas kernels  33.8 us (48%)
  waiting for transfers between devices  19.1 us (27%)
  starting transfers between devices  16.7 us (24%)
    ppermute x10, waiting for transfers between devices, send(): return lax.ppermute(x, 'seq', [(i, i ^ by) for i in range(size)])  18.2 us
    ppermute x10, starting transfers between devices, send(): return lax.ppermute(x, 'seq', [(i, i ^ by) for i in range(size)])  14.3 us
    pallas_call x3, Pallas kernels, on_device(): pl.pallas_call(functools.partial(near_kernel, sum(calls[:call]), width),...  10.8 us
    pallas_call x2, Pallas kernels, on_device(): pl.pallas_call(functools.partial(far_kernel, width, call), grid_spec=pltp...  7.6 us
    pallas_call x1, Pallas kernels, on_device(): pl.pallas_call(state_kernel, grid=(heads // STEP,), in_specs=[RESIDENT, p...  7.26 us
    pallas_call x1, Pallas kernels, on_device(): pl.pallas_call(functools.partial(mid_kernel, width), grid_spec=pltpu.Pref...  3.46 us
    pallas_call x5, Pallas kernels, call(): pl.pallas_call(kernel, in_specs=[scalar for _ in first] + [RESIDENT for _...  2.54 us
    ppermute x1, starting transfers between devices, shift(): return lax.ppermute(x, 'seq', [(i, i + by) for i in range(size - by)])  2.41 us
  transfers between devices with their start and end apart: 11, of which 7 were waited for; matrix products, arithmetic and copies ran while one was open for 0% of the time, Pallas kernels for 29%

profile of v3, /device:TPU:0, one launch (start us, length us, event | category | flops | bytes accessed | tf_op | source)
XLA Modules:
  0.0 69.7 jit_solution(6326051256972935083)
XLA Ops:
  0.0 1.0 %rim.1 = bf16[3,2304]{1,0:T(4,128)(2,1)S(1)} custom-call(bf16[1024,128]{1,0:T(8,128)(2,1)} %q_ref.3, bf16[1024,128]{1,0:T(8,128)(2,1)} %k_ref.3, bf16[1024,2048]{1,0:T(8,128)(2,1)} %v_ref.3), custom_call_target="tpu_custom_call" | custom-call | tf_op jit(solution)/shard_map/rim/pallas_call | solution.py:559
  1.0 2.4 %collective-permute-start = (bf16[3,2304]{1,0:T(4,128)(2,1)S(1)}, bf16[3,2304]{1,0:T(4,128)(2,1)S(1)}, u32[]{:S(2)}, u32[]{:S(2)}) collective-permute-start(bf16[3,2304]{1,0:T(4,128)(2,1)S(1)} %rim.1), channel_id=1, source_target_pairs={{0,1},{1,2},{2,3},{3,4},{4,5},{5,6},{6,7},{7,8},{8,9},{9,10},{10,1... | collective-permute-start | bytes 41480 | tf_op jit(solution)/shard_map/ppermute | solution.py:532
  3.4 0.8 %collective-permute-done.rim_ref = bf16[3,2304]{1,0:T(4,128)(2,1)S(1)} collective-permute-done((bf16[3,2304]{1,0:T(4,128)(2,1)S(1)}, bf16[3,2304]{1,0:T(4,128)(2,1)S(1)}, u32[]{:S(2)}, u32[]{:S(2)}) %collective-permute-start) | collective-permute-done | bytes 13856 | tf_op jit(solution)/shard_map/ppermute | solution.py:532
  4.3 7.3 %state.1 = (bf16[2048,1024]{1,0:T(8,128)(2,1)S(1)}, bf16[3,2048,128]{2,1,0:T(8,128)(2,1)S(1)}, bf16[2112,128]{1,0:T(8,128)(2,1)S(1)}, bf16[1024,128]{1,0:T(8,128)(2,1)S(1)}) custom-call(bf16[1024,128]{1,0:T(8,128)(2,1)S(1)} %copy-done, bf16[1024,2048]{1,0:T(8,128)(2,1)} %v_ref.3, bf16[3,2304]{1,0:T(4,128)(2,1)S(1)} %collective-permute-done.rim_ref, ...), custom_call_target="tpu_custom_call" | custom-call | flops 1000000000 | bytes 9000000 | tf_op jit(solution)/shard_map/state/pallas_call | solution.py:587
  11.5 0.0 copy-start.1
  11.5 2.7 %collective-permute-start.1 = (bf16[2112,128]{1,0:T(8,128)(2,1)S(1)}, bf16[2112,128]{1,0:T(8,128)(2,1)S(1)}, u32[]{:S(2)}, u32[]{:S(2)}) collective-permute-start(bf16[2112,128]{1,0:T(8,128)(2,1)S(1)} %get-tuple-element.28.own_ref), channel_id=1, source_target_pairs={{0,1},{1,0},{2,3},{3,2},{4,5},{5,4},{6,7},{7,6},{8,9},{9,8},{10,11... | collective-permute-start | bytes 1622024 | tf_op jit(solution)/shard_map/ppermute | solution.py:528
  14.3 0.6 tables.1
  14.9 0.9 %collective-permute-done.1.other_ref.chip_ref = bf16[2112,128]{1,0:T(8,128)(2,1)S(1)} collective-permute-done((bf16[2112,128]{1,0:T(8,128)(2,1)S(1)}, bf16[2112,128]{1,0:T(8,128)(2,1)S(1)}, u32[]{:S(2)}, u32[]{:S(2)}) %collective-permute-start.1) | collective-permute-done | bytes 540704 | tf_op jit(solution)/shard_map/ppermute | solution.py:528
  15.8 0.7 shard_map.73
  16.5 2.6 %collective-permute-start.3 = (bf16[576,128]{1,0:T(8,128)(2,1)S(1)}, bf16[576,128]{1,0:T(8,128)(2,1)S(1)}, u32[]{:S(2)}, u32[]{:S(2)}) collective-permute-start(bf16[576,128]{1,0:T(8,128)(2,1)S(1)} %get-tuple-element.30), channel_id=1, source_target_pairs={{0,2},{1,3},{2,0},{3,1},{4,6},{5,7},{6,4},{7,5},{8,10},{9,11},{10,... | collective-permute-start | bytes 442376 | tf_op jit(solution)/shard_map/ppermute | solution.py:528
  19.1 4.1 %collective-permute-done.3.last_ref.got_ref = bf16[576,128]{1,0:T(8,128)(2,1)S(1)} collective-permute-done((bf16[576,128]{1,0:T(8,128)(2,1)S(1)}, bf16[576,128]{1,0:T(8,128)(2,1)S(1)}, u32[]{:S(2)}, u32[]{:S(2)}) %collective-permute-start.3) | collective-permute-done | bytes 147488 | tf_op jit(solution)/shard_map/ppermute | solution.py:528
  23.3 0.6 shard_map.75
  23.9 2.8 %collective-permute-start.5 = (bf16[576,128]{1,0:T(8,128)(2,1)S(1)}, bf16[576,128]{1,0:T(8,128)(2,1)S(1)}, u32[]{:S(2)}, u32[]{:S(2)}) collective-permute-start(bf16[576,128]{1,0:T(8,128)(2,1)S(1)} %get-tuple-element.33), channel_id=1, source_target_pairs={{0,4},{1,5},{2,6},{3,7},{4,0},{5,1},{6,2},{7,3},{8,12},{9,13},{10,... | collective-permute-start | bytes 442376 | tf_op jit(solution)/shard_map/ppermute | solution.py:528
  26.7 2.6 %collective-permute-start.6 = (bf16[576,128]{1,0:T(8,128)(2,1)S(1)}, bf16[576,128]{1,0:T(8,128)(2,1)S(1)}, u32[]{:S(2)}, u32[]{:S(2)}) collective-permute-start(bf16[576,128]{1,0:T(8,128)(2,1)S(1)} %get-tuple-element.33), channel_id=1, source_target_pairs={{0,8},{1,9},{2,10},{3,11},{4,12},{5,13},{6,14},{7,15},{8,0},{9,1},... | collective-permute-start | bytes 442376 | tf_op jit(solution)/shard_map/ppermute | solution.py:528
  29.3 2.4 %collective-permute-done.5.refs_0_.next_ref = bf16[576,128]{1,0:T(8,128)(2,1)S(1)} collective-permute-done((bf16[576,128]{1,0:T(8,128)(2,1)S(1)}, bf16[576,128]{1,0:T(8,128)(2,1)S(1)}, u32[]{:S(2)}, u32[]{:S(2)}) %collective-permute-start.5) | collective-permute-done | bytes 147488 | tf_op jit(solution)/shard_map/ppermute | solution.py:528
  31.7 1.0 %collective-permute-start.8 = (bf16[576,128]{1,0:T(8,128)(2,1)S(1)}, bf16[576,128]{1,0:T(8,128)(2,1)S(1)}, u32[]{:S(2)}, u32[]{:S(2)}) collective-permute-start(bf16[576,128]{1,0:T(8,128)(2,1)S(1)} %collective-permute-done.5.refs_0_.next_ref), channel_id=1, source_target_pairs={{0,2},{1,3},{2,0},{3,1},{4,6},{5,7},{6,4},{7,5},{8,10},{9,11},{10,... | collective-permute-start | bytes 442376 | tf_op jit(solution)/shard_map/ppermute | solution.py:528
  32.7 7.6 %collective-permute-done.6.refs_1_ = bf16[576,128]{1,0:T(8,128)(2,1)S(1)} collective-permute-done((bf16[576,128]{1,0:T(8,128)(2,1)S(1)}, bf16[576,128]{1,0:T(8,128)(2,1)S(1)}, u32[]{:S(2)}, u32[]{:S(2)}) %collective-permute-start.6) | collective-permute-done | bytes 147488 | tf_op jit(solution)/shard_map/ppermute | solution.py:528
  40.3 0.7 shard_map.76
  40.9 0.7 collective-permute-start.9
  41.6 1.4 %collective-permute-start.2 = (bf16[512,128]{1,0:T(8,128)(2,1)S(1)}, bf16[512,128]{1,0:T(8,128)(2,1)S(1)}, u32[]{:S(2)}, u32[]{:S(2)}) collective-permute-start(bf16[512,128]{1,0:T(8,128)(2,1)S(1)} %get-tuple-element.29.mine_ref), channel_id=1, source_target_pairs={{0,2},{1,3},{2,0},{3,1},{4,6},{5,7},{6,4},{7,5},{8,10},{9,11},{10,... | collective-permute-start | bytes 393224 | tf_op jit(solution)/shard_map/ppermute | solution.py:528
  43.0 2.9 %collective-permute-done.9.swapped_ref = bf16[1,512,128]{2,1,0:T(8,128)(2,1)S(1)} collective-permute-done((bf16[1,512,128]{2,1,0:T(8,128)(2,1)S(1)}, bf16[1,512,128]{2,1,0:T(8,128)(2,1)S(1)}, u32[]{:S(2)}, u32[]{:S(2)}) %collective-permute-start.9) | collective-permute-done | bytes 131104 | tf_op jit(solution)/shard_map/ppermute | solution.py:528
  46.0 0.6 shard_map.77.high_ref
  46.6 0.1 collective-permute-start.10
  46.6 0.5 scores.1
  47.2 0.2 collective-permute-done.2.first_ref
  47.4 0.4 collective-permute-start.4
  47.8 2.7 %near.3.vt_ref = bf16[2048,1024]{1,0:T(8,128)(2,1)S(1)} custom-call(bf16[2048,1024]{1,0:T(8,128)(2,1)S(1)} %get-tuple-element.22.vt_ref, bf16[3,2048,128]{2,1,0:T(8,128)(2,1)S(1)} %get-tuple-element.23.st_ref, f32[17,8,16,128]{3,2,1,0:T(8,128)S(1)} %get-tuple-element.24.tab_ref, ...), custom_call_target="tpu_custom_call", output_to_operand_aliasing={{}: (0, {})} | custom-call | flops 1000000000 | bytes 4000000 | tf_op jit(solution)/shard_map/near/pallas_call | solution.py:633
  50.5 4.0 %near.4.vt_ref = bf16[2048,1024]{1,0:T(8,128)(2,1)S(1)} custom-call(bf16[2048,1024]{1,0:T(8,128)(2,1)S(1)} %near.3.vt_ref, bf16[3,2048,128]{2,1,0:T(8,128)(2,1)S(1)} %get-tuple-element.23.st_ref, f32[17,8,16,128]{3,2,1,0:T(8,128)S(1)} %get-tuple-element.24.tab_ref, bf16[4,256,256]{2,1,0:T(8,128)(2,1)S(1)} %get-tuple-element.26.sc, ...), custom_call_target="tpu_custom_call", output_to_operand_aliasing={{}: (0, {})} | custom-call | flops 1000000000 | bytes 4000000 | tf_op jit(solution)/shard_map/near/pallas_call | solution.py:633
  54.5 4.0 %near.5.near_ref = bf16[2048,1024]{1,0:T(8,128)(2,1)S(1)} custom-call(bf16[2048,1024]{1,0:T(8,128)(2,1)S(1)} %near.4.vt_ref, bf16[3,2048,128]{2,1,0:T(8,128)(2,1)S(1)} %get-tuple-element.23.st_ref, f32[17,8,16,128]{3,2,1,0:T(8,128)S(1)} %get-tuple-element.24.tab_ref, bf16[4,256,256]{2,1,0:T(8,128)(2,1)S(1)} %get-tuple-element.26.sc, ...), custom_call_target="tpu_custom_call", output_to_operand_aliasing={{}: (0, {})} | custom-call | flops 1000000000 | bytes 4000000 | tf_op jit(solution)/shard_map/near/pallas_call | solution.py:633
  58.6 3.5 %mid.1.near_ref = bf16[2048,1024]{1,0:T(8,128)(2,1)S(1)} custom-call(s32[3]{0:T(128)S(1)} %get-tuple-element.21.place_ref, bf16[2048,1024]{1,0:T(8,128)(2,1)S(1)} %near.5.near_ref, bf16[2112,128]{1,0:T(8,128)(2,1)S(1)} %collective-permute-done.1.other_ref.chip_ref, bf16[1024,128]{1,0:T(8,128)(2,1)S(1)} %shard_map.74.low_ref, ...), custom_call_target="tpu_custom_call", output_to_operand_aliasing={{}: (1, {})} | custom-call | flops 1000000000 | bytes 6000000 | tf_op jit(solution)/shard_map/mid/pallas_call | solution.py:680
  62.1 3.8 %far.2.refs_0_ = bf16[1024,2048]{1,0:T(8,128)(2,1)} custom-call(s32[3]{0:T(128)S(1)} %get-tuple-element.21.place_ref, bf16[2048,1024]{1,0:T(8,128)(2,1)S(1)} %mid.1.near_ref, bf16[2,1024,128]{2,1,0:T(8,128)(2,1)S(1)} %shard_map.77.high_ref, f32[4,8,16,128]{3,2,1,0:T(8,128)S(1)} %get-tuple-element.31.far_ref, bf16[128,1024]{1,0:T(8,128)(2,1)S(1)} %get-tuple-element.27.qt_ref, ...), custom_call_target="tpu_custom_call" | custom-call | flops 1000000000 | bytes 6000000 | tf_op jit(solution)/shard_map/far/pallas_call | solution.py:717
  65.9 3.8 %far.3 = bf16[1024,2048]{1,0:T(8,128)(2,1)} custom-call(s32[3]{0:T(128)S(1)} %get-tuple-element.21.place_ref, bf16[2048,1024]{1,0:T(8,128)(2,1)S(1)} %mid.1.near_ref, bf16[2,1024,128]{2,1,0:T(8,128)(2,1)S(1)} %collective-permute-done.10.high_ref, f32[4,8,16,128]{3,2,1,0:T(8,128)S(1)} %get-tuple-element.31.far_ref, ...), custom_call_target="tpu_custom_call", output_to_operand_aliasing={{}: (7, {})} | custom-call | flops 1000000000 | bytes 6000000 | tf_op jit(solution)/shard_map/far/pallas_call | solution.py:717
  (17 shorter events, 0.1 us)
Async XLA Ops:
  0.0 4.2 %copy-start = (bf16[1024,128]{1,0:T(8,128)(2,1)S(1)}, bf16[1024,128]{1,0:T(8,128)(2,1)}, u32[]{:S(2)}) copy-start(bf16[1024,128]{1,0:T(8,128)(2,1)} %k_ref.3) | copy-start | bytes 786436
  0.0 4.2 %copy-start.3 = (f32[16,1024]{1,0:T(8,128)S(1)}, f32[16,1024]{1,0:T(8,128)}, u32[]{:S(2)}) copy-start(f32[16,1024]{1,0:T(8,128)} %ld_ref.3) | copy-start | bytes 196612
  0.0 4.2 %copy-start.2 = (f32[4,2304]{1,0:T(4,128)S(1)}, f32[4,2304]{1,0:T(4,128)}, u32[]{:S(2)}) copy-start(f32[4,2304]{1,0:T(4,128)} %w_ref.1) | copy-start | bytes 110596
  0.0 14.3 %copy-start.5 = (bf16[15,16,1024]{2,1,0:T(8,128)(2,1)S(1)}, bf16[15,16,1024]{2,1,0:T(8,128)(2,1)}, u32[]{:S(2)}) copy-start(bf16[15,16,1024]{2,1,0:T(8,128)(2,1)} %lw_ref.1) | copy-start | bytes 1474564
  1.0 3.2 %collective-permute-start = (bf16[3,2304]{1,0:T(4,128)(2,1)S(1)}, bf16[3,2304]{1,0:T(4,128)(2,1)S(1)}, u32[]{:S(2)}, u32[]{:S(2)}) collective-permute-start(bf16[3,2304]{1,0:T(4,128)(2,1)S(1)} %rim.1), channel_id=1, source_target_pairs={{0,1},{1,2},{2,3},{3,4},{4,5},{5,6},{6,7},{7,8},{8,9},{9,10},{10,1... | collective-permute-start | bytes 41480 | tf_op jit(solution)/shard_map/ppermute | solution.py:532
  11.5 35.1 %copy-start.1 = (bf16[1024,128]{1,0:T(8,128)(2,1)S(1)}, bf16[1024,128]{1,0:T(8,128)(2,1)}, u32[]{:S(2)}) copy-start(bf16[1024,128]{1,0:T(8,128)(2,1)} %q_ref.3) | copy-start | bytes 786436
  11.5 4.3 %collective-permute-start.1 = (bf16[2112,128]{1,0:T(8,128)(2,1)S(1)}, bf16[2112,128]{1,0:T(8,128)(2,1)S(1)}, u32[]{:S(2)}, u32[]{:S(2)}) collective-permute-start(bf16[2112,128]{1,0:T(8,128)(2,1)S(1)} %get-tuple-element.28.own_ref), channel_id=1, source_target_pairs={{0,1},{1,0},{2,3},{3,2},{4,5},{5,4},{6,7},{7,6},{8,9},{9,8},{10,11... | collective-permute-start | bytes 1622024 | tf_op jit(solution)/shard_map/ppermute | solution.py:528
  16.5 6.8 %collective-permute-start.3 = (bf16[576,128]{1,0:T(8,128)(2,1)S(1)}, bf16[576,128]{1,0:T(8,128)(2,1)S(1)}, u32[]{:S(2)}, u32[]{:S(2)}) collective-permute-start(bf16[576,128]{1,0:T(8,128)(2,1)S(1)} %get-tuple-element.30), channel_id=1, source_target_pairs={{0,2},{1,3},{2,0},{3,1},{4,6},{5,7},{6,4},{7,5},{8,10},{9,11},{10,... | collective-permute-start | bytes 442376 | tf_op jit(solution)/shard_map/ppermute | solution.py:528
  23.9 7.8 %collective-permute-start.5 = (bf16[576,128]{1,0:T(8,128)(2,1)S(1)}, bf16[576,128]{1,0:T(8,128)(2,1)S(1)}, u32[]{:S(2)}, u32[]{:S(2)}) collective-permute-start(bf16[576,128]{1,0:T(8,128)(2,1)S(1)} %get-tuple-element.33), channel_id=1, source_target_pairs={{0,4},{1,5},{2,6},{3,7},{4,0},{5,1},{6,2},{7,3},{8,12},{9,13},{10,... | collective-permute-start | bytes 442376 | tf_op jit(solution)/shard_map/ppermute | solution.py:528
  26.7 13.6 %collective-permute-start.6 = (bf16[576,128]{1,0:T(8,128)(2,1)S(1)}, bf16[576,128]{1,0:T(8,128)(2,1)S(1)}, u32[]{:S(2)}, u32[]{:S(2)}) collective-permute-start(bf16[576,128]{1,0:T(8,128)(2,1)S(1)} %get-tuple-element.33), channel_id=1, source_target_pairs={{0,8},{1,9},{2,10},{3,11},{4,12},{5,13},{6,14},{7,15},{8,0},{9,1},... | collective-permute-start | bytes 442376 | tf_op jit(solution)/shard_map/ppermute | solution.py:528
  29.3 11.0 %collective-permute-start.7 = (bf16[576,128]{1,0:T(8,128)(2,1)S(1)}, bf16[576,128]{1,0:T(8,128)(2,1)S(1)}, u32[]{:S(2)}, u32[]{:S(2)}) collective-permute-start(bf16[576,128]{1,0:T(8,128)(2,1)S(1)} %get-tuple-element.33), channel_id=1, source_target_pairs={{0,12},{1,13},{2,14},{3,15},{4,8},{5,9},{6,10},{7,11},{8,4},{9,5},... | collective-permute-start | bytes 442376 | tf_op jit(solution)/shard_map/ppermute | solution.py:528
  31.7 14.3 %collective-permute-start.8 = (bf16[576,128]{1,0:T(8,128)(2,1)S(1)}, bf16[576,128]{1,0:T(8,128)(2,1)S(1)}, u32[]{:S(2)}, u32[]{:S(2)}) collective-permute-start(bf16[576,128]{1,0:T(8,128)(2,1)S(1)} %collective-permute-done.5.refs_0_.next_ref), channel_id=1, source_target_pairs={{0,2},{1,3},{2,0},{3,1},{4,6},{5,7},{6,4},{7,5},{8,10},{9,11},{10,... | collective-permute-start | bytes 442376 | tf_op jit(solution)/shard_map/ppermute | solution.py:528
  40.9 5.0 %collective-permute-start.9 = (bf16[1,512,128]{2,1,0:T(8,128)(2,1)S(1)}, bf16[1,512,128]{2,1,0:T(8,128)(2,1)S(1)}, u32[]{:S(2)}, u32[]{:S(2)}) collective-permute-start(bf16[1,512,128]{2,1,0:T(8,128)(2,1)S(1)} %get-tuple-element.36.part_ref), channel_id=1, source_target_pairs={{0,2},{1,3},{2,0},{3,1},{4,6},{5,7},{6,4},{7,5},{8,10},{9,11},{10,... | collective-permute-start | bytes 393224 | tf_op jit(solution)/shard_map/ppermute | solution.py:528
  41.6 5.8 %collective-permute-start.2 = (bf16[512,128]{1,0:T(8,128)(2,1)S(1)}, bf16[512,128]{1,0:T(8,128)(2,1)S(1)}, u32[]{:S(2)}, u32[]{:S(2)}) collective-permute-start(bf16[512,128]{1,0:T(8,128)(2,1)S(1)} %get-tuple-element.29.mine_ref), channel_id=1, source_target_pairs={{0,2},{1,3},{2,0},{3,1},{4,6},{5,7},{6,4},{7,5},{8,10},{9,11},{10,... | collective-permute-start | bytes 393224 | tf_op jit(solution)/shard_map/ppermute | solution.py:528
  46.6 19.3 %collective-permute-start.10 = (bf16[2,1024,128]{2,1,0:T(8,128)(2,1)S(1)}, bf16[2,1024,128]{2,1,0:T(8,128)(2,1)S(1)}, u32[]{:S(2)}, u32[]{:S(2)}) collective-permute-start(bf16[2,1024,128]{2,1,0:T(8,128)(2,1)S(1)} %shard_map.77.high_ref), channel_id=1, source_target_pairs={{0,1},{1,0},{2,3},{3,2},{4,5},{5,4},{6,7},{7,6},{8,9},{9,8},{10,11... | collective-permute-start | bytes 1572872 | tf_op jit(solution)/shard_map/ppermute | solution.py:528
  47.4 11.2 %collective-permute-start.4 = (bf16[1024,128]{1,0:T(8,128)(2,1)S(1)}, bf16[1024,128]{1,0:T(8,128)(2,1)S(1)}, u32[]{:S(2)}, u32[]{:S(2)}) collective-permute-start(bf16[1024,128]{1,0:T(8,128)(2,1)S(1)} %shard_map.74.low_ref), channel_id=1, source_target_pairs={{0,1},{1,0},{2,3},{3,2},{4,5},{5,4},{6,7},{7,6},{8,9},{9,8},{10,11... | collective-permute-start | bytes 786440 | tf_op jit(solution)/shard_map/ppermute | solution.py:528
  58.6 3.5 %copy-start.4 = (f32[2048]{0:T(1024)S(1)}, f32[2048]{0:T(1024)}, u32[]{:S(2)}) copy-start(f32[2048]{0:T(1024)} %param.13) | copy-start | bytes 24580

commit v4 on v3

--- a/solution.py
+++ b/solution.py
@@ -11,7 +11,7 @@
 EPSILON = 1e-05
 TILE = 128
 GROUP = 16
-NEAR_CALLS = (4, 6, 6)
+NEAR_CALLS = (6, 4, 6)
 STEP = 2
 
 
@@ -82,19 +82,18 @@
 
 
 def three_terms(wide):
-    terms = []
-    for _ in range(3):
-        term = wide.astype(jnp.bfloat16)
-        terms.append(term)
-        wide = wide - term.astype(jnp.float32)
-    terms.append(jnp.zeros_like(terms[0]))
-    return jnp.concatenate(terms, axis=0)
+    lane = lax.broadcasted_iota(jnp.int32, wide.shape, 1)
+    terms = jnp.zeros_like(wide)
+    for order in range(3):
+        term = wide.astype(jnp.bfloat16).astype(jnp.float32)
+        terms = jnp.where(lane == order, term, terms)
+        wide = wide - term
+    return terms.astype(jnp.bfloat16)
 
 
 def sum_terms(terms):
-    each = terms.shape[0] // 4
     wide = terms.astype(jnp.float32)
-    return wide[:each] + wide[each : 2 * each] + wide[2 * each : 3 * each]
+    return jnp.broadcast_to(wide[:, 0:1] + wide[:, 1:2] + wide[:, 2:3], wide.shape)
 
 
 def state_kernel(
@@ -127,7 +126,7 @@
             both = totals[low] + totals[high]
             total[pair] = jnp.exp(both)
             summed = both if summed is None else summed + both
-        g_ref[pl.ds(heads * width, 4 * heads), :] = three_terms(summed)
+        g_ref[pl.ds(heads * width, heads), :] = three_terms(summed)
         fill(buf.at[0], k_ref, rim_ref.at[:, state_dim : 2 * state_dim])
         for tile in range(length // TILE):
             at = tile * TILE
@@ -365,19 +364,21 @@
 
 
 def mid_kernel(
-    width, place_ref, near_ref, chip_ref, low_ref, low_other_ref, far_ref, qt_ref, off_ref, out_ref, rest
+    width, near_ref, chip_ref, low_ref, low_other_ref, far_ref, qt_ref, off_ref, out_ref, rest
 ):
     step, steps = pl.program_id(0), pl.num_programs(0)
+    core, _, _ = position()
+    half = steps // 2 * STEP
     for place in range(STEP):
-        own = slice(place * width, (place + 1) * width)
-        head = lax.rem(place_ref[0] * (steps // 2) + step, steps) * STEP + place
-        low = jnp.where(step < steps // 2, low_ref[own, :], low_other_ref[own, :])
+        head = lax.rem(core * (steps // 2) + step, steps) * STEP + place
+        rows = rows_of(lax.rem(head, half), width)
+        low = jnp.where(step < steps // 2, low_ref[rows, :], low_other_ref[rows, :])
 
         def finish(at, summed, head=head):
             out_ref[rows_of(head, width), at : at + 2 * TILE] = summed.astype(jnp.bfloat16)
 
         add_far(
-            (0, 1), head, width, near_ref, [chip_ref[own, :], low], far_ref, qt_ref, off_ref, rest.at[place], finish
+            (0, 1), head, width, near_ref, [chip_ref[rows_of(head, width), :], low], far_ref, qt_ref, off_ref, rest.at[place], finish
         )
 
 
@@ -412,11 +413,16 @@
         )
 
 
-def core_kernel(width, place_ref, own_ref, other_ref, theirs_ref, mine_ref, keep_ref, factor):
+def position():
+    index = lax.axis_index("seq")
+    return index & 1, index >> 1 & 1, index >> 2
+
+
+def core_kernel(width, own_ref, other_ref, theirs_ref, mine_ref, keep_ref, factor):
     heads = keep_ref.shape[1]
     states = heads * width
     quarter = heads // 4
-    core, side = place_ref[0], place_ref[1]
+    core, side, _ = position()
     upper = core == 1
     own_total = sum_terms(own_ref[states:, :])
     other_total = sum_terms(other_ref[states:, :])
@@ -434,10 +440,10 @@
     theirs_ref[quarter * width :, :] = three_terms(own_total + other_total)
 
 
-def side_kernel(width, place_ref, got_ref, mine_ref, chip_ref, message_ref, keep_ref, factor):
+def side_kernel(width, got_ref, mine_ref, chip_ref, message_ref, keep_ref, factor):
     heads = keep_ref.shape[1]
     quarter = heads // 4
-    core, side = place_ref[0], place_ref[1]
+    core, side, _ = position()
     upper = side == 1
     chip_total = chip_ref[0]
     got_total = sum_terms(got_ref[quarter * width :, :])
@@ -453,12 +459,12 @@
     message_ref[quarter * width :, :] = three_terms(chip_total + got_total)
 
 
-def plane_kernel(width, place_ref, *refs):
+def plane_kernel(width, *refs):
     far_ref, part_ref, factor = refs[-3:]
     came, keep_ref = refs[:-4], refs[-4]
     heads = keep_ref.shape[1]
     quarter = heads // 4
-    core, side, plane = place_ref[0], place_ref[1], place_ref[2]
+    core, side, plane = position()
     planes = len(came) + 1
     totals = [sum_terms(ref[quarter * width :, :]) for ref in came]
     zero = jnp.zeros_like(totals[0])
@@ -494,8 +500,8 @@
     out_ref[half:, :] = last_ref[0:half, :]
 
 
-def column_kernel(place_ref, next_ref, next_swapped_ref, part_ref, swapped_ref, out_ref):
-    side = place_ref[1]
+def column_kernel(next_ref, next_swapped_ref, part_ref, swapped_ref, out_ref):
+    _, side, _ = position()
     count, quarter, _ = part_ref.shape
     mine, theirs = rows_of(side, quarter), rows_of(1 - side, quarter)
     out_ref[0, mine, :] = next_ref[0:quarter, :]
@@ -506,30 +512,23 @@
 
 
 def glue(kernel, out_shape, scratch=()):
-    scalar = pl.BlockSpec(memory_space=pltpu.SMEM)
-
-    def call(*args, place=None):
-        first = [] if place is None else [place]
+    def call(*args):
         many = isinstance(out_shape, list)
         return pl.pallas_call(
             kernel,
-            in_specs=[scalar for _ in first] + [RESIDENT for _ in args],
+            in_specs=[RESIDENT for _ in args],
             out_specs=[RESIDENT for _ in out_shape] if many else RESIDENT,
             out_shape=out_shape,
             scratch_shapes=list(scratch),
             compiler_params=PARAMS,
             cost_estimate=pl.CostEstimate(flops=10**7, bytes_accessed=10**6, transcendentals=0),
-        )(*first, *args)
+        )(*args)
 
     return call
 
 
 def send(x, by, size):
     return lax.ppermute(x, "seq", [(i, i ^ by) for i in range(size)])
-
-
-def shift(x, by, size):
-    return lax.ppermute(x, "seq", [(i, i + by) for i in range(size - by)])
 
 
 def on_device(
@@ -547,7 +546,7 @@
     keys = state_keys(pairs)
     half, quarter = values_dim // 2, values_dim // 4
     half_heads = heads // 2
-    tail = 4 * heads
+    tail = heads
     half_steps = half_heads // STEP
     gain = norm_gain.reshape(1, values_dim)
     planes = size // 4
@@ -568,7 +567,7 @@
         compiler_params=pltpu.CompilerParams(vmem_limit_bytes=62 << 20),
         name="rim",
     )(query_inputs, key_inputs, value_inputs)
-    rims = shift(own_rim, 1, size)
+    rims = lax.ppermute(own_rim, "seq", [(i, i + 1) for i in range(size - 1)])
 
     tab, far_tab, place = pl.pallas_call(
         table_kernel,
@@ -651,15 +650,21 @@
     message_shape = pltpu.VMEM((quarter + tail, state_dim), jnp.bfloat16)
     theirs, mine, keep = glue(
         functools.partial(core_kernel, width),
-        [message_shape, pltpu.VMEM((quarter, state_dim), jnp.bfloat16), pltpu.VMEM((2, heads, state_dim), jnp.float32)],
+        [
+            message_shape,
+            pltpu.VMEM((quarter, state_dim), jnp.bfloat16),
+            pltpu.VMEM((2, heads, state_dim), jnp.float32),
+        ],
         [table],
-    )(group, other, place=place)
+    )(group, other)
 
     got = send(theirs, 2, size)
     got_rest = send(mine, 2, size)
     message, keep = glue(
-        functools.partial(side_kernel, width), [message_shape, pltpu.VMEM((2, heads, state_dim), jnp.float32)], [table]
-    )(got, mine, keep, place=place)
+        functools.partial(side_kernel, width),
+        [message_shape, pltpu.VMEM((2, heads, state_dim), jnp.float32)],
+        [table],
+    )(got, mine, keep)
 
     came = []
     for by in range(1, planes):
@@ -673,37 +678,29 @@
     count = bits - 2
     far_factor, part = glue(
         functools.partial(plane_kernel, width),
-        [pltpu.VMEM((bits, heads, state_dim), jnp.float32), pltpu.VMEM((count - 1, quarter, state_dim), jnp.bfloat16)],
+        [
+            pltpu.VMEM((bits, heads, state_dim), jnp.float32),
+            pltpu.VMEM((count - 1, quarter, state_dim), jnp.bfloat16),
+        ],
         [pltpu.VMEM((planes - 1, heads, state_dim), jnp.float32)],
-    )(*came, keep, place=place)
+    )(*came, keep)
 
     near = pl.pallas_call(
         functools.partial(mid_kernel, width),
-        grid_spec=pltpu.PrefetchScalarGridSpec(
-            num_scalar_prefetch=1,
-            grid=(2 * half_steps,),
-            in_specs=[
-                RESIDENT,
-                pl.BlockSpec((STEP * width, state_dim), lambda i, s: (lax.rem(s[0] * half_steps + i, 2 * half_steps), 0)),
-                pl.BlockSpec((STEP * width, state_dim), lambda i, s: (jnp.minimum(i, half_steps - 1), 0)),
-                pl.BlockSpec((STEP * width, state_dim), lambda i, s: (jnp.maximum(i - half_steps, 0), 0)),
-                RESIDENT,
-                RESIDENT,
-                RESIDENT,
-            ],
-            out_specs=RESIDENT,
-            scratch_shapes=[pltpu.VMEM((STEP, pairs, 2 * state_dim, 2 * TILE), jnp.bfloat16)],
-        ),
+        grid=(2 * half_steps,),
+        in_specs=[RESIDENT] * 7,
+        out_specs=RESIDENT,
+        scratch_shapes=[pltpu.VMEM((STEP, pairs, 2 * state_dim, 2 * TILE), jnp.bfloat16)],
         out_shape=pltpu.VMEM((values_dim, length), jnp.bfloat16),
-        input_output_aliases={1: 0},
+        input_output_aliases={0: 0},
         compiler_params=PARAMS,
         cost_estimate=pl.CostEstimate(flops=10**9, bytes_accessed=6 * 10**6, transcendentals=0),
         name="mid",
-    )(place, near, other, low, low_other, far_tab, qt, far_factor)
+    )(near, other, low, low_other, far_tab, qt, far_factor)
 
     swapped = send(part, 2, size)
     high = glue(column_kernel, pltpu.VMEM((count, half, state_dim), jnp.bfloat16))(
-        came[0], next_swapped, part, swapped, place=place
+        came[0], next_swapped, part, swapped
     )
     high_other = send(high, 1, size)
 

time: 69.9 us -> 67.1 us (0.960)
  Pallas kernels: 33.8 us -> 31.4 us
  waiting for transfers between devices: 19.1 us -> 18.2 us
    pallas_call x6, Pallas kernels: 6 us -> 3.67 us  [the longest x1 2.97 us: on_device(): pl.pallas_call(functools.partial(mid_kernel, width), grid=(2 * half_steps...]
    ppermute x10, waiting for transfers between devices: 18.2 us -> 17.4 us  [send(): return lax.ppermute(x, 'seq', [(i, i ^ by) for i in range(size)])]
  transfers between devices with their start and end apart: 11 -> 11, of which waited for: 7 -> 7; matrix products, arithmetic and copies ran while one was open for 0% -> 0% of each run, Pallas kernels for 29% -> 28%
where the time goes in v4:
time: 67.1 us; the launch traced here: 66.9 us
  Pallas kernels  31.4 us (47%)
  waiting for transfers between devices  18.2 us (27%)
  starting transfers between devices  17.1 us (25%)
    ppermute x10, waiting for transfers between devices, send(): return lax.ppermute(x, 'seq', [(i, i ^ by) for i in range(size)])  17.4 us
    ppermute x10, starting transfers between devices, send(): return lax.ppermute(x, 'seq', [(i, i ^ by) for i in range(size)])  14.5 us
    pallas_call x3, Pallas kernels, on_device(): pl.pallas_call(functools.partial(near_kernel, sum(calls[:call]), width),...  10.8 us
    pallas_call x2, Pallas kernels, on_device(): pl.pallas_call(functools.partial(far_kernel, width, call), grid_spec=pltp...  7.61 us
    pallas_call x1, Pallas kernels, on_device(): pl.pallas_call(state_kernel, grid=(heads // STEP,), in_specs=[RESIDENT, p...  7.26 us
    pallas_call x1, Pallas kernels, on_device(): pl.pallas_call(functools.partial(mid_kernel, width), grid=(2 * half_steps...  2.97 us
    ppermute x1, starting transfers between devices, on_device(): rims = lax.ppermute(own_rim, 'seq', [(i, i + 1) for i in range(size - 1)])  2.54 us
  transfers between devices with their start and end apart: 11, of which 7 were waited for; matrix products, arithmetic and copies ran while one was open for 0% of the time, Pallas kernels for 28%

profile of v4, /device:TPU:0, one launch (start us, length us, event | category | flops | bytes accessed | tf_op | source)
XLA Modules:
  0.0 66.9 jit_solution(1742834883873333275)
XLA Ops:
  0.0 1.0 %rim.1 = bf16[3,2304]{1,0:T(4,128)(2,1)S(1)} custom-call(bf16[1024,128]{1,0:T(8,128)(2,1)} %q_ref.3, bf16[1024,128]{1,0:T(8,128)(2,1)} %k_ref.3, bf16[1024,2048]{1,0:T(8,128)(2,1)} %v_ref.3), custom_call_target="tpu_custom_call" | custom-call | tf_op jit(solution)/shard_map/rim/pallas_call | solution.py:558
  1.0 0.0 copy-start.5
  1.0 2.5 %collective-permute-start = (bf16[3,2304]{1,0:T(4,128)(2,1)S(1)}, bf16[3,2304]{1,0:T(4,128)(2,1)S(1)}, u32[]{:S(2)}, u32[]{:S(2)}) collective-permute-start(bf16[3,2304]{1,0:T(4,128)(2,1)S(1)} %rim.1), channel_id=1, source_target_pairs={{0,1},{1,2},{2,3},{3,4},{4,5},{5,6},{6,7},{7,8},{8,9},{9,10},{10,1... | collective-permute-start | bytes 41480 | tf_op jit(solution)/shard_map/ppermute | solution.py:570
  3.5 0.8 %collective-permute-done.rim_ref = bf16[3,2304]{1,0:T(4,128)(2,1)S(1)} collective-permute-done((bf16[3,2304]{1,0:T(4,128)(2,1)S(1)}, bf16[3,2304]{1,0:T(4,128)(2,1)S(1)}, u32[]{:S(2)}, u32[]{:S(2)}) %collective-permute-start) | collective-permute-done | bytes 13856 | tf_op jit(solution)/shard_map/ppermute | solution.py:570
  4.4 7.3 %state.1 = (bf16[2048,1024]{1,0:T(8,128)(2,1)S(1)}, bf16[3,2048,128]{2,1,0:T(8,128)(2,1)S(1)}, bf16[2064,128]{1,0:T(8,128)(2,1)S(1)}, bf16[1024,128]{1,0:T(8,128)(2,1)S(1)}) custom-call(bf16[1024,128]{1,0:T(8,128)(2,1)S(1)} %copy-done, bf16[1024,2048]{1,0:T(8,128)(2,1)} %v_ref.3, bf16[3,2304]{1,0:T(4,128)(2,1)S(1)} %collective-permute-done.rim_ref, ...), custom_call_target="tpu_custom_call" | custom-call | flops 1000000000 | bytes 9000000 | tf_op jit(solution)/shard_map/state/pallas_call | solution.py:586
  11.6 0.0 copy-start.1
  11.6 2.7 %collective-permute-start.1 = (bf16[2064,128]{1,0:T(8,128)(2,1)S(1)}, bf16[2064,128]{1,0:T(8,128)(2,1)S(1)}, u32[]{:S(2)}, u32[]{:S(2)}) collective-permute-start(bf16[2064,128]{1,0:T(8,128)(2,1)S(1)} %get-tuple-element.28.own_ref), channel_id=1, source_target_pairs={{0,1},{1,0},{2,3},{3,2},{4,5},{5,4},{6,7},{7,6},{8,9},{9,8},{10,11... | collective-permute-start | bytes 1585160 | tf_op jit(solution)/shard_map/ppermute | solution.py:531
  14.4 1.5 %collective-permute-done.1.other_ref.chip_ref = bf16[2064,128]{1,0:T(8,128)(2,1)S(1)} collective-permute-done((bf16[2064,128]{1,0:T(8,128)(2,1)S(1)}, bf16[2064,128]{1,0:T(8,128)(2,1)S(1)}, u32[]{:S(2)}, u32[]{:S(2)}) %collective-permute-start.1) | collective-permute-done | bytes 528416 | tf_op jit(solution)/shard_map/ppermute | solution.py:531
  15.9 0.2 shard_map.73
  16.1 2.6 %collective-permute-start.3 = (bf16[528,128]{1,0:T(8,128)(2,1)S(1)}, bf16[528,128]{1,0:T(8,128)(2,1)S(1)}, u32[]{:S(2)}, u32[]{:S(2)}) collective-permute-start(bf16[528,128]{1,0:T(8,128)(2,1)S(1)} %get-tuple-element.30), channel_id=1, source_target_pairs={{0,2},{1,3},{2,0},{3,1},{4,6},{5,7},{6,4},{7,5},{8,10},{9,11},{10,... | collective-permute-start | bytes 405512 | tf_op jit(solution)/shard_map/ppermute | solution.py:531
  18.8 3.9 %collective-permute-done.3.last_ref.got_ref = bf16[528,128]{1,0:T(8,128)(2,1)S(1)} collective-permute-done((bf16[528,128]{1,0:T(8,128)(2,1)S(1)}, bf16[528,128]{1,0:T(8,128)(2,1)S(1)}, u32[]{:S(2)}, u32[]{:S(2)}) %collective-permute-start.3) | collective-permute-done | bytes 135200 | tf_op jit(solution)/shard_map/ppermute | solution.py:531
  22.7 0.2 shard_map.75
  22.8 2.8 %collective-permute-start.5 = (bf16[528,128]{1,0:T(8,128)(2,1)S(1)}, bf16[528,128]{1,0:T(8,128)(2,1)S(1)}, u32[]{:S(2)}, u32[]{:S(2)}) collective-permute-start(bf16[528,128]{1,0:T(8,128)(2,1)S(1)} %get-tuple-element.33), channel_id=1, source_target_pairs={{0,4},{1,5},{2,6},{3,7},{4,0},{5,1},{6,2},{7,3},{8,12},{9,13},{10,... | collective-permute-start | bytes 405512 | tf_op jit(solution)/shard_map/ppermute | solution.py:531
  25.6 2.6 %collective-permute-start.6 = (bf16[528,128]{1,0:T(8,128)(2,1)S(1)}, bf16[528,128]{1,0:T(8,128)(2,1)S(1)}, u32[]{:S(2)}, u32[]{:S(2)}) collective-permute-start(bf16[528,128]{1,0:T(8,128)(2,1)S(1)} %get-tuple-element.33), channel_id=1, source_target_pairs={{0,8},{1,9},{2,10},{3,11},{4,12},{5,13},{6,14},{7,15},{8,0},{9,1},... | collective-permute-start | bytes 405512 | tf_op jit(solution)/shard_map/ppermute | solution.py:531
  28.2 1.9 %collective-permute-done.5.refs_0_.next_ref = bf16[528,128]{1,0:T(8,128)(2,1)S(1)} collective-permute-done((bf16[528,128]{1,0:T(8,128)(2,1)S(1)}, bf16[528,128]{1,0:T(8,128)(2,1)S(1)}, u32[]{:S(2)}, u32[]{:S(2)}) %collective-permute-start.5) | collective-permute-done | bytes 135200 | tf_op jit(solution)/shard_map/ppermute | solution.py:531
  30.1 1.2 %collective-permute-start.8 = (bf16[528,128]{1,0:T(8,128)(2,1)S(1)}, bf16[528,128]{1,0:T(8,128)(2,1)S(1)}, u32[]{:S(2)}, u32[]{:S(2)}) collective-permute-start(bf16[528,128]{1,0:T(8,128)(2,1)S(1)} %collective-permute-done.5.refs_0_.next_ref), channel_id=1, source_target_pairs={{0,2},{1,3},{2,0},{3,1},{4,6},{5,7},{6,4},{7,5},{8,10},{9,11},{10,... | collective-permute-start | bytes 405512 | tf_op jit(solution)/shard_map/ppermute | solution.py:531
  31.3 7.0 %collective-permute-done.6.refs_1_ = bf16[528,128]{1,0:T(8,128)(2,1)S(1)} collective-permute-done((bf16[528,128]{1,0:T(8,128)(2,1)S(1)}, bf16[528,128]{1,0:T(8,128)(2,1)S(1)}, u32[]{:S(2)}, u32[]{:S(2)}) %collective-permute-start.6) | collective-permute-done | bytes 135200 | tf_op jit(solution)/shard_map/ppermute | solution.py:531
  38.3 0.2 shard_map.76
  38.5 0.7 %collective-permute-start.9 = (bf16[1,512,128]{2,1,0:T(8,128)(2,1)S(1)}, bf16[1,512,128]{2,1,0:T(8,128)(2,1)S(1)}, u32[]{:S(2)}, u32[]{:S(2)}) collective-permute-start(bf16[1,512,128]{2,1,0:T(8,128)(2,1)S(1)} %get-tuple-element.36.part_ref), channel_id=1, source_target_pairs={{0,2},{1,3},{2,0},{3,1},{4,6},{5,7},{6,4},{7,5},{8,10},{9,11},{10,... | collective-permute-start | bytes 393224 | tf_op jit(solution)/shard_map/ppermute | solution.py:531
  39.2 1.4 %collective-permute-start.2 = (bf16[512,128]{1,0:T(8,128)(2,1)S(1)}, bf16[512,128]{1,0:T(8,128)(2,1)S(1)}, u32[]{:S(2)}, u32[]{:S(2)}) collective-permute-start(bf16[512,128]{1,0:T(8,128)(2,1)S(1)} %get-tuple-element.29.mine_ref), channel_id=1, source_target_pairs={{0,2},{1,3},{2,0},{3,1},{4,6},{5,7},{6,4},{7,5},{8,10},{9,11},{10,... | collective-permute-start | bytes 393224 | tf_op jit(solution)/shard_map/ppermute | solution.py:531
  40.6 2.9 %collective-permute-done.9.swapped_ref = bf16[1,512,128]{2,1,0:T(8,128)(2,1)S(1)} collective-permute-done((bf16[1,512,128]{2,1,0:T(8,128)(2,1)S(1)}, bf16[1,512,128]{2,1,0:T(8,128)(2,1)S(1)}, u32[]{:S(2)}, u32[]{:S(2)}) %collective-permute-start.9) | collective-permute-done | bytes 131104 | tf_op jit(solution)/shard_map/ppermute | solution.py:531
  43.6 0.1 collective-permute-start.10
  43.7 0.6 tables.1
  44.3 0.5 scores.1
  44.9 0.1 collective-permute-done.2.first_ref
  45.0 0.5 collective-permute-start.4
  45.5 4.0 %near.3.vt_ref = bf16[2048,1024]{1,0:T(8,128)(2,1)S(1)} custom-call(bf16[2048,1024]{1,0:T(8,128)(2,1)S(1)} %get-tuple-element.22.vt_ref, bf16[3,2048,128]{2,1,0:T(8,128)(2,1)S(1)} %get-tuple-element.23.st_ref, f32[17,8,16,128]{3,2,1,0:T(8,128)S(1)} %get-tuple-element.24.tab_ref, ...), custom_call_target="tpu_custom_call", output_to_operand_aliasing={{}: (0, {})} | custom-call | flops 1000000000 | bytes 4000000 | tf_op jit(solution)/shard_map/near/pallas_call | solution.py:632
  49.5 2.7 %near.4.vt_ref = bf16[2048,1024]{1,0:T(8,128)(2,1)S(1)} custom-call(bf16[2048,1024]{1,0:T(8,128)(2,1)S(1)} %near.3.vt_ref, bf16[3,2048,128]{2,1,0:T(8,128)(2,1)S(1)} %get-tuple-element.23.st_ref, f32[17,8,16,128]{3,2,1,0:T(8,128)S(1)} %get-tuple-element.24.tab_ref, bf16[4,256,256]{2,1,0:T(8,128)(2,1)S(1)} %get-tuple-element.26.sc, ...), custom_call_target="tpu_custom_call", output_to_operand_aliasing={{}: (0, {})} | custom-call | flops 1000000000 | bytes 4000000 | tf_op jit(solution)/shard_map/near/pallas_call | solution.py:632
  52.2 4.0 %near.5.near_ref = bf16[2048,1024]{1,0:T(8,128)(2,1)S(1)} custom-call(bf16[2048,1024]{1,0:T(8,128)(2,1)S(1)} %near.4.vt_ref, bf16[3,2048,128]{2,1,0:T(8,128)(2,1)S(1)} %get-tuple-element.23.st_ref, f32[17,8,16,128]{3,2,1,0:T(8,128)S(1)} %get-tuple-element.24.tab_ref, bf16[4,256,256]{2,1,0:T(8,128)(2,1)S(1)} %get-tuple-element.26.sc, ...), custom_call_target="tpu_custom_call", output_to_operand_aliasing={{}: (0, {})} | custom-call | flops 1000000000 | bytes 4000000 | tf_op jit(solution)/shard_map/near/pallas_call | solution.py:632
  56.3 3.0 %mid.1.near_ref = bf16[2048,1024]{1,0:T(8,128)(2,1)S(1)} custom-call(bf16[2048,1024]{1,0:T(8,128)(2,1)S(1)} %near.5.near_ref, bf16[2064,128]{1,0:T(8,128)(2,1)S(1)} %collective-permute-done.1.other_ref.chip_ref, bf16[1024,128]{1,0:T(8,128)(2,1)S(1)} %shard_map.74.low_ref, ...), custom_call_target="tpu_custom_call", output_to_operand_aliasing={{}: (0, {})} | custom-call | flops 1000000000 | bytes 6000000 | tf_op jit(solution)/shard_map/mid/pallas_call | solution.py:688
  59.3 3.8 %far.2.refs_0_ = bf16[1024,2048]{1,0:T(8,128)(2,1)} custom-call(s32[3]{0:T(128)S(1)} %get-tuple-element.21.place_ref, bf16[2048,1024]{1,0:T(8,128)(2,1)S(1)} %mid.1.near_ref, bf16[2,1024,128]{2,1,0:T(8,128)(2,1)S(1)} %shard_map.77.high_ref, f32[4,8,16,128]{3,2,1,0:T(8,128)S(1)} %get-tuple-element.31.far_ref, bf16[128,1024]{1,0:T(8,128)(2,1)S(1)} %get-tuple-element.27.qt_ref, ...), custom_call_target="tpu_custom_call" | custom-call | flops 1000000000 | bytes 6000000 | tf_op jit(solution)/shard_map/far/pallas_call | solution.py:714
  63.1 3.8 %far.3 = bf16[1024,2048]{1,0:T(8,128)(2,1)} custom-call(s32[3]{0:T(128)S(1)} %get-tuple-element.21.place_ref, bf16[2048,1024]{1,0:T(8,128)(2,1)S(1)} %mid.1.near_ref, bf16[2,1024,128]{2,1,0:T(8,128)(2,1)S(1)} %collective-permute-done.10.high_ref, f32[4,8,16,128]{3,2,1,0:T(8,128)S(1)} %get-tuple-element.31.far_ref, ...), custom_call_target="tpu_custom_call", output_to_operand_aliasing={{}: (7, {})} | custom-call | flops 1000000000 | bytes 6000000 | tf_op jit(solution)/shard_map/far/pallas_call | solution.py:714
  (17 shorter events, 0.1 us)
Async XLA Ops:
  0.0 4.4 %copy-start = (bf16[1024,128]{1,0:T(8,128)(2,1)S(1)}, bf16[1024,128]{1,0:T(8,128)(2,1)}, u32[]{:S(2)}) copy-start(bf16[1024,128]{1,0:T(8,128)(2,1)} %k_ref.3) | copy-start | bytes 786436
  0.0 4.4 %copy-start.3 = (f32[16,1024]{1,0:T(8,128)S(1)}, f32[16,1024]{1,0:T(8,128)}, u32[]{:S(2)}) copy-start(f32[16,1024]{1,0:T(8,128)} %ld_ref.3) | copy-start | bytes 196612
  0.0 4.4 %copy-start.2 = (f32[4,2304]{1,0:T(4,128)S(1)}, f32[4,2304]{1,0:T(4,128)}, u32[]{:S(2)}) copy-start(f32[4,2304]{1,0:T(4,128)} %w_ref.1) | copy-start | bytes 110596
  1.0 42.7 %copy-start.5 = (bf16[15,16,1024]{2,1,0:T(8,128)(2,1)S(1)}, bf16[15,16,1024]{2,1,0:T(8,128)(2,1)}, u32[]{:S(2)}) copy-start(bf16[15,16,1024]{2,1,0:T(8,128)(2,1)} %lw_ref.1) | copy-start | bytes 1474564
  1.0 3.4 %collective-permute-start = (bf16[3,2304]{1,0:T(4,128)(2,1)S(1)}, bf16[3,2304]{1,0:T(4,128)(2,1)S(1)}, u32[]{:S(2)}, u32[]{:S(2)}) collective-permute-start(bf16[3,2304]{1,0:T(4,128)(2,1)S(1)} %rim.1), channel_id=1, source_target_pairs={{0,1},{1,2},{2,3},{3,4},{4,5},{5,6},{6,7},{7,8},{8,9},{9,10},{10,1... | collective-permute-start | bytes 41480 | tf_op jit(solution)/shard_map/ppermute | solution.py:570
  11.6 32.7 %copy-start.1 = (bf16[1024,128]{1,0:T(8,128)(2,1)S(1)}, bf16[1024,128]{1,0:T(8,128)(2,1)}, u32[]{:S(2)}) copy-start(bf16[1024,128]{1,0:T(8,128)(2,1)} %q_ref.3) | copy-start | bytes 786436
  11.6 4.3 %collective-permute-start.1 = (bf16[2064,128]{1,0:T(8,128)(2,1)S(1)}, bf16[2064,128]{1,0:T(8,128)(2,1)S(1)}, u32[]{:S(2)}, u32[]{:S(2)}) collective-permute-start(bf16[2064,128]{1,0:T(8,128)(2,1)S(1)} %get-tuple-element.28.own_ref), channel_id=1, source_target_pairs={{0,1},{1,0},{2,3},{3,2},{4,5},{5,4},{6,7},{7,6},{8,9},{9,8},{10,11... | collective-permute-start | bytes 1585160 | tf_op jit(solution)/shard_map/ppermute | solution.py:531
  16.1 6.5 %collective-permute-start.3 = (bf16[528,128]{1,0:T(8,128)(2,1)S(1)}, bf16[528,128]{1,0:T(8,128)(2,1)S(1)}, u32[]{:S(2)}, u32[]{:S(2)}) collective-permute-start(bf16[528,128]{1,0:T(8,128)(2,1)S(1)} %get-tuple-element.30), channel_id=1, source_target_pairs={{0,2},{1,3},{2,0},{3,1},{4,6},{5,7},{6,4},{7,5},{8,10},{9,11},{10,... | collective-permute-start | bytes 405512 | tf_op jit(solution)/shard_map/ppermute | solution.py:531
  22.8 7.2 %collective-permute-start.5 = (bf16[528,128]{1,0:T(8,128)(2,1)S(1)}, bf16[528,128]{1,0:T(8,128)(2,1)S(1)}, u32[]{:S(2)}, u32[]{:S(2)}) collective-permute-start(bf16[528,128]{1,0:T(8,128)(2,1)S(1)} %get-tuple-element.33), channel_id=1, source_target_pairs={{0,4},{1,5},{2,6},{3,7},{4,0},{5,1},{6,2},{7,3},{8,12},{9,13},{10,... | collective-permute-start | bytes 405512 | tf_op jit(solution)/shard_map/ppermute | solution.py:531
  25.6 12.7 %collective-permute-start.6 = (bf16[528,128]{1,0:T(8,128)(2,1)S(1)}, bf16[528,128]{1,0:T(8,128)(2,1)S(1)}, u32[]{:S(2)}, u32[]{:S(2)}) collective-permute-start(bf16[528,128]{1,0:T(8,128)(2,1)S(1)} %get-tuple-element.33), channel_id=1, source_target_pairs={{0,8},{1,9},{2,10},{3,11},{4,12},{5,13},{6,14},{7,15},{8,0},{9,1},... | collective-permute-start | bytes 405512 | tf_op jit(solution)/shard_map/ppermute | solution.py:531
  28.2 10.1 %collective-permute-start.7 = (bf16[528,128]{1,0:T(8,128)(2,1)S(1)}, bf16[528,128]{1,0:T(8,128)(2,1)S(1)}, u32[]{:S(2)}, u32[]{:S(2)}) collective-permute-start(bf16[528,128]{1,0:T(8,128)(2,1)S(1)} %get-tuple-element.33), channel_id=1, source_target_pairs={{0,12},{1,13},{2,14},{3,15},{4,8},{5,9},{6,10},{7,11},{8,4},{9,5},... | collective-permute-start | bytes 405512 | tf_op jit(solution)/shard_map/ppermute | solution.py:531
  30.1 13.5 %collective-permute-start.8 = (bf16[528,128]{1,0:T(8,128)(2,1)S(1)}, bf16[528,128]{1,0:T(8,128)(2,1)S(1)}, u32[]{:S(2)}, u32[]{:S(2)}) collective-permute-start(bf16[528,128]{1,0:T(8,128)(2,1)S(1)} %collective-permute-done.5.refs_0_.next_ref), channel_id=1, source_target_pairs={{0,2},{1,3},{2,0},{3,1},{4,6},{5,7},{6,4},{7,5},{8,10},{9,11},{10,... | collective-permute-start | bytes 405512 | tf_op jit(solution)/shard_map/ppermute | solution.py:531
  38.5 5.0 %collective-permute-start.9 = (bf16[1,512,128]{2,1,0:T(8,128)(2,1)S(1)}, bf16[1,512,128]{2,1,0:T(8,128)(2,1)S(1)}, u32[]{:S(2)}, u32[]{:S(2)}) collective-permute-start(bf16[1,512,128]{2,1,0:T(8,128)(2,1)S(1)} %get-tuple-element.36.part_ref), channel_id=1, source_target_pairs={{0,2},{1,3},{2,0},{3,1},{4,6},{5,7},{6,4},{7,5},{8,10},{9,11},{10,... | collective-permute-start | bytes 393224 | tf_op jit(solution)/shard_map/ppermute | solution.py:531
  39.2 5.8 %collective-permute-start.2 = (bf16[512,128]{1,0:T(8,128)(2,1)S(1)}, bf16[512,128]{1,0:T(8,128)(2,1)S(1)}, u32[]{:S(2)}, u32[]{:S(2)}) collective-permute-start(bf16[512,128]{1,0:T(8,128)(2,1)S(1)} %get-tuple-element.29.mine_ref), channel_id=1, source_target_pairs={{0,2},{1,3},{2,0},{3,1},{4,6},{5,7},{6,4},{7,5},{8,10},{9,11},{10,... | collective-permute-start | bytes 393224 | tf_op jit(solution)/shard_map/ppermute | solution.py:531
  43.6 19.5 %collective-permute-start.10 = (bf16[2,1024,128]{2,1,0:T(8,128)(2,1)S(1)}, bf16[2,1024,128]{2,1,0:T(8,128)(2,1)S(1)}, u32[]{:S(2)}, u32[]{:S(2)}) collective-permute-start(bf16[2,1024,128]{2,1,0:T(8,128)(2,1)S(1)} %shard_map.77.high_ref), channel_id=1, source_target_pairs={{0,1},{1,0},{2,3},{3,2},{4,5},{5,4},{6,7},{7,6},{8,9},{9,8},{10,11... | collective-permute-start | bytes 1572872 | tf_op jit(solution)/shard_map/ppermute | solution.py:531
  45.0 11.3 %collective-permute-start.4 = (bf16[1024,128]{1,0:T(8,128)(2,1)S(1)}, bf16[1024,128]{1,0:T(8,128)(2,1)S(1)}, u32[]{:S(2)}, u32[]{:S(2)}) collective-permute-start(bf16[1024,128]{1,0:T(8,128)(2,1)S(1)} %shard_map.74.low_ref), channel_id=1, source_target_pairs={{0,1},{1,0},{2,3},{3,2},{4,5},{5,4},{6,7},{7,6},{8,9},{9,8},{10,11... | collective-permute-start | bytes 786440 | tf_op jit(solution)/shard_map/ppermute | solution.py:531
  56.3 3.0 %copy-start.4 = (f32[2048]{0:T(1024)S(1)}, f32[2048]{0:T(1024)}, u32[]{:S(2)}) copy-start(f32[2048]{0:T(1024)} %param.13) | copy-start | bytes 24580

commit v5 on v4

--- a/solution.py
+++ b/solution.py
@@ -97,46 +97,31 @@
 
 
 def state_kernel(
-    k_ref, v_ref, rim_ref, wk_ref, wv_ref, ld_ref,
-    vt_ref, st_ref, g_ref, kc_ref,
-    buf, scale, total, values, sems,
+    k_ref, v_ref, rim_ref, wk_ref, wv_ref, scale, total, terms_ref, _, _early,
+    vt_ref, st_ref, g_ref, kc_ref, values,
+    buf, sems,
 ):
     step = pl.program_id(0)
-    heads = ld_ref.shape[0]
+    heads = scale.shape[1]
     length = v_ref.shape[0]
     width = v_ref.shape[1] // heads
     state_dim = k_ref.shape[1]
     pairs = length // (2 * TILE)
     steps = heads // STEP
 
-    def fetch(order):
-        lanes = slice(order * STEP * width, (order + 1) * STEP * width)
-        return pltpu.make_async_copy(v_ref.at[:, lanes], values.at[order], sems.at[order])
-
     @pl.when(step == 0)
     def _():
-        for order in range(steps):
-            fetch(order).start()
-        local, _, totals = tile_decays(ld_ref[...])
-        summed = None
-        for pair in range(pairs):
-            low, high = 2 * pair, 2 * pair + 1
-            scale[low] = jnp.exp(totals[low] - local[low] + totals[high])
-            scale[high] = jnp.exp(totals[high] - local[high])
-            both = totals[low] + totals[high]
-            total[pair] = jnp.exp(both)
-            summed = both if summed is None else summed + both
-        g_ref[pl.ds(heads * width, heads), :] = three_terms(summed)
-        fill(buf.at[0], k_ref, rim_ref.at[:, state_dim : 2 * state_dim])
-        for tile in range(length // TILE):
-            at = tile * TILE
-            kc_ref[at : at + TILE, :] = conv_tile(buf.at[0], 0.5 * wk_ref[...], at).astype(jnp.bfloat16)
-
-    for order in range(steps):
+        for order in range(steps // 2, steps):
+            fetch(v_ref, values, sems, order).start()
+        g_ref[pl.ds(heads * width, heads), :] = terms_ref[...]
+        fill(buf.at[0], k_ref.at[0:TILE, :], rim_ref.at[:, state_dim : 2 * state_dim])
+        kc_ref[0:TILE, :] = conv_tile(buf.at[0], 0.5 * wk_ref[...], 0).astype(jnp.bfloat16)
+
+    for order in range(steps // 2, steps):
 
         @pl.when(step == order)
         def _(order=order):
-            fetch(order).wait()
+            fetch(v_ref, values, sems, order).wait()
 
     for place in range(STEP):
         lanes = slice(place * width, (place + 1) * width)
@@ -187,11 +172,19 @@
     }
 
 
-def table_kernel(ld_ref, lw_ref, tab_ref, far_ref, place_ref):
-    index = lax.axis_index("seq")
-    place_ref[0] = index & 1
-    place_ref[1] = index >> 1 & 1
-    place_ref[2] = index >> 2
+def fetch(v_ref, values, sems, order):
+    lanes = slice(order * values.shape[2], (order + 1) * values.shape[2])
+    return pltpu.make_async_copy(v_ref.at[:, lanes], values.at[order], sems.at[order])
+
+
+def table_kernel(
+    ld_ref, lw_ref, k_ref, wk_ref, v_ref,
+    tab_ref, far_ref, scale_ref, total_ref, terms_ref, kc_ref, values,
+    buf, sems,
+):
+    early = values.shape[0] // 2
+    for order in range(early):
+        fetch(v_ref, values, sems, order).start()
     heads, length = ld_ref.shape
     levels = lw_ref.shape[0]
     pairs = length // (2 * TILE)
@@ -199,6 +192,16 @@
     inner = log2(GROUP) + 1
     tile_level = log2(TILE)
     locals_, middles, totals = tile_decays(ld_ref[...])
+    for pair in range(pairs):
+        low, high = 2 * pair, 2 * pair + 1
+        scale_ref[low] = jnp.exp(totals[low] - locals_[low] + totals[high])
+        scale_ref[high] = jnp.exp(totals[high] - locals_[high])
+        total_ref[pair] = jnp.exp(totals[low] + totals[high])
+    state_dim = k_ref.shape[1]
+    weight = 0.5 * wk_ref[:, state_dim : 2 * state_dim]
+    buf[pl.ds(8, length), :] = k_ref[...].astype(jnp.float32)
+    for at in range(TILE, length, TILE):
+        kc_ref[at : at + TILE, :] = conv_tile(buf, weight, at).astype(jnp.bfloat16)
     block = lax.broadcasted_iota(jnp.int32, (heads, TILE), 1) // GROUP
     zero = jnp.zeros((heads, TILE), jnp.float32)
     pair_total = []
@@ -242,6 +245,9 @@
                 far_ref[level - first, tile] = weight[level] * whole_decay
         pair_total.append(totals[low] + totals[low + 1])
         running = running + pair_total[-1]
+    terms_ref[...] = three_terms(running)
+    for order in range(early):
+        fetch(v_ref, values, sems, order).wait()
 
 
 def rim_kernel(q_ref, k_ref, v_ref, out_ref, last, sems):
@@ -382,12 +388,12 @@
         )
 
 
-def far_kernel(width, other, place_ref, near_ref, high_ref, far_ref, qt_ref, off_ref, gain_ref, *refs):
+def far_kernel(width, other, near_ref, high_ref, far_ref, qt_ref, off_ref, gain_ref, *refs):
     out_ref, rest = refs[-2:]
     count = high_ref.shape[0]
     for place in range(STEP):
         own = slice(place * width, (place + 1) * width)
-        core = 1 - place_ref[0] if other else place_ref[0]
+        core = 1 - position()[0] if other else position()[0]
         head = (core * pl.num_programs(0) + pl.program_id(0)) * STEP + place
         gain = jnp.broadcast_to(gain_ref[:, own], (TILE, TILE)).T
 
@@ -569,21 +575,29 @@
     )(query_inputs, key_inputs, value_inputs)
     rims = lax.ppermute(own_rim, "seq", [(i, i + 1) for i in range(size - 1)])
 
-    tab, far_tab, place = pl.pallas_call(
+    tab, far_tab, scale, total, terms, kc, values = pl.pallas_call(
         table_kernel,
-        in_specs=[RESIDENT] * 2,
-        out_specs=[RESIDENT] * 2 + [pl.BlockSpec(memory_space=pltpu.SMEM)],
+        in_specs=[RESIDENT] * 4 + [pl.BlockSpec(memory_space=pl.ANY)],
+        out_specs=[RESIDENT] * 7,
         out_shape=[
             pltpu.VMEM((rows["size"], length // TILE, heads, TILE), jnp.float32),
             pltpu.VMEM((bits, length // TILE, heads, TILE), jnp.float32),
-            shape_of((3,), jnp.int32),
+            pltpu.VMEM((length // TILE, heads, TILE), jnp.float32),
+            pltpu.VMEM((pairs, heads, TILE), jnp.float32),
+            pltpu.VMEM((heads, TILE), jnp.bfloat16),
+            pltpu.VMEM((length, state_dim), jnp.bfloat16),
+            pltpu.VMEM((heads // STEP, length, STEP * width), jnp.bfloat16),
+        ],
+        scratch_shapes=[
+            pltpu.VMEM((length + 8, TILE), jnp.float32),
+            pltpu.SemaphoreType.DMA((heads // STEP,)),
         ],
         compiler_params=PARAMS,
         cost_estimate=pl.CostEstimate(flops=10**9, bytes_accessed=3 * 10**6, transcendentals=0),
         name="tables",
-    )(log_decay, level_weight)
-
-    vt, st, group, kc = pl.pallas_call(
+    )(log_decay, level_weight, key_inputs, conv_weight, value_inputs)
+
+    vt, st, group, kc, _ = pl.pallas_call(
         state_kernel,
         grid=(heads // STEP,),
         in_specs=[
@@ -593,25 +607,28 @@
             pl.BlockSpec((taps, state_dim), lambda i: (0, 1)),
             pl.BlockSpec((taps, STEP * width), lambda i: (0, 2 * state_dim // (STEP * width) + i)),
             RESIDENT,
-        ],
-        out_specs=[RESIDENT] * 4,
+            RESIDENT,
+            RESIDENT,
+            RESIDENT,
+            RESIDENT,
+        ],
+        input_output_aliases={8: 3, 9: 4},
+        out_specs=[RESIDENT] * 5,
         out_shape=[
             pltpu.VMEM((values_dim, length), jnp.bfloat16),
             pltpu.VMEM((len(keys), values_dim, state_dim), jnp.bfloat16),
             pltpu.VMEM((values_dim + tail, state_dim), jnp.bfloat16),
             pltpu.VMEM((length, state_dim), jnp.bfloat16),
+            pltpu.VMEM((heads // STEP, length, STEP * width), jnp.bfloat16),
         ],
         scratch_shapes=[
             pltpu.VMEM((STEP, length + 8, TILE), jnp.float32),
-            pltpu.VMEM((length // TILE, heads, TILE), jnp.float32),
-            pltpu.VMEM((pairs, heads, TILE), jnp.float32),
-            pltpu.VMEM((heads // STEP, length, STEP * width), jnp.bfloat16),
             pltpu.SemaphoreType.DMA((heads // STEP,)),
         ],
         compiler_params=PARAMS,
         cost_estimate=pl.CostEstimate(flops=10**9, bytes_accessed=9 * 10**6, transcendentals=0),
         name="state",
-    )(key_inputs, value_inputs, rims, conv_weight, conv_weight, log_decay)
+    )(key_inputs, value_inputs, rims, conv_weight, conv_weight, scale, total, terms, kc, values)
 
     qt, sc = pl.pallas_call(
         score_kernel,
@@ -708,32 +725,30 @@
     for call, states in enumerate((high, high_other)):
         before = [] if out is None else [out]
 
-        def columns(i, s, other=call):
-            return (0, (1 - s[0] if other else s[0]) * half_steps + i)
+        def columns(i, other=call):
+            core = position()[0]
+            return (0, (1 - core if other else core) * half_steps + i)
 
         out = pl.pallas_call(
             functools.partial(far_kernel, width, call),
-            grid_spec=pltpu.PrefetchScalarGridSpec(
-                num_scalar_prefetch=1,
-                grid=(half_steps,),
-                in_specs=[
-                    RESIDENT,
-                    pl.BlockSpec((count, STEP * width, state_dim), lambda i, s: (0, i, 0)),
-                    RESIDENT,
-                    RESIDENT,
-                    RESIDENT,
-                    pl.BlockSpec((1, STEP * width), columns),
-                ]
-                + [pl.BlockSpec(memory_space=pl.ANY) for _ in before],
-                out_specs=pl.BlockSpec((length, STEP * width), columns),
-                scratch_shapes=[pltpu.VMEM((STEP, pairs, count * state_dim, 2 * TILE), jnp.bfloat16)],
-            ),
+            grid=(half_steps,),
+            in_specs=[
+                RESIDENT,
+                pl.BlockSpec((count, STEP * width, state_dim), lambda i: (0, i, 0)),
+                RESIDENT,
+                RESIDENT,
+                RESIDENT,
+                pl.BlockSpec((1, STEP * width), columns),
+            ]
+            + [pl.BlockSpec(memory_space=pl.ANY) for _ in before],
+            out_specs=pl.BlockSpec((length, STEP * width), columns),
+            scratch_shapes=[pltpu.VMEM((STEP, pairs, count * state_dim, 2 * TILE), jnp.bfloat16)],
             out_shape=shape_of((length, values_dim), jnp.bfloat16),
-            input_output_aliases={7: 0} if before else {},
+            input_output_aliases={6: 0} if before else {},
             compiler_params=PARAMS,
             cost_estimate=pl.CostEstimate(flops=10**9, bytes_accessed=6 * 10**6, transcendentals=0),
             name="far",
-        )(place, near, states, far_tab, qt, far_factor, gain, *before)
+        )(near, states, far_tab, qt, far_factor, gain, *before)
     return out
 
 

time: 67.1 us -> 66.4 us (0.990)
  waiting for transfers between devices: 18.2 us -> 20.9 us
  starting transfers between devices: 17.1 us -> 14.8 us
  Pallas kernels: 31.4 us -> 30.3 us
    ppermute x10, waiting for transfers between devices: 17.4 us -> 20.9 us  [send(): return lax.ppermute(x, 'seq', [(i, i ^ by) for i in range(size)])]
    ppermute x10, starting transfers between devices: 14.5 us -> 12.4 us  [send(): return lax.ppermute(x, 'seq', [(i, i ^ by) for i in range(size)])]
    pallas_call x1, Pallas kernels: 7.26 us -> 6.29 us  [on_device(): pl.pallas_call(state_kernel, grid=(heads // STEP,), in_specs=[RESIDENT, p...]
    ppermute x1, waiting for transfers between devices: 0.82 us -> 0.01 us  [on_device(): rims = lax.ppermute(own_rim, 'seq', [(i, i + 1) for i in range(size - 1)])]
  transfers between devices with their start and end apart: 11 -> 11, of which waited for: 7 -> 7; matrix products, arithmetic and copies ran while one was open for 0% -> 0% of each run, Pallas kernels for 28% -> 29%
where the time goes in v5:
time: 66.4 us; the launch traced here: 66.3 us
  Pallas kernels  30.3 us (46%)
  waiting for transfers between devices  20.9 us (31%)
  starting transfers between devices  14.8 us (22%)
    ppermute x10, waiting for transfers between devices, send(): return lax.ppermute(x, 'seq', [(i, i ^ by) for i in range(size)])  20.9 us
    ppermute x10, starting transfers between devices, send(): return lax.ppermute(x, 'seq', [(i, i ^ by) for i in range(size)])  12.4 us
    pallas_call x3, Pallas kernels, on_device(): pl.pallas_call(functools.partial(near_kernel, sum(calls[:call]), width),...  10.7 us
    pallas_call x2, Pallas kernels, on_device(): pl.pallas_call(functools.partial(far_kernel, width, call), grid=(half_ste...  6.54 us
    pallas_call x1, Pallas kernels, on_device(): pl.pallas_call(state_kernel, grid=(heads // STEP,), in_specs=[RESIDENT, p...  6.29 us
    pallas_call x1, Pallas kernels, on_device(): pl.pallas_call(functools.partial(mid_kernel, width), grid=(2 * half_steps...  2.95 us
    ppermute x1, starting transfers between devices, on_device(): rims = lax.ppermute(own_rim, 'seq', [(i, i + 1) for i in range(size - 1)])  2.41 us
    pallas_call x1, Pallas kernels, on_device(): pl.pallas_call(table_kernel, in_specs=[RESIDENT] * 4 + [pl.BlockSpec(memo...  1.62 us
  transfers between devices with their start and end apart: 11, of which 7 were waited for; matrix products, arithmetic and copies ran while one was open for 0% of the time, Pallas kernels for 29%

profile of v5, /device:TPU:0, one launch (start us, length us, event | category | flops | bytes accessed | tf_op | source)
XLA Modules:
  0.0 66.3 jit_solution(14508521015110953869)
XLA Ops:
  0.0 1.0 %rim.1 = bf16[3,2304]{1,0:T(4,128)(2,1)S(1)} custom-call(bf16[1024,128]{1,0:T(8,128)(2,1)} %q_ref.3, bf16[1024,128]{1,0:T(8,128)(2,1)} %k_ref.5, bf16[1024,2048]{1,0:T(8,128)(2,1)} %v_ref.5), custom_call_target="tpu_custom_call" | custom-call | tf_op jit(solution)/shard_map/rim/pallas_call | solution.py:564
  1.0 2.4 %collective-permute-start = (bf16[3,2304]{1,0:T(4,128)(2,1)S(1)}, bf16[3,2304]{1,0:T(4,128)(2,1)S(1)}, u32[]{:S(2)}, u32[]{:S(2)}) collective-permute-start(bf16[3,2304]{1,0:T(4,128)(2,1)S(1)} %rim.1), channel_id=1, source_target_pairs={{0,1},{1,2},{2,3},{3,4},{4,5},{5,6},{6,7},{7,8},{8,9},{9,10},{10,1... | collective-permute-start | bytes 41480 | tf_op jit(solution)/shard_map/ppermute | solution.py:576
  3.5 1.6 %tables.1 = (f32[17,8,16,128]{3,2,1,0:T(8,128)S(1)}, f32[4,8,16,128]{3,2,1,0:T(8,128)S(1)}, f32[8,16,128]{2,1,0:T(8,128)S(1)}, f32[4,16,128]{2,1,0:T(8,128)S(1)}...) custom-call(f32[16,1024]{1,0:T(8,128)S(1)} %copy-done.4, ...), custom_call_target="tpu_custom_call" | custom-call | flops 1000000000 | bytes 3000000 | tf_op jit(solution)/shard_map/tables/pallas_call | solution.py:578
  5.1 0.0 copy-start.1
  5.1 6.3 %state.1 = (bf16[2048,1024]{1,0:T(8,128)(2,1)S(1)}, bf16[3,2048,128]{2,1,0:T(8,128)(2,1)S(1)}, bf16[2064,128]{1,0:T(8,128)(2,1)S(1)}, bf16[1024,128]{1,0:T(8,128)(2,1)S(1)}, bf16[8,1024,256]{2,1,0:T(8,128)(2,1)S(1)}) custom-call(bf16[1024,128]{1,0:T(8,128)(2,1)S(1)} %copy-done, ...), custom_call_target="tpu_custom_call", output_to_operand_aliasing={{3}: (8, {}), {4}: (9, {})} | custom-call | flops 1000000000 | bytes 9000000 | tf_op jit(solution)/shard_map/state/pallas_call | solution.py:600
  11.4 2.7 %collective-permute-start.1 = (bf16[2064,128]{1,0:T(8,128)(2,1)S(1)}, bf16[2064,128]{1,0:T(8,128)(2,1)S(1)}, u32[]{:S(2)}, u32[]{:S(2)}) collective-permute-start(bf16[2064,128]{1,0:T(8,128)(2,1)S(1)} %get-tuple-element.36.own_ref), channel_id=1, source_target_pairs={{0,1},{1,0},{2,3},{3,2},{4,5},{5,4},{6,7},{7,6},{8,9},{9,8},{10,11... | collective-permute-start | bytes 1585160 | tf_op jit(solution)/shard_map/ppermute | solution.py:537
  14.1 1.5 %collective-permute-done.1.other_ref.chip_ref = bf16[2064,128]{1,0:T(8,128)(2,1)S(1)} collective-permute-done((bf16[2064,128]{1,0:T(8,128)(2,1)S(1)}, bf16[2064,128]{1,0:T(8,128)(2,1)S(1)}, u32[]{:S(2)}, u32[]{:S(2)}) %collective-permute-start.1) | collective-permute-done | bytes 528416 | tf_op jit(solution)/shard_map/ppermute | solution.py:537
  15.6 0.2 shard_map.73
  15.9 1.8 %collective-permute-start.3 = (bf16[528,128]{1,0:T(8,128)(2,1)S(1)}, bf16[528,128]{1,0:T(8,128)(2,1)S(1)}, u32[]{:S(2)}, u32[]{:S(2)}) collective-permute-start(bf16[528,128]{1,0:T(8,128)(2,1)S(1)} %get-tuple-element.38), channel_id=1, source_target_pairs={{0,2},{1,3},{2,0},{3,1},{4,6},{5,7},{6,4},{7,5},{8,10},{9,11},{10,... | collective-permute-start | bytes 405512 | tf_op jit(solution)/shard_map/ppermute | solution.py:537
  17.6 4.2 %collective-permute-done.3.last_ref.got_ref = bf16[528,128]{1,0:T(8,128)(2,1)S(1)} collective-permute-done((bf16[528,128]{1,0:T(8,128)(2,1)S(1)}, bf16[528,128]{1,0:T(8,128)(2,1)S(1)}, u32[]{:S(2)}, u32[]{:S(2)}) %collective-permute-start.3) | collective-permute-done | bytes 135200 | tf_op jit(solution)/shard_map/ppermute | solution.py:537
  21.8 0.2 shard_map.75
  22.0 2.5 %collective-permute-start.5 = (bf16[528,128]{1,0:T(8,128)(2,1)S(1)}, bf16[528,128]{1,0:T(8,128)(2,1)S(1)}, u32[]{:S(2)}, u32[]{:S(2)}) collective-permute-start(bf16[528,128]{1,0:T(8,128)(2,1)S(1)} %get-tuple-element.41), channel_id=1, source_target_pairs={{0,4},{1,5},{2,6},{3,7},{4,0},{5,1},{6,2},{7,3},{8,12},{9,13},{10,... | collective-permute-start | bytes 405512 | tf_op jit(solution)/shard_map/ppermute | solution.py:537
  24.5 2.5 %collective-permute-start.7 = (bf16[528,128]{1,0:T(8,128)(2,1)S(1)}, bf16[528,128]{1,0:T(8,128)(2,1)S(1)}, u32[]{:S(2)}, u32[]{:S(2)}) collective-permute-start(bf16[528,128]{1,0:T(8,128)(2,1)S(1)} %get-tuple-element.41), channel_id=1, source_target_pairs={{0,12},{1,13},{2,14},{3,15},{4,8},{5,9},{6,10},{7,11},{8,4},{9,5},... | collective-permute-start | bytes 405512 | tf_op jit(solution)/shard_map/ppermute | solution.py:537
  26.9 0.1 collective-permute-start.6
  27.1 0.9 %collective-permute-done.5.refs_0_.next_ref = bf16[528,128]{1,0:T(8,128)(2,1)S(1)} collective-permute-done((bf16[528,128]{1,0:T(8,128)(2,1)S(1)}, bf16[528,128]{1,0:T(8,128)(2,1)S(1)}, u32[]{:S(2)}, u32[]{:S(2)}) %collective-permute-start.5) | collective-permute-done | bytes 135200 | tf_op jit(solution)/shard_map/ppermute | solution.py:537
  27.9 0.6 collective-permute-start.8
  28.6 5.5 %collective-permute-done.7.refs_2_ = bf16[528,128]{1,0:T(8,128)(2,1)S(1)} collective-permute-done((bf16[528,128]{1,0:T(8,128)(2,1)S(1)}, bf16[528,128]{1,0:T(8,128)(2,1)S(1)}, u32[]{:S(2)}, u32[]{:S(2)}) %collective-permute-start.7) | collective-permute-done | bytes 135200 | tf_op jit(solution)/shard_map/ppermute | solution.py:537
  34.0 4.5 %collective-permute-done.6.refs_1_ = bf16[528,128]{1,0:T(8,128)(2,1)S(1)} collective-permute-done((bf16[528,128]{1,0:T(8,128)(2,1)S(1)}, bf16[528,128]{1,0:T(8,128)(2,1)S(1)}, u32[]{:S(2)}, u32[]{:S(2)}) %collective-permute-start.6) | collective-permute-done | bytes 135200 | tf_op jit(solution)/shard_map/ppermute | solution.py:537
  38.5 0.2 shard_map.76
  38.7 0.7 %collective-permute-start.9 = (bf16[1,512,128]{2,1,0:T(8,128)(2,1)S(1)}, bf16[1,512,128]{2,1,0:T(8,128)(2,1)S(1)}, u32[]{:S(2)}, u32[]{:S(2)}) collective-permute-start(bf16[1,512,128]{2,1,0:T(8,128)(2,1)S(1)} %get-tuple-element.44.part_ref), channel_id=1, source_target_pairs={{0,2},{1,3},{2,0},{3,1},{4,6},{5,7},{6,4},{7,5},{8,10},{9,11},{10,... | collective-permute-start | bytes 393224 | tf_op jit(solution)/shard_map/ppermute | solution.py:537
  39.4 1.4 %collective-permute-start.2 = (bf16[512,128]{1,0:T(8,128)(2,1)S(1)}, bf16[512,128]{1,0:T(8,128)(2,1)S(1)}, u32[]{:S(2)}, u32[]{:S(2)}) collective-permute-start(bf16[512,128]{1,0:T(8,128)(2,1)S(1)} %get-tuple-element.37.mine_ref), channel_id=1, source_target_pairs={{0,2},{1,3},{2,0},{3,1},{4,6},{5,7},{6,4},{7,5},{8,10},{9,11},{10,... | collective-permute-start | bytes 393224 | tf_op jit(solution)/shard_map/ppermute | solution.py:537
  40.8 3.7 %collective-permute-done.9.swapped_ref = bf16[1,512,128]{2,1,0:T(8,128)(2,1)S(1)} collective-permute-done((bf16[1,512,128]{2,1,0:T(8,128)(2,1)S(1)}, bf16[1,512,128]{2,1,0:T(8,128)(2,1)S(1)}, u32[]{:S(2)}, u32[]{:S(2)}) %collective-permute-start.9) | collective-permute-done | bytes 131104 | tf_op jit(solution)/shard_map/ppermute | solution.py:537
  44.5 0.1 collective-permute-start.10
  44.6 0.5 scores.1
  45.2 0.7 %collective-permute-done.2.first_ref = bf16[512,128]{1,0:T(8,128)(2,1)S(1)} collective-permute-done((bf16[512,128]{1,0:T(8,128)(2,1)S(1)}, bf16[512,128]{1,0:T(8,128)(2,1)S(1)}, u32[]{:S(2)}, u32[]{:S(2)}) %collective-permute-start.2) | collective-permute-done | bytes 131104 | tf_op jit(solution)/shard_map/ppermute | solution.py:537
  45.9 0.1 collective-permute-start.4
  46.0 4.0 %near.3.vt_ref = bf16[2048,1024]{1,0:T(8,128)(2,1)S(1)} custom-call(bf16[2048,1024]{1,0:T(8,128)(2,1)S(1)} %get-tuple-element.30.vt_ref, bf16[3,2048,128]{2,1,0:T(8,128)(2,1)S(1)} %get-tuple-element.31.st_ref, f32[17,8,16,128]{3,2,1,0:T(8,128)S(1)} %get-tuple-element.32.tab_ref, ...), custom_call_target="tpu_custom_call", output_to_operand_aliasing={{}: (0, {})} | custom-call | flops 1000000000 | bytes 4000000 | tf_op jit(solution)/shard_map/near/pallas_call | solution.py:649
  50.0 2.7 %near.4.vt_ref = bf16[2048,1024]{1,0:T(8,128)(2,1)S(1)} custom-call(bf16[2048,1024]{1,0:T(8,128)(2,1)S(1)} %near.3.vt_ref, bf16[3,2048,128]{2,1,0:T(8,128)(2,1)S(1)} %get-tuple-element.31.st_ref, f32[17,8,16,128]{3,2,1,0:T(8,128)S(1)} %get-tuple-element.32.tab_ref, bf16[4,256,256]{2,1,0:T(8,128)(2,1)S(1)} %get-tuple-element.34.sc, ...), custom_call_target="tpu_custom_call", output_to_operand_aliasing={{}: (0, {})} | custom-call | flops 1000000000 | bytes 4000000 | tf_op jit(solution)/shard_map/near/pallas_call | solution.py:649
  52.7 4.0 %near.5.near_ref = bf16[2048,1024]{1,0:T(8,128)(2,1)S(1)} custom-call(bf16[2048,1024]{1,0:T(8,128)(2,1)S(1)} %near.4.vt_ref, bf16[3,2048,128]{2,1,0:T(8,128)(2,1)S(1)} %get-tuple-element.31.st_ref, f32[17,8,16,128]{3,2,1,0:T(8,128)S(1)} %get-tuple-element.32.tab_ref, bf16[4,256,256]{2,1,0:T(8,128)(2,1)S(1)} %get-tuple-element.34.sc, ...), custom_call_target="tpu_custom_call", output_to_operand_aliasing={{}: (0, {})} | custom-call | flops 1000000000 | bytes 4000000 | tf_op jit(solution)/shard_map/near/pallas_call | solution.py:649
  56.8 3.0 %mid.1.near_ref = bf16[2048,1024]{1,0:T(8,128)(2,1)S(1)} custom-call(bf16[2048,1024]{1,0:T(8,128)(2,1)S(1)} %near.5.near_ref, bf16[2064,128]{1,0:T(8,128)(2,1)S(1)} %collective-permute-done.1.other_ref.chip_ref, bf16[1024,128]{1,0:T(8,128)(2,1)S(1)} %shard_map.74.low_ref, ...), custom_call_target="tpu_custom_call", output_to_operand_aliasing={{}: (0, {})} | custom-call | flops 1000000000 | bytes 6000000 | tf_op jit(solution)/shard_map/mid/pallas_call | solution.py:705
  59.7 3.3 %far.2.refs_0_ = bf16[1024,2048]{1,0:T(8,128)(2,1)} custom-call(bf16[2048,1024]{1,0:T(8,128)(2,1)S(1)} %mid.1.near_ref, bf16[2,1024,128]{2,1,0:T(8,128)(2,1)S(1)} %shard_map.77.high_ref, f32[4,8,16,128]{3,2,1,0:T(8,128)S(1)} %get-tuple-element.39.far_ref, bf16[128,1024]{1,0:T(8,128)(2,1)S(1)} %get-tuple-element.35.qt_ref, ...), custom_call_target="tpu_custom_call" | custom-call | flops 1000000000 | bytes 6000000 | tf_op jit(solution)/shard_map/far/pallas_call | solution.py:732
  63.0 3.3 %far.3 = bf16[1024,2048]{1,0:T(8,128)(2,1)} custom-call(bf16[2048,1024]{1,0:T(8,128)(2,1)S(1)} %mid.1.near_ref, bf16[2,1024,128]{2,1,0:T(8,128)(2,1)S(1)} %collective-permute-done.10.high_ref, f32[4,8,16,128]{3,2,1,0:T(8,128)S(1)} %get-tuple-element.39.far_ref, bf16[128,1024]{1,0:T(8,128)(2,1)S(1)} %get-tuple-element.35.qt_ref, ...), custom_call_target="tpu_custom_call", output_to_operand_aliasing={{}: (6, {})} | custom-call | flops 1000000000 | bytes 6000000 | tf_op jit(solution)/shard_map/far/pallas_call | solution.py:732
  (17 shorter events, 0.1 us)
Async XLA Ops:
  0.0 3.4 %copy-start = (bf16[1024,128]{1,0:T(8,128)(2,1)S(1)}, bf16[1024,128]{1,0:T(8,128)(2,1)}, u32[]{:S(2)}) copy-start(bf16[1024,128]{1,0:T(8,128)(2,1)} %k_ref.5) | copy-start | bytes 786436
  0.0 3.4 %copy-start.2 = (f32[4,2304]{1,0:T(4,128)S(1)}, f32[4,2304]{1,0:T(4,128)}, u32[]{:S(2)}) copy-start(f32[4,2304]{1,0:T(4,128)} %w_ref.1) | copy-start | bytes 110596
  0.0 3.4 %copy-start.3 = (bf16[15,16,1024]{2,1,0:T(8,128)(2,1)S(1)}, bf16[15,16,1024]{2,1,0:T(8,128)(2,1)}, u32[]{:S(2)}) copy-start(bf16[15,16,1024]{2,1,0:T(8,128)(2,1)} %lw_ref.1) | copy-start | bytes 1474564
  0.0 3.4 %copy-start.4 = (f32[16,1024]{1,0:T(8,128)S(1)}, f32[16,1024]{1,0:T(8,128)}, u32[]{:S(2)}) copy-start(f32[16,1024]{1,0:T(8,128)} %ld_ref.1) | copy-start | bytes 196612
  1.0 4.1 %collective-permute-start = (bf16[3,2304]{1,0:T(4,128)(2,1)S(1)}, bf16[3,2304]{1,0:T(4,128)(2,1)S(1)}, u32[]{:S(2)}, u32[]{:S(2)}) collective-permute-start(bf16[3,2304]{1,0:T(4,128)(2,1)S(1)} %rim.1), channel_id=1, source_target_pairs={{0,1},{1,2},{2,3},{3,4},{4,5},{5,6},{6,7},{7,8},{8,9},{9,10},{10,1... | collective-permute-start | bytes 41480 | tf_op jit(solution)/shard_map/ppermute | solution.py:576
  5.1 39.5 %copy-start.1 = (bf16[1024,128]{1,0:T(8,128)(2,1)S(1)}, bf16[1024,128]{1,0:T(8,128)(2,1)}, u32[]{:S(2)}) copy-start(bf16[1024,128]{1,0:T(8,128)(2,1)} %q_ref.3) | copy-start | bytes 786436
  11.4 4.2 %collective-permute-start.1 = (bf16[2064,128]{1,0:T(8,128)(2,1)S(1)}, bf16[2064,128]{1,0:T(8,128)(2,1)S(1)}, u32[]{:S(2)}, u32[]{:S(2)}) collective-permute-start(bf16[2064,128]{1,0:T(8,128)(2,1)S(1)} %get-tuple-element.36.own_ref), channel_id=1, source_target_pairs={{0,1},{1,0},{2,3},{3,2},{4,5},{5,4},{6,7},{7,6},{8,9},{9,8},{10,11... | collective-permute-start | bytes 1585160 | tf_op jit(solution)/shard_map/ppermute | solution.py:537
  15.9 5.9 %collective-permute-start.3 = (bf16[528,128]{1,0:T(8,128)(2,1)S(1)}, bf16[528,128]{1,0:T(8,128)(2,1)S(1)}, u32[]{:S(2)}, u32[]{:S(2)}) collective-permute-start(bf16[528,128]{1,0:T(8,128)(2,1)S(1)} %get-tuple-element.38), channel_id=1, source_target_pairs={{0,2},{1,3},{2,0},{3,1},{4,6},{5,7},{6,4},{7,5},{8,10},{9,11},{10,... | collective-permute-start | bytes 405512 | tf_op jit(solution)/shard_map/ppermute | solution.py:537
  22.0 6.0 %collective-permute-start.5 = (bf16[528,128]{1,0:T(8,128)(2,1)S(1)}, bf16[528,128]{1,0:T(8,128)(2,1)S(1)}, u32[]{:S(2)}, u32[]{:S(2)}) collective-permute-start(bf16[528,128]{1,0:T(8,128)(2,1)S(1)} %get-tuple-element.41), channel_id=1, source_target_pairs={{0,4},{1,5},{2,6},{3,7},{4,0},{5,1},{6,2},{7,3},{8,12},{9,13},{10,... | collective-permute-start | bytes 405512 | tf_op jit(solution)/shard_map/ppermute | solution.py:537
  24.5 9.6 %collective-permute-start.7 = (bf16[528,128]{1,0:T(8,128)(2,1)S(1)}, bf16[528,128]{1,0:T(8,128)(2,1)S(1)}, u32[]{:S(2)}, u32[]{:S(2)}) collective-permute-start(bf16[528,128]{1,0:T(8,128)(2,1)S(1)} %get-tuple-element.41), channel_id=1, source_target_pairs={{0,12},{1,13},{2,14},{3,15},{4,8},{5,9},{6,10},{7,11},{8,4},{9,5},... | collective-permute-start | bytes 405512 | tf_op jit(solution)/shard_map/ppermute | solution.py:537
  26.9 11.6 %collective-permute-start.6 = (bf16[528,128]{1,0:T(8,128)(2,1)S(1)}, bf16[528,128]{1,0:T(8,128)(2,1)S(1)}, u32[]{:S(2)}, u32[]{:S(2)}) collective-permute-start(bf16[528,128]{1,0:T(8,128)(2,1)S(1)} %get-tuple-element.41), channel_id=1, source_target_pairs={{0,8},{1,9},{2,10},{3,11},{4,12},{5,13},{6,14},{7,15},{8,0},{9,1},... | collective-permute-start | bytes 405512 | tf_op jit(solution)/shard_map/ppermute | solution.py:537
  27.9 16.6 %collective-permute-start.8 = (bf16[528,128]{1,0:T(8,128)(2,1)S(1)}, bf16[528,128]{1,0:T(8,128)(2,1)S(1)}, u32[]{:S(2)}, u32[]{:S(2)}) collective-permute-start(bf16[528,128]{1,0:T(8,128)(2,1)S(1)} %collective-permute-done.5.refs_0_.next_ref), channel_id=1, source_target_pairs={{0,2},{1,3},{2,0},{3,1},{4,6},{5,7},{6,4},{7,5},{8,10},{9,11},{10,... | collective-permute-start | bytes 405512 | tf_op jit(solution)/shard_map/ppermute | solution.py:537
  38.7 5.8 %collective-permute-start.9 = (bf16[1,512,128]{2,1,0:T(8,128)(2,1)S(1)}, bf16[1,512,128]{2,1,0:T(8,128)(2,1)S(1)}, u32[]{:S(2)}, u32[]{:S(2)}) collective-permute-start(bf16[1,512,128]{2,1,0:T(8,128)(2,1)S(1)} %get-tuple-element.44.part_ref), channel_id=1, source_target_pairs={{0,2},{1,3},{2,0},{3,1},{4,6},{5,7},{6,4},{7,5},{8,10},{9,11},{10,... | collective-permute-start | bytes 393224 | tf_op jit(solution)/shard_map/ppermute | solution.py:537
  39.4 6.5 %collective-permute-start.2 = (bf16[512,128]{1,0:T(8,128)(2,1)S(1)}, bf16[512,128]{1,0:T(8,128)(2,1)S(1)}, u32[]{:S(2)}, u32[]{:S(2)}) collective-permute-start(bf16[512,128]{1,0:T(8,128)(2,1)S(1)} %get-tuple-element.37.mine_ref), channel_id=1, source_target_pairs={{0,2},{1,3},{2,0},{3,1},{4,6},{5,7},{6,4},{7,5},{8,10},{9,11},{10,... | collective-permute-start | bytes 393224 | tf_op jit(solution)/shard_map/ppermute | solution.py:537
  44.5 18.5 %collective-permute-start.10 = (bf16[2,1024,128]{2,1,0:T(8,128)(2,1)S(1)}, bf16[2,1024,128]{2,1,0:T(8,128)(2,1)S(1)}, u32[]{:S(2)}, u32[]{:S(2)}) collective-permute-start(bf16[2,1024,128]{2,1,0:T(8,128)(2,1)S(1)} %shard_map.77.high_ref), channel_id=1, source_target_pairs={{0,1},{1,0},{2,3},{3,2},{4,5},{5,4},{6,7},{7,6},{8,9},{9,8},{10,11... | collective-permute-start | bytes 1572872 | tf_op jit(solution)/shard_map/ppermute | solution.py:537
  45.9 10.8 %collective-permute-start.4 = (bf16[1024,128]{1,0:T(8,128)(2,1)S(1)}, bf16[1024,128]{1,0:T(8,128)(2,1)S(1)}, u32[]{:S(2)}, u32[]{:S(2)}) collective-permute-start(bf16[1024,128]{1,0:T(8,128)(2,1)S(1)} %shard_map.74.low_ref), channel_id=1, source_target_pairs={{0,1},{1,0},{2,3},{3,2},{4,5},{5,4},{6,7},{7,6},{8,9},{9,8},{10,11... | collective-permute-start | bytes 786440 | tf_op jit(solution)/shard_map/ppermute | solution.py:537
  56.7 3.0 %copy-start.5 = (f32[2048]{0:T(1024)S(1)}, f32[2048]{0:T(1024)}, u32[]{:S(2)}) copy-start(f32[2048]{0:T(1024)} %param.13) | copy-start | bytes 24580
